TPU v7x, 256 devices: a whole 4x4x8 slice. The times are simulated.
256 devices in a mesh: dp: 32 (over x, z), seq: 8 (over y, core).
Axes of the slice: x: 4, y: 4, z: 8, core: 2. Of those that a mesh axis runs over, the one named last changes fastest.
Arguments:
- xbc: bfloat16 [32, 2048, 2816], P('dp', 'seq'), may hold values from -6 to 6
- gate_input: bfloat16 [32, 2048, 2560], P('dp', 'seq'), may hold values from -6 to 6
- dt_raw: bfloat16 [32, 2048, 40], P('dp', 'seq'), may hold values from -3 to 3
- conv_weight: float32 [4, 2816], replicated, may hold values from -3 to 3
- conv_bias: float32 [2816], replicated, may hold values from -3 to 3
- dt_bias: float32 [40], replicated, may hold values from -0.5 to 0.5
- a_rate: float32 [40], replicated, may hold values from 9.765625e-05 to 0.05
- d_skip: float32 [40], replicated, may hold values from 0.5 to 1.5
- norm_gain: float32 [2560], replicated, may hold values from 0.25 to 1.75
- labels: int32 [32], P('dp'), may hold values from 0 to 1, as said below
- readout: int32 [32, 4], P('dp'), may hold values from 0 to 2047
Outputs:
- layer_out: bfloat16 [32, 2048, 2560], P('dp', 'seq')
- steering: float32 [2560, 128], P(('dp', 'seq'))
Inputs may be any that keep to these rules, and one draw needn't show every extreme that they name: `labels`: every label is 0 or 1, and both classes occur.
All inputs are finite; a program needn't handle non-finite values.
Results may differ from a plain program's by a relative error of at most 0.0034.
Values may be sent and summed in bfloat16 or wider, within the bound.
A program may use at most 64 MiB of HBM per device.

v0:
```python
import jax
import jax.numpy as jnp
from jax import lax
from jax.sharding import PartitionSpec as P

H = 40
P_SIZE = 64
N = 128
KW = 4
R = 4


group_heads = 8
highest = lax.Precision.HIGHEST


def from_behind(block, axis, distance):
    devices = range(lax.axis_size(axis))
    route = [(i - distance, i) for i in devices if i - distance in devices]
    return lax.ppermute(block, axis, route)


def local_terms(x_vals, b_vals, c_vals, dt_vals, cumulative, points, offset):
    row_count = x_vals.shape[0]
    x_wide = x_vals.astype(jnp.float32).reshape(row_count, H, P_SIZE)
    b_wide = b_vals.astype(jnp.float32)
    c_wide = c_vals.astype(jnp.float32)
    scores = lax.dot_general(
        c_vals, b_vals, (((1,), (1,)), ((), ())), preferred_element_type=jnp.float32
    )
    positions = jnp.arange(row_count, dtype=jnp.int32)
    causal = positions[:, None] >= positions[None, :]
    cum_heads = cumulative.T
    dt_heads = dt_vals.T

    def group_step(group_index, buffer):
        head_start = group_index * group_heads
        cum_group = lax.dynamic_slice_in_dim(cum_heads, head_start, group_heads, 0)
        dt_group = lax.dynamic_slice_in_dim(dt_heads, head_start, group_heads, 0)
        x_group = lax.dynamic_slice_in_dim(x_wide, head_start, group_heads, 1)
        spread = jnp.where(causal[None], cum_group[:, :, None] - cum_group[:, None, :], -1e30)
        weight = jnp.exp(spread) * dt_group[:, None, :] * scores[None]
        partial_value = jnp.einsum("hts,shp->thp", weight, x_group, precision=highest)
        return lax.dynamic_update_slice_in_dim(buffer, partial_value, head_start, 1)

    diagonal_part = lax.fori_loop(
        0, H // group_heads, group_step, jnp.zeros((row_count, H, P_SIZE), jnp.float32)
    )
    final_log = cumulative[row_count - 1]
    to_end = jnp.exp(final_log[None, :] - cumulative) * dt_vals
    decay_total = jnp.exp(final_log)
    local_state = jnp.einsum(
        "sk,sn->kn",
        (to_end[:, :, None] * x_wide).reshape(row_count, H * P_SIZE),
        b_wide,
        precision=highest,
    ).reshape(H, P_SIZE, N)
    local_index = points - offset
    owned_flag = ((local_index >= 0) & (local_index < row_count)).astype(jnp.float32)
    one_hot = (positions[None, :] == local_index[:, None]).astype(jnp.float32)
    cum_at = jnp.dot(one_hot, cumulative, precision=highest)
    before = positions[None, :] <= local_index[:, None]
    spread = jnp.where(before[:, :, None], cum_at[:, None, :] - cumulative[None], -1e30)
    read_weight = jnp.sum(owned_flag[:, None, None] * jnp.exp(spread), axis=0) * dt_vals / R
    carry_weight = jnp.sum(owned_flag[:, None] * jnp.exp(cum_at), axis=0) / R
    read_local = jnp.einsum(
        "sk,sn->kn",
        (read_weight[:, :, None] * x_wide).reshape(row_count, H * P_SIZE),
        b_wide,
        precision=highest,
    ).reshape(H, P_SIZE, N)
    return (diagonal_part, x_wide, c_wide, local_state, decay_total, read_local, carry_weight)


def finish_block(diagonal_part, x_wide, c_wide, cumulative, h_in, gate_rows, d_skip, norm_gain):
    row_count = x_wide.shape[0]
    incoming = jnp.einsum("tn,hpn->thp", c_wide, h_in, precision=highest)
    ssm_out = (
        diagonal_part + jnp.exp(cumulative)[:, :, None] * incoming + d_skip[None, :, None] * x_wide
    )
    gated_out = ssm_out.reshape(row_count, H * P_SIZE) * jax.nn.silu(gate_rows.astype(jnp.float32))
    inv_rms = lax.rsqrt(jnp.mean(gated_out * gated_out, axis=-1, keepdims=True) + 1e-05)
    return (gated_out * inv_rms * norm_gain).astype(jnp.bfloat16)


def on_device(
    xbc,
    gate_input,
    dt_raw,
    conv_weight,
    conv_bias,
    dt_bias,
    a_rate,
    d_skip,
    norm_gain,
    labels,
    readout,
):
    row_count = xbc.shape[1]
    n_one = lax.psum(jnp.sum(labels.astype(jnp.float32)), "dp")
    edge_rows = from_behind(xbc[:, row_count - (KW - 1) :, :], "seq", 1)
    padded = jnp.concatenate([edge_rows, xbc], axis=1)[0].astype(jnp.float32)
    conv_sum = conv_bias
    for tap_index in range(KW):
        conv_sum = conv_sum + conv_weight[tap_index] * padded[tap_index : tap_index + row_count]
    activated = jax.nn.silu(conv_sum).astype(jnp.bfloat16)
    dt_vals = jax.nn.softplus(dt_raw[0].astype(jnp.float32) + dt_bias)
    cumulative = jnp.cumsum(-a_rate * dt_vals, axis=0)
    offset = lax.axis_index("seq") * row_count
    diagonal_part, x_wide, c_wide, local_state, decay_total, read_local, carry_weight = local_terms(
        activated[:, : H * P_SIZE],
        activated[:, H * P_SIZE : H * P_SIZE + N],
        activated[:, H * P_SIZE + N :],
        dt_vals,
        cumulative,
        readout[0],
        offset,
    )
    h_in = jnp.zeros((H, P_SIZE, N), jnp.float32)
    for step_index in range(lax.axis_size("seq") - 1):
        h_in = from_behind(decay_total[:, None, None] * h_in + local_state, "seq", 1)
    layer_out = finish_block(
        diagonal_part, x_wide, c_wide, cumulative, h_in, gate_input[0], d_skip, norm_gain
    )
    mean_state = carry_weight[:, None, None] * h_in + read_local
    batch_count = lax.axis_size("dp")
    class_value = labels[0].astype(jnp.float32)
    class_weight = class_value / n_one - (1.0 - class_value) / (batch_count - n_one)
    partial_value = (class_weight * mean_state).reshape(H * P_SIZE, N)
    steering = lax.psum_scatter(partial_value, ("dp", "seq"), scatter_dimension=0, tiled=True)
    return (layer_out[None], steering)


def solution(mesh):
    return jax.shard_map(
        on_device,
        mesh=mesh,
        in_specs=(
            P("dp", "seq", None),
            P("dp", "seq", None),
            P("dp", "seq", None),
            P(),
            P(),
            P(),
            P(),
            P(),
            P(),
            P("dp"),
            P("dp", None),
        ),
        out_specs=(P("dp", "seq", None), P(("dp", "seq"), None)),
        check_vma=False,
    )
```

profile of v0, /device:TPU:6, one launch (start us, length us, event | category | flops | bytes accessed | tf_op | source)
XLA Modules:
  0.0 523.5 jit_solution(17056972736447716053)
XLA Ops:
  17.1 3.2 copy.46
  22.1 3.4 copy.50
  31.6 3.2 copy.47
  34.8 3.0 broadcast_add_fusion
  37.9 3.8 collective-permute-start.1
  44.5 13.9 %collective-permute-start.2 = (f32[40,64,128]{2,1,0:T(8,128)S(1)}, f32[40,64,128]{2,1,0:T(8,128)S(1)}, u32[]{:S(2)}, u32[]{:S(2)}) collective-permute-start(f32[40,64,128]{2,1,0:T(8,128)S(1)} %multiply_add_fusion.6), channel_id=1, source_target_pairs={{0,1},{1,2},{2,3},{3,4},{4,5},{5,6},{6,7},{8,9},{9,10},{10,11},{11... | collective-permute-start | bytes 3932168 | tf_op jit(solution)/shard_map/ppermute | solution.py:20
  61.2 16.4 %collective-permute-start.3 = (f32[40,64,128]{2,1,0:T(8,128)S(1)}, f32[40,64,128]{2,1,0:T(8,128)S(1)}, u32[]{:S(2)}, u32[]{:S(2)}) collective-permute-start(f32[40,64,128]{2,1,0:T(8,128)S(1)} %multiply_add_fusion.5), channel_id=1, source_target_pairs={{0,1},{1,2},{2,3},{3,4},{4,5},{5,6},{6,7},{8,9},{9,10},{10,11},{11... | collective-permute-start | bytes 3932168 | tf_op jit(solution)/shard_map/ppermute | solution.py:20
  80.4 16.4 %collective-permute-start.4 = (f32[40,64,128]{2,1,0:T(8,128)S(1)}, f32[40,64,128]{2,1,0:T(8,128)S(1)}, u32[]{:S(2)}, u32[]{:S(2)}) collective-permute-start(f32[40,64,128]{2,1,0:T(8,128)S(1)} %multiply_add_fusion.4), channel_id=1, source_target_pairs={{0,1},{1,2},{2,3},{3,4},{4,5},{5,6},{6,7},{8,9},{9,10},{10,11},{11... | collective-permute-start | bytes 3932168 | tf_op jit(solution)/shard_map/ppermute | solution.py:20
  99.6 16.4 %collective-permute-start.5 = (f32[40,64,128]{2,1,0:T(8,128)S(1)}, f32[40,64,128]{2,1,0:T(8,128)S(1)}, u32[]{:S(2)}, u32[]{:S(2)}) collective-permute-start(f32[40,64,128]{2,1,0:T(8,128)S(1)} %multiply_add_fusion.3), channel_id=1, source_target_pairs={{0,1},{1,2},{2,3},{3,4},{4,5},{5,6},{6,7},{8,9},{9,10},{10,11},{11... | collective-permute-start | bytes 3932168 | tf_op jit(solution)/shard_map/ppermute | solution.py:20
  119.8 17.3 %collective-permute-start.6 = (f32[40,64,128]{2,1,0:T(8,128)}, f32[40,64,128]{2,1,0:T(8,128)}, u32[]{:S(2)}, u32[]{:S(2)}) collective-permute-start(f32[40,64,128]{2,1,0:T(8,128)} %multiply_add_fusion.2), channel_id=1, source_target_pairs={{0,1},{1,2},{2,3},{3,4},{4,5},{5,6},{6,7},{8,9},{9,10},{10,11},{11... | collective-permute-start | bytes 3932168 | tf_op jit(solution)/shard_map/ppermute | solution.py:20
  137.8 67.2 %psum.7 = f32[]{:T(128)} all-reduce(f32[]{:T(128)} %bitcast.16), channel_id=1, replica_groups=mesh['dp'=32,'seq'=8] {'dp'}, use_global_device_ids=true, to_apply=%region_5.6 | all-reduce | flops 1 | bytes 8 | tf_op jit(solution)/shard_map/psum | solution.py:100
  209.3 3.2 copy.51
  214.4 3.3 copy.43
  223.8 22.0 %while.14 = (s32[]{:T(128)}, f32[256,40,64]{0,2,1:T(8,128)}, f32[256,40,64]{0,2,1:T(8,128)}, f32[40,256]{1,0:T(8,128)S(1)}, f32[40,256]{1,0:T(8,128)S(1)}, /*ind...) while((s32[]{:T(128)}, f32[256,40,64]{0,2,1:T(8,128)}, ...), condition=%wide.region_3.4_spmd.clone, body=%wide.region_2.3_spmd.clone.sunk | while | flops 404815872 | bytes 1500311 | solution.py:46
  223.9 4.4 fusion.63
  228.3 4.4 fusion.63
  232.7 4.4 fusion.63
  237.1 4.3 fusion.63
  241.5 4.3 fusion.63
  245.8 4.1 add_multiply_fusion
  250.0 6.6 %multiply_reduce_fusion = (f32[256]{0:T(256)S(1)}, f32[256,40,64]{0,2,1:T(8,128)}) fusion(f32[256,40,64]{0,2,1:T(8,128)} %bitcast.125, f32[256,40,64]{0,2,1:T(8,128)} %get-tuple-element.257, f32[40]{0:T(128)S(1)} %copy-done.6, f32[256,40,64]{0,2,1:T(8,128)} %get-tuple-element.126, f32[40,64,128]{2,1,0:T(8,128)S(1)} %collective-permute-done.7, ...), kind=kOutput, calls=%fused_computation.36 | convolution fusion | flops 1013841664 | bytes 11904512 | tf_op jit(solution)/shard_map/tn,hpn->thp/dot_general | solution.py:77
  256.6 3.3 copy.48
  259.9 3.8 multiply_convert_fusion.1
  263.7 251.6 %all-reduce.3.cloned.1.call-done = f32[2560,128]{1,0:T(8,128)} async-done(((f32[2560,128]{1,0:T(8,128)}), f32[2560,128]{1,0:T(8,128)}) %all-reduce.3.cloned.1.call-update) | async-done | bytes 1310736
  (70 shorter events, 45.1 us)
Async XLA Ops:
  7.2 508.1 %all-reduce.3.cloned.1.call-start = ((), (), s32[]{:S(2)}) async-start(), calls=%async_computation | async-start | bytes 2621440
  8.0 17.4 %collective-permute-start = (bf16[1,3,2816]{2,1,0:T(4,128)(2,1)S(1)}, bf16[1,3,2816]{2,1,0:T(4,128)(2,1)S(1)}, u32[]{:S(2)}, u32[]{:S(2)}) collective-permute-start(bf16[1,3,2816]{2,1,0:T(4,128)(2,1)S(1)} %slice.58), channel_id=1, source_target_pairs={{0,1},{1,2},{2,3},{3,4},{4,5},{5,6},{6,7},{8,9},{9,10},{10,11},{11... | collective-permute-start | bytes 50696 | tf_op jit(solution)/shard_map/ppermute | solution.py:20
  22.1 3.4 copy-start.3
  25.4 0.7 copy-start.5
  26.1 1.9 copy-start
  26.1 2.5 copy-start.1
  37.9 6.4 %collective-permute-start.1 = (f32[40,64,128]{2,1,0:T(8,128)S(1)}, f32[40,64,128]{2,1,0:T(8,128)S(1)}, u32[]{:S(2)}, u32[]{:S(2)}) collective-permute-start(f32[40,64,128]{2,1,0:T(8,128)S(1)} %get-tuple-element.177), channel_id=1, source_target_pairs={{0,1},{1,2},{2,3},{3,4},{4,5},{5,6},{6,7},{8,9},{9,10},{10,11},{11... | collective-permute-start | bytes 3932168 | tf_op jit(solution)/shard_map/ppermute | solution.py:20
  44.5 16.5 %collective-permute-start.2 = (f32[40,64,128]{2,1,0:T(8,128)S(1)}, f32[40,64,128]{2,1,0:T(8,128)S(1)}, u32[]{:S(2)}, u32[]{:S(2)}) collective-permute-start(f32[40,64,128]{2,1,0:T(8,128)S(1)} %multiply_add_fusion.6), channel_id=1, source_target_pairs={{0,1},{1,2},{2,3},{3,4},{4,5},{5,6},{6,7},{8,9},{9,10},{10,11},{11... | collective-permute-start | bytes 3932168 | tf_op jit(solution)/shard_map/ppermute | solution.py:20
  61.2 18.9 %collective-permute-start.3 = (f32[40,64,128]{2,1,0:T(8,128)S(1)}, f32[40,64,128]{2,1,0:T(8,128)S(1)}, u32[]{:S(2)}, u32[]{:S(2)}) collective-permute-start(f32[40,64,128]{2,1,0:T(8,128)S(1)} %multiply_add_fusion.5), channel_id=1, source_target_pairs={{0,1},{1,2},{2,3},{3,4},{4,5},{5,6},{6,7},{8,9},{9,10},{10,11},{11... | collective-permute-start | bytes 3932168 | tf_op jit(solution)/shard_map/ppermute | solution.py:20
  80.4 18.9 %collective-permute-start.4 = (f32[40,64,128]{2,1,0:T(8,128)S(1)}, f32[40,64,128]{2,1,0:T(8,128)S(1)}, u32[]{:S(2)}, u32[]{:S(2)}) collective-permute-start(f32[40,64,128]{2,1,0:T(8,128)S(1)} %multiply_add_fusion.4), channel_id=1, source_target_pairs={{0,1},{1,2},{2,3},{3,4},{4,5},{5,6},{6,7},{8,9},{9,10},{10,11},{11... | collective-permute-start | bytes 3932168 | tf_op jit(solution)/shard_map/ppermute | solution.py:20
  99.6 18.9 %collective-permute-start.5 = (f32[40,64,128]{2,1,0:T(8,128)S(1)}, f32[40,64,128]{2,1,0:T(8,128)S(1)}, u32[]{:S(2)}, u32[]{:S(2)}) collective-permute-start(f32[40,64,128]{2,1,0:T(8,128)S(1)} %multiply_add_fusion.3), channel_id=1, source_target_pairs={{0,1},{1,2},{2,3},{3,4},{4,5},{5,6},{6,7},{8,9},{9,10},{10,11},{11... | collective-permute-start | bytes 3932168 | tf_op jit(solution)/shard_map/ppermute | solution.py:20
  119.8 98.0 %collective-permute-start.6 = (f32[40,64,128]{2,1,0:T(8,128)}, f32[40,64,128]{2,1,0:T(8,128)}, u32[]{:S(2)}, u32[]{:S(2)}) collective-permute-start(f32[40,64,128]{2,1,0:T(8,128)} %multiply_add_fusion.2), channel_id=1, source_target_pairs={{0,1},{1,2},{2,3},{3,4},{4,5},{5,6},{6,7},{8,9},{9,10},{10,11},{11... | collective-permute-start | bytes 3932168 | tf_op jit(solution)/shard_map/ppermute | solution.py:20
  220.4 25.4 %collective-permute-start.7 = (f32[40,64,128]{2,1,0:T(8,128)}, f32[40,64,128]{2,1,0:T(8,128)S(1)}, u32[]{:S(2)}, u32[]{:S(2)}) collective-permute-start(f32[40,64,128]{2,1,0:T(8,128)} %multiply_add_fusion.1), channel_id=1, source_target_pairs={{0,1},{1,2},{2,3},{3,4},{4,5},{5,6},{6,7},{8,9},{9,10},{10,11},{11... | collective-permute-start | bytes 3932168 | tf_op jit(solution)/shard_map/ppermute | solution.py:20
  245.8 4.1 copy-start.6
  256.6 3.3 copy-start.2
  256.6 3.3 copy-start.4
Sparse Core Ops, SparseCore 0:
  250.1 265.1 all-reduce.2
where the time goes:
time: 525 us; the launch traced here: 523 us
  waiting for transfers between devices  264 us (50%)
  starting transfers between devices  87.5 us (17%)
  blocking collectives  67.2 us (13%)
  matrix products  36 us (7%)
  local copies, waits for them, and re-layouts  32.4 us (6%)
  other arithmetic  19.6 us (4%)
  between operations  16.4 us (3%)
    unnamed x2, waiting for transfers between devices  252 us
    ppermute x8, starting transfers between devices, from_behind(): return lax.ppermute(block, axis, route)  87.4 us
    psum x1, blocking collectives, on_device(): n_one = lax.psum(jnp.sum(labels.astype(jnp.float32)), 'dp')  67.2 us
    dot_general x5, matrix products, group_step(): jnp.einsum('hts,shp->thp', weight, x_group, precision=highest)  21.8 us
    ppermute x8, waiting for transfers between devices, from_behind(): return lax.ppermute(block, axis, route)  12.8 us
  transfers between devices with their start and end apart: 9, of which 6 were waited for; matrix products, arithmetic and copies ran while one was open for 12% of the time, Pallas kernels for 0%

commit v1 on v0

--- a/solution.py
+++ b/solution.py
@@ -63,13 +63,9 @@
     spread = jnp.where(before[:, :, None], cum_at[:, None, :] - cumulative[None], -1e30)
     read_weight = jnp.sum(owned_flag[:, None, None] * jnp.exp(spread), axis=0) * dt_vals / R
     carry_weight = jnp.sum(owned_flag[:, None] * jnp.exp(cum_at), axis=0) / R
-    read_local = jnp.einsum(
-        "sk,sn->kn",
-        (read_weight[:, :, None] * x_wide).reshape(row_count, H * P_SIZE),
-        b_wide,
-        precision=highest,
-    ).reshape(H, P_SIZE, N)
-    return (diagonal_part, x_wide, c_wide, local_state, decay_total, read_local, carry_weight)
+    return (
+        diagonal_part, x_wide, b_wide, c_wide, local_state, decay_total, to_end, read_weight, carry_weight
+    )
 
 
 def finish_block(diagonal_part, x_wide, c_wide, cumulative, h_in, gate_rows, d_skip, norm_gain):
@@ -97,7 +93,9 @@
     readout,
 ):
     row_count = xbc.shape[1]
-    n_one = lax.psum(jnp.sum(labels.astype(jnp.float32)), "dp")
+    seq_count = lax.axis_size("seq")
+    me = lax.axis_index("seq")
+    n_one = jnp.sum(lax.all_gather(labels, "dp", tiled=True).astype(jnp.float32))
     edge_rows = from_behind(xbc[:, row_count - (KW - 1) :, :], "seq", 1)
     padded = jnp.concatenate([edge_rows, xbc], axis=1)[0].astype(jnp.float32)
     conv_sum = conv_bias
@@ -106,8 +104,9 @@
     activated = jax.nn.silu(conv_sum).astype(jnp.bfloat16)
     dt_vals = jax.nn.softplus(dt_raw[0].astype(jnp.float32) + dt_bias)
     cumulative = jnp.cumsum(-a_rate * dt_vals, axis=0)
-    offset = lax.axis_index("seq") * row_count
-    diagonal_part, x_wide, c_wide, local_state, decay_total, read_local, carry_weight = local_terms(
+    offset = me * row_count
+    (diagonal_part, x_wide, b_wide, c_wide, local_state, decay_total, to_end, read_weight,
+     carry_weight) = local_terms(
         activated[:, : H * P_SIZE],
         activated[:, H * P_SIZE : H * P_SIZE + N],
         activated[:, H * P_SIZE + N :],
@@ -116,18 +115,31 @@
         readout[0],
         offset,
     )
+    scalars = lax.all_gather(jnp.stack([decay_total, carry_weight]), "seq")
+    coef_rows = [jnp.zeros_like(decay_total)]
+    for later in range(seq_count - 1, 0, -1):
+        coef_rows.append(scalars[later, 1] + scalars[later, 0] * coef_rows[-1])
+    coef_all = jnp.stack(coef_rows[::-1])
+    coef = jnp.sum(jnp.where((jnp.arange(seq_count) == me)[:, None], coef_all, 0.0), axis=0)
+    mean_weight = coef[None, :] * to_end + read_weight
+    mean_local = jnp.einsum(
+        "sk,sn->kn",
+        (mean_weight[:, :, None] * x_wide).reshape(row_count, H * P_SIZE),
+        b_wide,
+        precision=highest,
+    )
+    batch_count = lax.axis_size("dp")
+    class_value = labels[0].astype(jnp.float32)
+    class_weight = class_value / n_one - (1.0 - class_value) / (batch_count - n_one)
+    partial_value = class_weight * mean_local
+    steering = lax.psum_scatter(partial_value, "dp", scatter_dimension=0, tiled=True)
+    steering = lax.psum_scatter(steering, "seq", scatter_dimension=0, tiled=True)
     h_in = jnp.zeros((H, P_SIZE, N), jnp.float32)
-    for step_index in range(lax.axis_size("seq") - 1):
+    for step_index in range(seq_count - 1):
         h_in = from_behind(decay_total[:, None, None] * h_in + local_state, "seq", 1)
     layer_out = finish_block(
         diagonal_part, x_wide, c_wide, cumulative, h_in, gate_input[0], d_skip, norm_gain
     )
-    mean_state = carry_weight[:, None, None] * h_in + read_local
-    batch_count = lax.axis_size("dp")
-    class_value = labels[0].astype(jnp.float32)
-    class_weight = class_value / n_one - (1.0 - class_value) / (batch_count - n_one)
-    partial_value = (class_weight * mean_state).reshape(H * P_SIZE, N)
-    steering = lax.psum_scatter(partial_value, ("dp", "seq"), scatter_dimension=0, tiled=True)
     return (layer_out[None], steering)
 
 

time: 525 us -> 430 us (0.82)
  waiting for transfers between devices: 264 us -> 187 us
  blocking collectives: 67.2 us -> 56.7 us
  starting transfers between devices: 87.5 us -> 79 us
    unnamed x2 -> x1, waiting for transfers between devices: 252 us -> 0.02 us
    reduce_scatter x0 -> x1, waiting for transfers between devices: none -> 176 us  [on_device(): lax.psum_scatter(partial_value, 'dp', scatter_dimension=0, tiled=True)]
    psum x1 -> x0, blocking collectives: 67.2 us -> none  [on_device(): n_one = lax.psum(jnp.sum(labels.astype(jnp.float32)), 'dp')]
    unnamed x0 -> x2, blocking collectives: none -> 45.7 us
    all_gather x0 -> x1, blocking collectives: none -> 11 us  [on_device(): scalars = lax.all_gather(jnp.stack([decay_total, carry_weight]), 'seq')]
    ppermute x8, starting transfers between devices: 87.4 us -> 78.9 us  [from_behind(): return lax.ppermute(block, axis, route)]
  transfers between devices with their start and end apart: 9 -> 9, of which waited for: 6 -> 5; matrix products, arithmetic and copies ran while one was open for 12% -> 14% of each run, Pallas kernels for 0% -> 0%
where the time goes in v1:
time: 430 us; the launch traced here: 429 us
  waiting for transfers between devices  187 us (43%)
  starting transfers between devices  79 us (18%)
  blocking collectives  56.7 us (13%)
  matrix products  37.2 us (9%)
  local copies, waits for them, and re-layouts  31.1 us (7%)
  other arithmetic  21.3 us (5%)
  between operations  16.9 us (4%)
    reduce_scatter x1, waiting for transfers between devices, on_device(): lax.psum_scatter(partial_value, 'dp', scatter_dimension=0, tiled=True)  176 us
    ppermute x8, starting transfers between devices, from_behind(): return lax.ppermute(block, axis, route)  78.9 us
    unnamed x2, blocking collectives  45.7 us
    dot_general x5, matrix products, group_step(): jnp.einsum('hts,shp->thp', weight, x_group, precision=highest)  21.8 us
    all_gather x1, blocking collectives, on_device(): scalars = lax.all_gather(jnp.stack([decay_total, carry_weight]), 'seq')  11 us
    ppermute x8, waiting for transfers between devices, from_behind(): return lax.ppermute(block, axis, route)  10.3 us
  transfers between devices with their start and end apart: 9, of which 5 were waited for; matrix products, arithmetic and copies ran while one was open for 14% of the time, Pallas kernels for 0%

profile of v1, /device:TPU:6, one launch (start us, length us, event | category | flops | bytes accessed | tf_op | source)
XLA Modules:
  0.0 428.8 jit_solution(15018987699717450809)
XLA Ops:
  14.1 11.0 %all-gather.1 = f32[8,2,40]{2,1,0:T(2,128)S(1)} all-gather(f32[1,2,40]{2,1,0:T(2,128)S(1)} %maximum_bitcast_fusion), channel_id=2, replica_groups=mesh['dp'=32,'seq'=8] {'seq'}, dimensions={0}, use_global_device_ids=true | all-gather | bytes 2880 | tf_op jit(solution)/shard_map/all_gather | solution.py:118
  29.1 3.4 copy.72
  36.9 3.3 copy.73
  40.2 3.0 broadcast_add_fusion
  48.3 13.9 %collective-permute-start.2 = (f32[40,64,128]{2,1,0:T(8,128)S(1)}, f32[40,64,128]{2,1,0:T(8,128)S(1)}, u32[]{:S(2)}, u32[]{:S(2)}) collective-permute-start(f32[40,64,128]{2,1,0:T(8,128)S(1)} %multiply_add_fusion.6), channel_id=1, source_target_pairs={{0,1},{1,2},{2,3},{3,4},{4,5},{5,6},{6,7},{8,9},{9,10},{10,11},{11... | collective-permute-start | bytes 3932168 | tf_op jit(solution)/shard_map/ppermute | solution.py:20
  65.0 16.4 %collective-permute-start.3 = (f32[40,64,128]{2,1,0:T(8,128)S(1)}, f32[40,64,128]{2,1,0:T(8,128)S(1)}, u32[]{:S(2)}, u32[]{:S(2)}) collective-permute-start(f32[40,64,128]{2,1,0:T(8,128)S(1)} %multiply_add_fusion.5), channel_id=1, source_target_pairs={{0,1},{1,2},{2,3},{3,4},{4,5},{5,6},{6,7},{8,9},{9,10},{10,11},{11... | collective-permute-start | bytes 3932168 | tf_op jit(solution)/shard_map/ppermute | solution.py:20
  84.2 16.4 %collective-permute-start.4 = (f32[40,64,128]{2,1,0:T(8,128)S(1)}, f32[40,64,128]{2,1,0:T(8,128)S(1)}, u32[]{:S(2)}, u32[]{:S(2)}) collective-permute-start(f32[40,64,128]{2,1,0:T(8,128)S(1)} %multiply_add_fusion.4), channel_id=1, source_target_pairs={{0,1},{1,2},{2,3},{3,4},{4,5},{5,6},{6,7},{8,9},{9,10},{10,11},{11... | collective-permute-start | bytes 3932168 | tf_op jit(solution)/shard_map/ppermute | solution.py:20
  104.4 17.4 %collective-permute-start.5 = (f32[40,64,128]{2,1,0:T(8,128)}, f32[40,64,128]{2,1,0:T(8,128)}, u32[]{:S(2)}, u32[]{:S(2)}) collective-permute-start(f32[40,64,128]{2,1,0:T(8,128)} %multiply_add_fusion.3), channel_id=1, source_target_pairs={{0,1},{1,2},{2,3},{3,4},{4,5},{5,6},{6,7},{8,9},{9,10},{10,11},{11... | collective-permute-start | bytes 3932168 | tf_op jit(solution)/shard_map/ppermute | solution.py:20
  126.6 3.3 copy.79
  131.9 21.3 %all-reduce = s32[32]{0:T(128)S(1)} all-reduce(s32[32]{0:T(128)S(1)} %dynamic-update-slice), channel_id=1, replica_groups=mesh['dp'=32,'seq'=8] {'dp'}, use_global_device_ids=true, to_apply=%add | all-reduce | flops 32 | bytes 256
  163.2 3.3 copy.64
  166.4 5.0 %convolution_multiply_fusion = f32[2560,128]{1,0:T(8,128)} fusion(f32[256,2560]{1,0:T(8,128)} %copy.79, bf16[256,2816]{1,0:T(8,128)(2,1)S(1)} %multiply_convert_fusion, f32[]{:T(128)S(6)} %sub.87), kind=kOutput, calls=%fused_computation.21 | convolution fusion | flops 1008271360 | bytes 5308420 | tf_op jit(solution)/shard_map/sk,sn->kn/dot_general | solution.py:125
  174.2 8.5 %collective-permute-start.7 = (f32[40,64,128]{2,1,0:T(8,128)}, f32[40,64,128]{2,1,0:T(8,128)}, u32[]{:S(2)}, u32[]{:S(2)}) collective-permute-start(f32[40,64,128]{2,1,0:T(8,128)} %multiply_add_fusion.1), channel_id=1, source_target_pairs={{0,1},{1,2},{2,3},{3,4},{4,5},{5,6},{6,7},{8,9},{9,10},{10,11},{11... | collective-permute-start | bytes 3932168 | tf_op jit(solution)/shard_map/ppermute | solution.py:20
  184.5 21.9 %while.14 = (s32[]{:T(128)}, f32[256,40,64]{0,2,1:T(8,128)}, f32[256,40,64]{0,2,1:T(8,128)}, f32[40,256]{1,0:T(8,128)S(1)}, f32[40,256]{1,0:T(8,128)S(1)}, /*ind...) while((s32[]{:T(128)}, f32[256,40,64]{0,2,1:T(8,128)}, ...), condition=%wide.region_3.4_spmd.clone, body=%wide.region_2.3_spmd.clone.sunk | while | flops 404815872 | bytes 1500311 | solution.py:46
  184.6 4.4 %fusion.79 = f32[256,40,64]{0,2,1:T(8,128)} fusion(f32[256,40,64]{0,2,1:T(8,128)} %get-tuple-element.248, s32[]{:T(128)S(6)} %select_n.58, f32[256,256]{1,0:T(8,128)S(1)} %get-tuple-element.262, f32[8,256]{1,0:T(8,128)S(1)} %get-tuple-element.235, f32[8,256]{1,0:T(8,128)S(1)} %get-tuple-element.236, pred[256,256]{1,0:T(8,128)(4,1)S(1)} %iota_compare_fusion.6, ...), kind=kOutput, calls=%fused_computation.8.clone.1 | convolution fusion | flops 404750336 | bytes 1401856 | tf_op jit(solution)/shard_map/while/body/eval_jaxpr/hts,shp->thp/dot_general | solution.py:43
  188.9 4.4 %fusion.79 = f32[256,40,64]{0,2,1:T(8,128)} fusion(f32[256,40,64]{0,2,1:T(8,128)} %get-tuple-element.248, s32[]{:T(128)S(6)} %select_n.58, f32[256,256]{1,0:T(8,128)S(1)} %get-tuple-element.262, f32[8,256]{1,0:T(8,128)S(1)} %get-tuple-element.235, f32[8,256]{1,0:T(8,128)S(1)} %get-tuple-element.236, pred[256,256]{1,0:T(8,128)(4,1)S(1)} %iota_compare_fusion.6, ...), kind=kOutput, calls=%fused_computation.8.clone.1 | convolution fusion | flops 404750336 | bytes 1401856 | tf_op jit(solution)/shard_map/while/body/eval_jaxpr/hts,shp->thp/dot_general | solution.py:43
  193.3 4.4 %fusion.79 = f32[256,40,64]{0,2,1:T(8,128)} fusion(f32[256,40,64]{0,2,1:T(8,128)} %get-tuple-element.248, s32[]{:T(128)S(6)} %select_n.58, f32[256,256]{1,0:T(8,128)S(1)} %get-tuple-element.262, f32[8,256]{1,0:T(8,128)S(1)} %get-tuple-element.235, f32[8,256]{1,0:T(8,128)S(1)} %get-tuple-element.236, pred[256,256]{1,0:T(8,128)(4,1)S(1)} %iota_compare_fusion.6, ...), kind=kOutput, calls=%fused_computation.8.clone.1 | convolution fusion | flops 404750336 | bytes 1401856 | tf_op jit(solution)/shard_map/while/body/eval_jaxpr/hts,shp->thp/dot_general | solution.py:43
  197.7 4.4 %fusion.79 = f32[256,40,64]{0,2,1:T(8,128)} fusion(f32[256,40,64]{0,2,1:T(8,128)} %get-tuple-element.248, s32[]{:T(128)S(6)} %select_n.58, f32[256,256]{1,0:T(8,128)S(1)} %get-tuple-element.262, f32[8,256]{1,0:T(8,128)S(1)} %get-tuple-element.235, f32[8,256]{1,0:T(8,128)S(1)} %get-tuple-element.236, pred[256,256]{1,0:T(8,128)(4,1)S(1)} %iota_compare_fusion.6, ...), kind=kOutput, calls=%fused_computation.8.clone.1 | convolution fusion | flops 404750336 | bytes 1401856 | tf_op jit(solution)/shard_map/while/body/eval_jaxpr/hts,shp->thp/dot_general | solution.py:43
  202.1 4.3 %fusion.79 = f32[256,40,64]{0,2,1:T(8,128)} fusion(f32[256,40,64]{0,2,1:T(8,128)} %get-tuple-element.248, s32[]{:T(128)S(6)} %select_n.58, f32[256,256]{1,0:T(8,128)S(1)} %get-tuple-element.262, f32[8,256]{1,0:T(8,128)S(1)} %get-tuple-element.235, f32[8,256]{1,0:T(8,128)S(1)} %get-tuple-element.236, pred[256,256]{1,0:T(8,128)(4,1)S(1)} %iota_compare_fusion.6, ...), kind=kOutput, calls=%fused_computation.8.clone.1 | convolution fusion | flops 404750336 | bytes 1401856 | tf_op jit(solution)/shard_map/while/body/eval_jaxpr/hts,shp->thp/dot_general | solution.py:43
  206.4 176.3 %reduce-scatter.2.cloned.1.call-done = f32[80,128]{1,0:T(8,128)} async-done(((f32[2560,128]{1,0:T(8,128)}), f32[80,128]{1,0:T(8,128)}) %reduce-scatter.2.cloned.1.call-update) | async-done | bytes 40976 | tf_op jit(solution)/shard_map/reduce_scatter | solution.py:135
  382.7 24.5 %all-reduce.1 = f32[80,128]{1,0:T(8,128)S(1)} all-reduce(f32[80,128]{1,0:T(8,128)} %reduce-scatter.2.cloned.1.call-done), channel_id=4, replica_groups=mesh['dp'=32,'seq'=8] {'seq'}, use_global_device_ids=true, to_apply=%region_10.11.clone | all-reduce | flops 10240 | bytes 81920
  407.8 7.0 %multiply_reduce_fusion = (f32[256]{0:T(256)S(1)}, f32[256,40,64]{0,2,1:T(8,128)}) fusion(f32[256,40,64]{0,2,1:T(8,128)} %bitcast.193, f32[256,40,64]{0,2,1:T(8,128)} %get-tuple-element.270, f32[40]{0:T(128)S(1)} %copy-done.5, f32[256,40,64]{0,2,1:T(8,128)} %get-tuple-element.126, f32[40,64,128]{2,1,0:T(8,128)} %collective-permute-done.7, ...), kind=kOutput, calls=%fused_computation.37 | convolution fusion | flops 1013841664 | bytes 11904512 | tf_op jit(solution)/shard_map/tn,hpn->thp/dot_general | solution.py:73
  414.8 3.3 copy.74
  418.2 3.8 multiply_convert_fusion.1
  (92 shorter events, 49.4 us)
Async XLA Ops:
  7.2 375.6 %reduce-scatter.2.cloned.1.call-start = ((), (), s32[]{:S(2)}) async-start(), calls=%async_computation.1 | async-start | bytes 1351680 | tf_op jit(solution)/shard_map/reduce_scatter | solution.py:135
  8.0 24.5 %collective-permute-start = (bf16[1,3,2816]{2,1,0:T(4,128)(2,1)S(1)}, bf16[1,3,2816]{2,1,0:T(4,128)(2,1)S(1)}, u32[]{:S(2)}, u32[]{:S(2)}) collective-permute-start(bf16[1,3,2816]{2,1,0:T(4,128)(2,1)S(1)} %slice.100), channel_id=1, source_target_pairs={{0,1},{1,2},{2,3},{3,4},{4,5},{5,6},{6,7},{8,9},{9,10},{10,11},{11... | collective-permute-start | bytes 50696 | tf_op jit(solution)/shard_map/ppermute | solution.py:20
  29.1 3.4 copy-start.2
  32.5 0.7 copy-start.4
  33.2 1.9 copy-start
  43.2 4.9 %collective-permute-start.1 = (f32[40,64,128]{2,1,0:T(8,128)S(1)}, f32[40,64,128]{2,1,0:T(8,128)S(1)}, u32[]{:S(2)}, u32[]{:S(2)}) collective-permute-start(f32[40,64,128]{2,1,0:T(8,128)S(1)} %get-tuple-element.192), channel_id=1, source_target_pairs={{0,1},{1,2},{2,3},{3,4},{4,5},{5,6},{6,7},{8,9},{9,10},{10,11},{11... | collective-permute-start | bytes 3932168 | tf_op jit(solution)/shard_map/ppermute | solution.py:20
  48.3 16.5 %collective-permute-start.2 = (f32[40,64,128]{2,1,0:T(8,128)S(1)}, f32[40,64,128]{2,1,0:T(8,128)S(1)}, u32[]{:S(2)}, u32[]{:S(2)}) collective-permute-start(f32[40,64,128]{2,1,0:T(8,128)S(1)} %multiply_add_fusion.6), channel_id=1, source_target_pairs={{0,1},{1,2},{2,3},{3,4},{4,5},{5,6},{6,7},{8,9},{9,10},{10,11},{11... | collective-permute-start | bytes 3932168 | tf_op jit(solution)/shard_map/ppermute | solution.py:20
  65.0 18.9 %collective-permute-start.3 = (f32[40,64,128]{2,1,0:T(8,128)S(1)}, f32[40,64,128]{2,1,0:T(8,128)S(1)}, u32[]{:S(2)}, u32[]{:S(2)}) collective-permute-start(f32[40,64,128]{2,1,0:T(8,128)S(1)} %multiply_add_fusion.5), channel_id=1, source_target_pairs={{0,1},{1,2},{2,3},{3,4},{4,5},{5,6},{6,7},{8,9},{9,10},{10,11},{11... | collective-permute-start | bytes 3932168 | tf_op jit(solution)/shard_map/ppermute | solution.py:20
  84.2 18.9 %collective-permute-start.4 = (f32[40,64,128]{2,1,0:T(8,128)S(1)}, f32[40,64,128]{2,1,0:T(8,128)S(1)}, u32[]{:S(2)}, u32[]{:S(2)}) collective-permute-start(f32[40,64,128]{2,1,0:T(8,128)S(1)} %multiply_add_fusion.4), channel_id=1, source_target_pairs={{0,1},{1,2},{2,3},{3,4},{4,5},{5,6},{6,7},{8,9},{9,10},{10,11},{11... | collective-permute-start | bytes 3932168 | tf_op jit(solution)/shard_map/ppermute | solution.py:20
  104.4 51.9 %collective-permute-start.5 = (f32[40,64,128]{2,1,0:T(8,128)}, f32[40,64,128]{2,1,0:T(8,128)}, u32[]{:S(2)}, u32[]{:S(2)}) collective-permute-start(f32[40,64,128]{2,1,0:T(8,128)} %multiply_add_fusion.3), channel_id=1, source_target_pairs={{0,1},{1,2},{2,3},{3,4},{4,5},{5,6},{6,7},{8,9},{9,10},{10,11},{11... | collective-permute-start | bytes 3932168 | tf_op jit(solution)/shard_map/ppermute | solution.py:20
  126.6 3.9 copy-start.7
  126.6 28.5 %copy-start.6 = (u32[256]{0:T(256)S(1)}, u32[256]{0:T(256)}, u32[]{:S(2)}) copy-start(u32[256]{0:T(256)} %constant.88) | copy-start | bytes 3076
  158.9 12.7 %collective-permute-start.6 = (f32[40,64,128]{2,1,0:T(8,128)}, f32[40,64,128]{2,1,0:T(8,128)}, u32[]{:S(2)}, u32[]{:S(2)}) collective-permute-start(f32[40,64,128]{2,1,0:T(8,128)} %multiply_add_fusion.2), channel_id=1, source_target_pairs={{0,1},{1,2},{2,3},{3,4},{4,5},{5,6},{6,7},{8,9},{9,10},{10,11},{11... | collective-permute-start | bytes 3932168 | tf_op jit(solution)/shard_map/ppermute | solution.py:20
  174.2 233.6 %collective-permute-start.7 = (f32[40,64,128]{2,1,0:T(8,128)}, f32[40,64,128]{2,1,0:T(8,128)}, u32[]{:S(2)}, u32[]{:S(2)}) collective-permute-start(f32[40,64,128]{2,1,0:T(8,128)} %multiply_add_fusion.1), channel_id=1, source_target_pairs={{0,1},{1,2},{2,3},{3,4},{4,5},{5,6},{6,7},{8,9},{9,10},{10,11},{11... | collective-permute-start | bytes 3932168 | tf_op jit(solution)/shard_map/ppermute | solution.py:20
  184.5 223.3 %copy-start.5 = (f32[40]{0:T(128)S(1)}, f32[40]{0:T(128)}, u32[]{:S(2)}) copy-start(f32[40]{0:T(128)} %param.20) | copy-start | bytes 484
  414.8 3.3 copy-start.1
  414.8 3.3 copy-start.3
Sparse Core Ops, SparseCore 0:
  171.6 211.1 reduce-scatter.1

commit v2 on v1

--- a/solution.py
+++ b/solution.py
@@ -2,12 +2,106 @@
 import jax.numpy as jnp
 from jax import lax
 from jax.sharding import PartitionSpec as P
+from jax.experimental import pallas as pl
+from jax.experimental.pallas import tpu as pltpu
+import functools
 
 H = 40
 P_SIZE = 64
 N = 128
 KW = 4
 R = 4
+
+
+MESH_ID = pl.DeviceIdType.MESH
+
+
+def _halving_plan(dp_count, seq_count):
+    plan = []
+    bit = 1
+    while bit < seq_count:
+        plan.append(("seq", bit))
+        bit *= 2
+    bit = 1
+    while bit < dp_count:
+        plan.append(("dp", bit))
+        bit *= 2
+    return plan
+
+
+def _reduce_scatter_kernel(plan, in_ref, out_ref, acc, *rest):
+    rounds = len(plan)
+    recv = rest[:rounds]
+    send_sem, recv_sem = rest[rounds], rest[rounds + 1]
+    coords = {"dp": lax.axis_index("dp"), "seq": lax.axis_index("seq")}
+
+    def partner_of(axis, bit):
+        me = coords[axis]
+        return me + bit - 2 * bit * ((me // bit) % 2)
+
+    def device_of(axis, bit):
+        if axis == "dp":
+            return (partner_of(axis, bit), coords["seq"])
+        return (coords["dp"], partner_of(axis, bit))
+
+    barrier = pltpu.get_barrier_semaphore()
+    for axis, bit in plan:
+        pl.semaphore_signal(barrier, inc=1, device_id=device_of(axis, bit), device_id_type=MESH_ID)
+    pl.semaphore_wait(barrier, rounds)
+
+    size = in_ref.shape[0]
+    base = 0
+    copies = []
+    for index, (axis, bit) in enumerate(plan):
+        half = size // 2
+        mine = (coords[axis] // bit) % 2
+        keep = base + mine * half
+        give = base + (1 - mine) * half
+        source = in_ref if index == 0 else acc
+        copy = pltpu.make_async_remote_copy(
+            src_ref=source.at[pl.ds(give, half)],
+            dst_ref=recv[index],
+            send_sem=send_sem.at[index],
+            recv_sem=recv_sem.at[index],
+            device_id=device_of(axis, bit),
+            device_id_type=MESH_ID,
+        )
+        copy.start()
+        copy.wait_recv()
+        acc[pl.ds(keep, half)] = source[pl.ds(keep, half)] + recv[index][...]
+        copies.append(copy)
+        base = keep
+        size = half
+    out_ref[...] = acc[pl.ds(base, 1)]
+    for copy in copies:
+        copy.wait_send()
+
+
+def reduce_scatter_blocks(blocks):
+    dp_count = lax.axis_size("dp")
+    seq_count = lax.axis_size("seq")
+    plan = _halving_plan(dp_count, seq_count)
+    n_blocks, rows, cols = blocks.shape
+    recv_shapes = [pltpu.VMEM((n_blocks >> (i + 1), rows, cols), blocks.dtype) for i in range(len(plan))]
+    return pl.pallas_call(
+        functools.partial(_reduce_scatter_kernel, plan),
+        out_shape=jax.ShapeDtypeStruct((1, rows, cols), blocks.dtype),
+        in_specs=[pl.BlockSpec(memory_space=pltpu.VMEM)],
+        out_specs=pl.BlockSpec(memory_space=pltpu.VMEM),
+        scratch_shapes=[pltpu.VMEM((n_blocks, rows, cols), blocks.dtype)] + recv_shapes + [
+            pltpu.SemaphoreType.DMA((len(plan),)),
+            pltpu.SemaphoreType.DMA((len(plan),)),
+        ],
+        compiler_params=pltpu.CompilerParams(collective_id=1, has_side_effects=True),
+    )(blocks)
+
+
+def to_halving_order(partial, dp_count, seq_count, rows):
+    total_bits = (dp_count * seq_count).bit_length() - 1
+    cols = partial.shape[-1]
+    view = partial.reshape((2,) * total_bits + (rows, cols))
+    order = tuple(range(total_bits - 1, -1, -1)) + (total_bits, total_bits + 1)
+    return view.transpose(order).reshape(dp_count * seq_count, rows, cols)
 
 
 group_heads = 8
@@ -132,8 +226,9 @@
     class_value = labels[0].astype(jnp.float32)
     class_weight = class_value / n_one - (1.0 - class_value) / (batch_count - n_one)
     partial_value = class_weight * mean_local
-    steering = lax.psum_scatter(partial_value, "dp", scatter_dimension=0, tiled=True)
-    steering = lax.psum_scatter(steering, "seq", scatter_dimension=0, tiled=True)
+    block_rows = partial_value.shape[0] // (batch_count * seq_count)
+    blocks = to_halving_order(partial_value, batch_count, seq_count, block_rows)
+    steering = reduce_scatter_blocks(blocks)[0]
     h_in = jnp.zeros((H, P_SIZE, N), jnp.float32)
     for step_index in range(seq_count - 1):
         h_in = from_behind(decay_total[:, None, None] * h_in + local_state, "seq", 1)

time: 430 us -> 257 us (0.60)
  waiting for transfers between devices: 187 us -> 10.3 us
  Pallas kernels: 0 us -> 39.7 us
  blocking collectives: 56.7 us -> 32.3 us
  between operations: 16.9 us -> 2.88 us
  starting transfers between devices: 79 us -> 71.8 us
  local copies, waits for them, and re-layouts: 31.1 us -> 36.4 us
    reduce_scatter x1 -> x0, waiting for transfers between devices: 176 us -> none  [on_device(): lax.psum_scatter(partial_value, 'dp', scatter_dimension=0, tiled=True)]
    pallas_call x0 -> x1, Pallas kernels: none -> 39.7 us  [reduce_scatter_blocks(): pl.pallas_call(functools.partial(_reduce_scatter_kernel, plan), out_shape...]
    unnamed x2 -> x1, blocking collectives: 45.7 us -> 21.3 us
    ppermute x8, starting transfers between devices: 78.9 us -> 71.8 us  [from_behind(): return lax.ppermute(block, axis, route)]
  transfers between devices with their start and end apart: 9 -> 8, of which waited for: 5 -> 4; matrix products, arithmetic and copies ran while one was open for 14% -> 24% of each run, Pallas kernels for 0% -> 16%
where the time goes in v2:
time: 257 us; the launch traced here: 252 us
  starting transfers between devices  71.8 us (28%)
  Pallas kernels  39.7 us (15%)
  matrix products  37.3 us (15%)
  local copies, waits for them, and re-layouts  36.4 us (14%)
  blocking collectives  32.3 us (13%)
  other arithmetic  21.4 us (8%)
  waiting for transfers between devices  10.3 us (4%)
  between operations  2.88 us (1%)
    ppermute x8, starting transfers between devices, from_behind(): return lax.ppermute(block, axis, route)  71.8 us
    pallas_call x1, Pallas kernels, reduce_scatter_blocks(): pl.pallas_call(functools.partial(_reduce_scatter_kernel, plan), out_shape...  39.7 us
    dot_general x5, matrix products, group_step(): jnp.einsum('hts,shp->thp', weight, x_group, precision=highest)  21.7 us
    unnamed x1, blocking collectives  21.3 us
    all_gather x1, blocking collectives, on_device(): scalars = lax.all_gather(jnp.stack([decay_total, carry_weight]), 'seq')  11 us
    ppermute x8, waiting for transfers between devices, from_behind(): return lax.ppermute(block, axis, route)  10.3 us
    add x6, other arithmetic, on_device(): decay_total[:, None, None] * h_in + local_state  7.12 us
    dot_general x1, matrix products, finish_block(): incoming = jnp.einsum('tn,hpn->thp', c_wide, h_in, precision=highest)  7.05 us
  transfers between devices with their start and end apart: 8, of which 4 were waited for; matrix products, arithmetic and copies ran while one was open for 24% of the time, Pallas kernels for 16%

profile of v2, /device:TPU:6, one launch (start us, length us, event | category | flops | bytes accessed | tf_op | source)
XLA Modules:
  0.0 251.9 jit_solution(12718198536122036425)
XLA Ops:
  7.6 11.0 %all-gather.1 = f32[8,2,40]{2,1,0:T(2,128)S(1)} all-gather(f32[1,2,40]{2,1,0:T(2,128)S(1)} %maximum_bitcast_fusion), channel_id=2, replica_groups=mesh['dp'=32,'seq'=8] {'seq'}, dimensions={0}, use_global_device_ids=true | all-gather | bytes 2880 | tf_op jit(solution)/shard_map/all_gather | solution.py:212
  21.6 3.4 %copy.77 = f32[256,2560]{1,0:T(8,128)} copy(f32[256,2560]{0,1:T(8,128)} %bitcast.191) | data formatting | bytes 5242880 | tf_op jit(solution)/shard_map/mul | solution.py:148
  29.4 3.3 %copy.78 = f32[2560,256]{1,0:T(8,128)} copy(f32[2560,256]{0,1:T(8,128)} %multiply_bitcast_fusion) | data formatting | bytes 5242880 | tf_op jit(solution)/shard_map/sk,sn->kn/dot_general | solution.py:146
  32.7 3.0 %broadcast_add_fusion = (f32[40,64,128]{2,1,0:T(8,128)S(1)}, f32[40,64,128]{2,1,0:T(8,128)S(1)}) fusion(f32[40]{0:T(128)S(1)} %get-tuple-element.184, f32[40,64,256]{2,1,0:T(8,128)} %bitcast.190, bf16[256,2816]{1,0:T(8,128)(2,1)S(1)} %multiply_convert_fusion), kind=kOutput, calls=%fused_computation.48 | convolution fusion | flops 1006960640 | bytes 5308928 | tf_op jit(solution)/shard_map/sk,sn->kn/dot_general | solution.py:146
  40.8 13.9 %collective-permute-start.2 = (f32[40,64,128]{2,1,0:T(8,128)S(1)}, f32[40,64,128]{2,1,0:T(8,128)S(1)}, u32[]{:S(2)}, u32[]{:S(2)}) collective-permute-start(f32[40,64,128]{2,1,0:T(8,128)S(1)} %multiply_add_fusion.6), channel_id=1, source_target_pairs={{0,1},{1,2},{2,3},{3,4},{4,5},{5,6},{6,7},{8,9},{9,10},{10,11},{11... | collective-permute-start | bytes 3932168 | tf_op jit(solution)/shard_map/ppermute | solution.py:114
  57.5 16.4 %collective-permute-start.3 = (f32[40,64,128]{2,1,0:T(8,128)S(1)}, f32[40,64,128]{2,1,0:T(8,128)S(1)}, u32[]{:S(2)}, u32[]{:S(2)}) collective-permute-start(f32[40,64,128]{2,1,0:T(8,128)S(1)} %multiply_add_fusion.5), channel_id=1, source_target_pairs={{0,1},{1,2},{2,3},{3,4},{4,5},{5,6},{6,7},{8,9},{9,10},{10,11},{11... | collective-permute-start | bytes 3932168 | tf_op jit(solution)/shard_map/ppermute | solution.py:114
  76.7 16.4 %collective-permute-start.4 = (f32[40,64,128]{2,1,0:T(8,128)S(1)}, f32[40,64,128]{2,1,0:T(8,128)S(1)}, u32[]{:S(2)}, u32[]{:S(2)}) collective-permute-start(f32[40,64,128]{2,1,0:T(8,128)S(1)} %multiply_add_fusion.4), channel_id=1, source_target_pairs={{0,1},{1,2},{2,3},{3,4},{4,5},{5,6},{6,7},{8,9},{9,10},{10,11},{11... | collective-permute-start | bytes 3932168 | tf_op jit(solution)/shard_map/ppermute | solution.py:114
  96.9 17.4 %collective-permute-start.5 = (f32[40,64,128]{2,1,0:T(8,128)}, f32[40,64,128]{2,1,0:T(8,128)}, u32[]{:S(2)}, u32[]{:S(2)}) collective-permute-start(f32[40,64,128]{2,1,0:T(8,128)} %multiply_add_fusion.3), channel_id=1, source_target_pairs={{0,1},{1,2},{2,3},{3,4},{4,5},{5,6},{6,7},{8,9},{9,10},{10,11},{11... | collective-permute-start | bytes 3932168 | tf_op jit(solution)/shard_map/ppermute | solution.py:114
  114.4 2.8 %copy.80 = f32[1,256,2560]{1,2,0:T(8,128)} copy(bf16[1,256,2560]{2,1,0:T(8,128)(2,1)} %param.14) | data formatting | bytes 3932160 | tf_op jit(solution)/shard_map/convert_element_type | solution.py:171
  119.1 3.2 %copy.84 = f32[256,2560]{1,0:T(8,128)} copy(f32[256,2560]{0,1:T(8,128)} %bitcast.192) | data formatting | bytes 5242880 | tf_op jit(solution)/shard_map/mul | solution.py:221
  124.4 21.3 %all-reduce = s32[32]{0:T(128)S(1)} all-reduce(s32[32]{0:T(128)S(1)} %dynamic-update-slice), channel_id=1, replica_groups=mesh['dp'=32,'seq'=8] {'dp'}, use_global_device_ids=true, to_apply=%add | all-reduce | flops 32 | bytes 256
  154.4 3.3 %copy.69 = f32[256,2560]{0,1:T(8,128)} copy(f32[256,2560]{1,0:T(8,128)} %slice_convert_fusion) | data formatting | bytes 5242880 | tf_op jit(solution)/shard_map/convert_element_type | solution.py:119
  157.6 5.0 %convolution_multiply_fusion = f32[2560,128]{1,0:T(8,128)} fusion(f32[256,2560]{1,0:T(8,128)} %copy.84, bf16[256,2816]{1,0:T(8,128)(2,1)S(1)} %multiply_convert_fusion, f32[]{:T(128)S(6)} %sub.87), kind=kOutput, calls=%fused_computation.21 | convolution fusion | flops 1008271360 | bytes 5308420 | tf_op jit(solution)/shard_map/sk,sn->kn/dot_general | solution.py:219
  165.3 3.2 %copy.85 = f32[2,2,2,2,2,2,2,2,10,128]{9,8,7,6,5,4,3,2,1,0:T(8,128)} copy(f32[2,2,2,2,2,2,2,2,10,128]{9,8,0,1,2,3,4,5,6,7:T(8,128)} %bitcast.193) | data formatting | bytes 2621440 | tf_op jit(solution)/shard_map/transpose | solution.py:104
  168.5 39.7 %shard_map.122 = f32[1,10,128]{2,1,0:T(8,128)} custom-call(f32[256,10,128]{2,1,0:T(8,128)} %bitcast.194), custom_call_target="tpu_custom_call" | custom-call | tf_op jit(solution)/shard_map/pallas_call | solution.py:86
  214.2 21.9 %while.14 = (s32[]{:T(128)}, f32[256,40,64]{0,2,1:T(8,128)}, f32[256,40,64]{0,2,1:T(8,128)}, f32[40,256]{1,0:T(8,128)S(1)}, f32[40,256]{1,0:T(8,128)S(1)}, /*ind...) while((s32[]{:T(128)}, f32[256,40,64]{0,2,1:T(8,128)}, ...), condition=%wide.region_3.4_spmd.clone, body=%wide.region_2.3_spmd.clone.sunk | while | flops 404815872 | bytes 1500311 | solution.py:140
  214.2 4.3 %fusion.79 = f32[256,40,64]{0,2,1:T(8,128)} fusion(f32[256,40,64]{0,2,1:T(8,128)} %get-tuple-element.248, s32[]{:T(128)S(6)} %select_n.58, f32[256,256]{1,0:T(8,128)S(1)} %get-tuple-element.262, f32[8,256]{1,0:T(8,128)S(1)} %get-tuple-element.235, f32[8,256]{1,0:T(8,128)S(1)} %get-tuple-element.236, pred[256,256]{1,0:T(8,128)(4,1)S(1)} %iota_compare_fusion.6, ...), kind=kOutput, calls=%fused_computation.8.clone.1 | convolution fusion | flops 404750336 | bytes 1401856 | tf_op jit(solution)/shard_map/while/body/eval_jaxpr/hts,shp->thp/dot_general | solution.py:137
  218.6 4.3 %fusion.79 = f32[256,40,64]{0,2,1:T(8,128)} fusion(f32[256,40,64]{0,2,1:T(8,128)} %get-tuple-element.248, s32[]{:T(128)S(6)} %select_n.58, f32[256,256]{1,0:T(8,128)S(1)} %get-tuple-element.262, f32[8,256]{1,0:T(8,128)S(1)} %get-tuple-element.235, f32[8,256]{1,0:T(8,128)S(1)} %get-tuple-element.236, pred[256,256]{1,0:T(8,128)(4,1)S(1)} %iota_compare_fusion.6, ...), kind=kOutput, calls=%fused_computation.8.clone.1 | convolution fusion | flops 404750336 | bytes 1401856 | tf_op jit(solution)/shard_map/while/body/eval_jaxpr/hts,shp->thp/dot_general | solution.py:137
  223.0 4.3 %fusion.79 = f32[256,40,64]{0,2,1:T(8,128)} fusion(f32[256,40,64]{0,2,1:T(8,128)} %get-tuple-element.248, s32[]{:T(128)S(6)} %select_n.58, f32[256,256]{1,0:T(8,128)S(1)} %get-tuple-element.262, f32[8,256]{1,0:T(8,128)S(1)} %get-tuple-element.235, f32[8,256]{1,0:T(8,128)S(1)} %get-tuple-element.236, pred[256,256]{1,0:T(8,128)(4,1)S(1)} %iota_compare_fusion.6, ...), kind=kOutput, calls=%fused_computation.8.clone.1 | convolution fusion | flops 404750336 | bytes 1401856 | tf_op jit(solution)/shard_map/while/body/eval_jaxpr/hts,shp->thp/dot_general | solution.py:137
  227.3 4.4 %fusion.79 = f32[256,40,64]{0,2,1:T(8,128)} fusion(f32[256,40,64]{0,2,1:T(8,128)} %get-tuple-element.248, s32[]{:T(128)S(6)} %select_n.58, f32[256,256]{1,0:T(8,128)S(1)} %get-tuple-element.262, f32[8,256]{1,0:T(8,128)S(1)} %get-tuple-element.235, f32[8,256]{1,0:T(8,128)S(1)} %get-tuple-element.236, pred[256,256]{1,0:T(8,128)(4,1)S(1)} %iota_compare_fusion.6, ...), kind=kOutput, calls=%fused_computation.8.clone.1 | convolution fusion | flops 404750336 | bytes 1401856 | tf_op jit(solution)/shard_map/while/body/eval_jaxpr/hts,shp->thp/dot_general | solution.py:137
  231.7 4.3 %fusion.79 = f32[256,40,64]{0,2,1:T(8,128)} fusion(f32[256,40,64]{0,2,1:T(8,128)} %get-tuple-element.248, s32[]{:T(128)S(6)} %select_n.58, f32[256,256]{1,0:T(8,128)S(1)} %get-tuple-element.262, f32[8,256]{1,0:T(8,128)S(1)} %get-tuple-element.235, f32[8,256]{1,0:T(8,128)S(1)} %get-tuple-element.236, pred[256,256]{1,0:T(8,128)(4,1)S(1)} %iota_compare_fusion.6, ...), kind=kOutput, calls=%fused_computation.8.clone.1 | convolution fusion | flops 404750336 | bytes 1401856 | tf_op jit(solution)/shard_map/while/body/eval_jaxpr/hts,shp->thp/dot_general | solution.py:137
  237.1 7.0 %multiply_reduce_fusion = (f32[256]{0:T(256)S(1)}, f32[256,40,64]{0,2,1:T(8,128)}) fusion(f32[256,40,64]{0,2,1:T(8,128)} %bitcast.197, f32[256,40,64]{0,2,1:T(8,128)} %get-tuple-element.271, f32[40]{0:T(128)S(1)} %copy-done.8, f32[256,40,64]{0,2,1:T(8,128)} %get-tuple-element.126, f32[40,64,128]{2,1,0:T(8,128)} %copy-done.7, ...), kind=kOutput, calls=%fused_computation.37 | convolution fusion | flops 1013841664 | bytes 11904512 | tf_op jit(solution)/shard_map/tn,hpn->thp/dot_general | solution.py:167
  244.2 3.3 %copy.79 = f32[1,256,2560]{2,1,0:T(8,128)} copy(f32[1,256,2560]{1,2,0:T(8,128)} %bitcast.196) | data formatting | bytes 5242880 | tf_op jit(solution)/shard_map/reshape | solution.py:171
  247.5 3.8 %multiply_convert_fusion.1 = bf16[1,256,2560]{2,1,0:T(8,128)(2,1)} fusion(f32[1,256,2560]{2,1,0:T(8,128)} %copy.79, f32[2560]{0:T(1024)S(1)} %copy-done.5, f32[256]{0:T(256)S(1)} %add_rsqrt_fusion, bf16[1,256,2560]{2,1,0:T(8,128)(2,1)S(1)} %copy-done.1), kind=kLoop, calls=%fused_computation.36 | loop fusion | flops 5898240 | bytes 5254144 | tf_op jit(solution)/shard_map/convert_element_type | solution.py:173
  (94 shorter events, 49.9 us)
Async XLA Ops:
  0.6 19.1 %copy-start.3 = (f32[4,2816]{1,0:T(4,128)S(1)}, f32[4,2816]{1,0:T(4,128)}, u32[]{:S(2)}) copy-start(f32[4,2816]{1,0:T(4,128)} %param.16) | copy-start | bytes 135172
  1.5 23.5 %collective-permute-start = (bf16[1,3,2816]{2,1,0:T(4,128)(2,1)S(1)}, bf16[1,3,2816]{2,1,0:T(4,128)(2,1)S(1)}, u32[]{:S(2)}, u32[]{:S(2)}) collective-permute-start(bf16[1,3,2816]{2,1,0:T(4,128)(2,1)S(1)} %slice.100), channel_id=1, source_target_pairs={{0,1},{1,2},{2,3},{3,4},{4,5},{5,6},{6,7},{8,9},{9,10},{10,11},{11... | collective-permute-start | bytes 50696 | tf_op jit(solution)/shard_map/ppermute | solution.py:114
  21.6 3.4 %copy-start.2 = (bf16[1,256,2816]{2,1,0:T(8,128)(2,1)S(1)}, bf16[1,256,2816]{2,1,0:T(8,128)(2,1)}, u32[]{:S(2)}) copy-start(bf16[1,256,2816]{2,1,0:T(8,128)(2,1)} %param.13) | copy-start | bytes 4325380
  25.0 0.7 copy-start.6
  25.7 1.9 copy-start
  35.7 4.9 %collective-permute-start.1 = (f32[40,64,128]{2,1,0:T(8,128)S(1)}, f32[40,64,128]{2,1,0:T(8,128)S(1)}, u32[]{:S(2)}, u32[]{:S(2)}) collective-permute-start(f32[40,64,128]{2,1,0:T(8,128)S(1)} %get-tuple-element.192), channel_id=1, source_target_pairs={{0,1},{1,2},{2,3},{3,4},{4,5},{5,6},{6,7},{8,9},{9,10},{10,11},{11... | collective-permute-start | bytes 3932168 | tf_op jit(solution)/shard_map/ppermute | solution.py:114
  40.8 16.5 %collective-permute-start.2 = (f32[40,64,128]{2,1,0:T(8,128)S(1)}, f32[40,64,128]{2,1,0:T(8,128)S(1)}, u32[]{:S(2)}, u32[]{:S(2)}) collective-permute-start(f32[40,64,128]{2,1,0:T(8,128)S(1)} %multiply_add_fusion.6), channel_id=1, source_target_pairs={{0,1},{1,2},{2,3},{3,4},{4,5},{5,6},{6,7},{8,9},{9,10},{10,11},{11... | collective-permute-start | bytes 3932168 | tf_op jit(solution)/shard_map/ppermute | solution.py:114
  57.5 18.9 %collective-permute-start.3 = (f32[40,64,128]{2,1,0:T(8,128)S(1)}, f32[40,64,128]{2,1,0:T(8,128)S(1)}, u32[]{:S(2)}, u32[]{:S(2)}) collective-permute-start(f32[40,64,128]{2,1,0:T(8,128)S(1)} %multiply_add_fusion.5), channel_id=1, source_target_pairs={{0,1},{1,2},{2,3},{3,4},{4,5},{5,6},{6,7},{8,9},{9,10},{10,11},{11... | collective-permute-start | bytes 3932168 | tf_op jit(solution)/shard_map/ppermute | solution.py:114
  76.7 18.9 %collective-permute-start.4 = (f32[40,64,128]{2,1,0:T(8,128)S(1)}, f32[40,64,128]{2,1,0:T(8,128)S(1)}, u32[]{:S(2)}, u32[]{:S(2)}) collective-permute-start(f32[40,64,128]{2,1,0:T(8,128)S(1)} %multiply_add_fusion.4), channel_id=1, source_target_pairs={{0,1},{1,2},{2,3},{3,4},{4,5},{5,6},{6,7},{8,9},{9,10},{10,11},{11... | collective-permute-start | bytes 3932168 | tf_op jit(solution)/shard_map/ppermute | solution.py:114
  96.9 50.7 %collective-permute-start.5 = (f32[40,64,128]{2,1,0:T(8,128)}, f32[40,64,128]{2,1,0:T(8,128)}, u32[]{:S(2)}, u32[]{:S(2)}) collective-permute-start(f32[40,64,128]{2,1,0:T(8,128)} %multiply_add_fusion.3), channel_id=1, source_target_pairs={{0,1},{1,2},{2,3},{3,4},{4,5},{5,6},{6,7},{8,9},{9,10},{10,11},{11... | collective-permute-start | bytes 3932168 | tf_op jit(solution)/shard_map/ppermute | solution.py:114
  119.1 3.9 %copy-start.9 = (u32[256]{0:T(256)S(1)}, u32[256]{0:T(256)}, u32[]{:S(2)}) copy-start(u32[256]{0:T(256)} %constant.82) | copy-start | bytes 3076
  150.1 58.3 %collective-permute-start.6 = (f32[40,64,128]{2,1,0:T(8,128)}, f32[40,64,128]{2,1,0:T(8,128)}, u32[]{:S(2)}, u32[]{:S(2)}) collective-permute-start(f32[40,64,128]{2,1,0:T(8,128)} %multiply_add_fusion.2), channel_id=1, source_target_pairs={{0,1},{1,2},{2,3},{3,4},{4,5},{5,6},{6,7},{8,9},{9,10},{10,11},{11... | collective-permute-start | bytes 3932168 | tf_op jit(solution)/shard_map/ppermute | solution.py:114
  211.0 25.1 %collective-permute-start.7 = (f32[40,64,128]{2,1,0:T(8,128)}, f32[40,64,128]{2,1,0:T(8,128)S(1)}, u32[]{:S(2)}, u32[]{:S(2)}) collective-permute-start(f32[40,64,128]{2,1,0:T(8,128)} %multiply_add_fusion.1), channel_id=1, source_target_pairs={{0,1},{1,2},{2,3},{3,4},{4,5},{5,6},{6,7},{8,9},{9,10},{10,11},{11... | collective-permute-start | bytes 3932168 | tf_op jit(solution)/shard_map/ppermute | solution.py:114
  214.2 22.9 %copy-start.8 = (f32[40]{0:T(128)S(1)}, f32[40]{0:T(128)}, u32[]{:S(2)}) copy-start(f32[40]{0:T(128)} %param.20) | copy-start | bytes 484
  236.0 1.1 copy-start.7
  244.2 3.3 %copy-start.1 = (bf16[1,256,2560]{2,1,0:T(8,128)(2,1)S(1)}, bf16[1,256,2560]{2,1,0:T(8,128)(2,1)}, u32[]{:S(2)}) copy-start(bf16[1,256,2560]{2,1,0:T(8,128)(2,1)} %param.14) | copy-start | bytes 3932164
  244.2 3.3 %copy-start.5 = (f32[2560]{0:T(1024)S(1)}, f32[2560]{0:T(1024)}, u32[]{:S(2)}) copy-start(f32[2560]{0:T(1024)} %param.21) | copy-start | bytes 30724
  247.5 3.8 %copy-start.4 = (f32[1,10,128]{2,1,0:T(8,128)S(1)}, f32[1,10,128]{2,1,0:T(8,128)}, u32[]{:S(2)}) copy-start(f32[1,10,128]{2,1,0:T(8,128)} %shard_map.122) | copy-start | bytes 15364

commit v3 on v2

--- a/solution.py
+++ b/solution.py
@@ -102,6 +102,80 @@
     view = partial.reshape((2,) * total_bits + (rows, cols))
     order = tuple(range(total_bits - 1, -1, -1)) + (total_bits, total_bits + 1)
     return view.transpose(order).reshape(dp_count * seq_count, rows, cols)
+
+
+def _chain_kernel(chunk, local_ref, decay_ref, hin_ref, send_buf, send_sem, recv_sem):
+    count = lax.axis_size("seq")
+    me = lax.axis_index("seq")
+    row_id = lax.axis_index("dp")
+    has_left = (me + count - 1) // count
+    has_right = (2 * count - 2 - me) // count
+    left = me - has_left
+    right = me + has_right
+    pieces = local_ref.shape[0] // chunk
+
+    barrier = pltpu.get_barrier_semaphore()
+
+    @pl.when(has_left == 1)
+    def _():
+        pl.semaphore_signal(barrier, inc=1, device_id=(row_id, left), device_id_type=MESH_ID)
+
+    @pl.when(has_right == 1)
+    def _():
+        pl.semaphore_signal(barrier, inc=1, device_id=(row_id, right), device_id_type=MESH_ID)
+
+    pl.semaphore_wait(barrier, has_left + has_right)
+
+    def link(source, piece):
+        rows = pl.ds(piece * chunk, chunk)
+        return pltpu.make_async_remote_copy(
+            src_ref=source.at[rows],
+            dst_ref=hin_ref.at[rows],
+            send_sem=send_sem.at[piece],
+            recv_sem=recv_sem.at[piece],
+            device_id=(row_id, right),
+            device_id_type=MESH_ID,
+        )
+
+    @pl.when(has_left == 0)
+    def _():
+        hin_ref[...] = jnp.zeros_like(hin_ref)
+        for piece in range(pieces):
+            link(local_ref, piece).start()
+
+    @pl.when(has_left == 1)
+    def _():
+        for piece in range(pieces):
+            rows = pl.ds(piece * chunk, chunk)
+            link(send_buf, piece).wait_recv()
+
+            @pl.when(has_right == 1)
+            def _():
+                send_buf[rows] = decay_ref[rows] * hin_ref[rows] + local_ref[rows]
+                link(send_buf, piece).start()
+
+    @pl.when(has_right == 1)
+    def _():
+        for piece in range(pieces):
+            link(send_buf, piece).wait_send()
+
+
+def carry_chain(local_state, decay_total, pieces=8):
+    heads = local_state.shape[0]
+    chunk = heads // pieces
+    decay = jnp.broadcast_to(decay_total[:, None, None], (heads, 1, local_state.shape[2]))
+    return pl.pallas_call(
+        functools.partial(_chain_kernel, chunk),
+        out_shape=jax.ShapeDtypeStruct(local_state.shape, local_state.dtype),
+        in_specs=[pl.BlockSpec(memory_space=pltpu.VMEM)] * 2,
+        out_specs=pl.BlockSpec(memory_space=pltpu.VMEM),
+        scratch_shapes=[
+            pltpu.VMEM(local_state.shape, local_state.dtype),
+            pltpu.SemaphoreType.DMA((pieces,)),
+            pltpu.SemaphoreType.DMA((pieces,)),
+        ],
+        compiler_params=pltpu.CompilerParams(collective_id=2, has_side_effects=True),
+    )(local_state, decay)
 
 
 group_heads = 8
@@ -229,9 +303,7 @@
     block_rows = partial_value.shape[0] // (batch_count * seq_count)
     blocks = to_halving_order(partial_value, batch_count, seq_count, block_rows)
     steering = reduce_scatter_blocks(blocks)[0]
-    h_in = jnp.zeros((H, P_SIZE, N), jnp.float32)
-    for step_index in range(seq_count - 1):
-        h_in = from_behind(decay_total[:, None, None] * h_in + local_state, "seq", 1)
+    h_in = carry_chain(local_state, decay_total)
     layer_out = finish_block(
         diagonal_part, x_wide, c_wide, cumulative, h_in, gate_input[0], d_skip, norm_gain
     )

time: 257 us -> 195 us (0.76); the launches traced: 252 us -> 194 us
  starting transfers between devices: 71.8 us -> 1.74 us
  Pallas kernels: 39.7 us -> 73.2 us
  waiting for transfers between devices: 10.3 us -> 0.01 us
  other arithmetic: 21.4 us -> 15.3 us
  local copies, waits for them, and re-layouts: 36.4 us -> 31.4 us
    ppermute x8 -> x1, starting transfers between devices: 71.8 us -> 1.74 us  [from_behind(): return lax.ppermute(block, axis, route)]
    pallas_call x1, Pallas kernels: 39.7 us -> 68 us  [reduce_scatter_blocks(): pl.pallas_call(functools.partial(_reduce_scatter_kernel, plan), out_shape...]
    ppermute x8 -> x1, waiting for transfers between devices: 10.3 us -> 0.01 us  [from_behind(): return lax.ppermute(block, axis, route)]
    add x6 -> x0, other arithmetic: 7.12 us -> none  [on_device(): decay_total[:, None, None] * h_in + local_state]
    pallas_call x0 -> x1, Pallas kernels: none -> 5.28 us  [carry_chain(): pl.pallas_call(functools.partial(_chain_kernel, chunk), out_shape=jax.Sha...]
    mul x2, local copies, waits for them, and re-layouts: 5.08 us -> 2.32 us  [local_terms(): to_end[:, :, None] * x_wide]
    mul x2, local copies, waits for them, and re-layouts: 5.02 us -> 2.32 us  [on_device(): mean_weight[:, :, None] * x_wide]
  transfers between devices with their start and end apart: 8 -> 1, of which waited for: 4 -> 0; matrix products, arithmetic and copies ran while one was open for 24% -> 9% of each run, Pallas kernels for 16% -> 0%
where the time goes in v3:
time: 195 us; the launch traced here: 194 us
  Pallas kernels  73.2 us (38%)
  matrix products  37.3 us (19%)
  blocking collectives  32.2 us (17%)
  local copies, waits for them, and re-layouts  31.4 us (16%)
  other arithmetic  15.3 us (8%)
  between operations  2.85 us (1%)
    pallas_call x1, Pallas kernels, reduce_scatter_blocks(): pl.pallas_call(functools.partial(_reduce_scatter_kernel, plan), out_shape...  68 us
    dot_general x5, matrix products, group_step(): jnp.einsum('hts,shp->thp', weight, x_group, precision=highest)  21.8 us
    unnamed x1, blocking collectives  21.2 us
    all_gather x1, blocking collectives, on_device(): scalars = lax.all_gather(jnp.stack([decay_total, carry_weight]), 'seq')  11 us
    dot_general x1, matrix products, finish_block(): incoming = jnp.einsum('tn,hpn->thp', c_wide, h_in, precision=highest)  7.05 us
    pallas_call x1, Pallas kernels, carry_chain(): pl.pallas_call(functools.partial(_chain_kernel, chunk), out_shape=jax.Sha...  5.28 us
    unnamed x18, local copies, waits for them, and re-layouts  4.17 us
    dot_general x1, matrix products, local_terms(): jnp.einsum('sk,sn->kn', (to_end[:, :, None] * x_wide).reshape(row_count,...  4.06 us
  transfers between devices with their start and end apart: 1, of which 0 were waited for; matrix products, arithmetic and copies ran while one was open for 9% of the time, Pallas kernels for 0%

profile of v3, /device:TPU:6, one launch (start us, length us, event | category | flops | bytes accessed | tf_op | source)
XLA Modules:
  0.0 194.1 jit_solution(11241085053341124302)
XLA Ops:
  7.5 11.0 %all-gather.1 = f32[8,2,40]{2,1,0:T(2,128)S(1)} all-gather(f32[1,2,40]{2,1,0:T(2,128)S(1)} %maximum_bitcast_fusion), channel_id=2, replica_groups=mesh['dp'=32,'seq'=8] {'seq'}, dimensions={0}, use_global_device_ids=true | all-gather | bytes 2880 | tf_op jit(solution)/shard_map/all_gather | solution.py:286
  22.5 21.2 %all-reduce = s32[32]{0:T(128)S(1)} all-reduce(s32[32]{0:T(128)S(1)} %dynamic-update-slice), channel_id=1, replica_groups=mesh['dp'=32,'seq'=8] {'dp'}, use_global_device_ids=true, to_apply=%add | all-reduce | flops 32 | bytes 256
  45.6 2.1 %copy.76 = f32[256,2560]{1,0:T(8,128)} copy(f32[256,2560]{0,1:T(8,128)S(1)} %bitcast.186) | data formatting | bytes 5242880 | tf_op jit(solution)/shard_map/mul | solution.py:222
  47.9 2.9 %copy.79 = f32[1,256,2560]{1,2,0:T(8,128)} copy(bf16[1,256,2560]{2,1,0:T(8,128)(2,1)} %param.14) | data formatting | bytes 3932160 | tf_op jit(solution)/shard_map/convert_element_type | solution.py:245
  51.0 2.1 %copy.83 = f32[256,2560]{1,0:T(8,128)} copy(f32[256,2560]{0,1:T(8,128)S(1)} %bitcast.187) | data formatting | bytes 5242880 | tf_op jit(solution)/shard_map/mul | solution.py:295
  56.1 1.9 multiply_convert_fusion
  58.1 1.9 slice_convert_fusion
  60.7 1.8 multiply_bitcast_fusion
  62.6 3.2 %copy.77 = f32[2560,256]{1,0:T(8,128)} copy(f32[2560,256]{0,1:T(8,128)} %multiply_bitcast_fusion) | data formatting | bytes 5242880 | tf_op jit(solution)/shard_map/sk,sn->kn/dot_general | solution.py:220
  65.8 4.1 %fusion.38.local_ref = f32[40,64,128]{2,1,0:T(8,128)} fusion(f32[40,64,256]{2,1,0:T(8,128)} %bitcast.188, bf16[256,2816]{1,0:T(8,128)(2,1)S(1)} %multiply_convert_fusion), kind=kOutput, calls=%fused_computation.53 | convolution fusion | flops 1006632960 | bytes 3997696 | tf_op jit(solution)/shard_map/sk,sn->kn/dot_general | solution.py:220
  69.9 3.2 %copy.68 = f32[256,2560]{0,1:T(8,128)} copy(f32[256,2560]{1,0:T(8,128)} %slice_convert_fusion) | data formatting | bytes 5242880 | tf_op jit(solution)/shard_map/convert_element_type | solution.py:193
  74.9 21.9 %while.14 = (s32[]{:T(128)}, f32[256,40,64]{0,2,1:T(8,128)}, f32[256,40,64]{0,2,1:T(8,128)}, f32[40,256]{1,0:T(8,128)S(1)}, f32[40,256]{1,0:T(8,128)S(1)}, /*ind...) while((s32[]{:T(128)}, f32[256,40,64]{0,2,1:T(8,128)}, ...), condition=%wide.region_3.4_spmd.clone, body=%wide.region_2.3_spmd.clone.sunk | while | flops 404815872 | bytes 1500311 | solution.py:214
  75.0 4.4 %fusion.79 = f32[256,40,64]{0,2,1:T(8,128)} fusion(f32[256,40,64]{0,2,1:T(8,128)} %get-tuple-element.244, s32[]{:T(128)S(6)} %select_n.58, f32[256,256]{1,0:T(8,128)S(1)} %get-tuple-element.258, f32[8,256]{1,0:T(8,128)S(1)} %get-tuple-element.231, f32[8,256]{1,0:T(8,128)S(1)} %get-tuple-element.232, pred[256,256]{1,0:T(8,128)(4,1)S(1)} %iota_compare_fusion.6, ...), kind=kOutput, calls=%fused_computation.8.clone.1 | convolution fusion | flops 404750336 | bytes 1401856 | tf_op jit(solution)/shard_map/while/body/eval_jaxpr/hts,shp->thp/dot_general | solution.py:211
  79.4 4.4 %fusion.79 = f32[256,40,64]{0,2,1:T(8,128)} fusion(f32[256,40,64]{0,2,1:T(8,128)} %get-tuple-element.244, s32[]{:T(128)S(6)} %select_n.58, f32[256,256]{1,0:T(8,128)S(1)} %get-tuple-element.258, f32[8,256]{1,0:T(8,128)S(1)} %get-tuple-element.231, f32[8,256]{1,0:T(8,128)S(1)} %get-tuple-element.232, pred[256,256]{1,0:T(8,128)(4,1)S(1)} %iota_compare_fusion.6, ...), kind=kOutput, calls=%fused_computation.8.clone.1 | convolution fusion | flops 404750336 | bytes 1401856 | tf_op jit(solution)/shard_map/while/body/eval_jaxpr/hts,shp->thp/dot_general | solution.py:211
  83.7 4.3 %fusion.79 = f32[256,40,64]{0,2,1:T(8,128)} fusion(f32[256,40,64]{0,2,1:T(8,128)} %get-tuple-element.244, s32[]{:T(128)S(6)} %select_n.58, f32[256,256]{1,0:T(8,128)S(1)} %get-tuple-element.258, f32[8,256]{1,0:T(8,128)S(1)} %get-tuple-element.231, f32[8,256]{1,0:T(8,128)S(1)} %get-tuple-element.232, pred[256,256]{1,0:T(8,128)(4,1)S(1)} %iota_compare_fusion.6, ...), kind=kOutput, calls=%fused_computation.8.clone.1 | convolution fusion | flops 404750336 | bytes 1401856 | tf_op jit(solution)/shard_map/while/body/eval_jaxpr/hts,shp->thp/dot_general | solution.py:211
  88.1 4.3 %fusion.79 = f32[256,40,64]{0,2,1:T(8,128)} fusion(f32[256,40,64]{0,2,1:T(8,128)} %get-tuple-element.244, s32[]{:T(128)S(6)} %select_n.58, f32[256,256]{1,0:T(8,128)S(1)} %get-tuple-element.258, f32[8,256]{1,0:T(8,128)S(1)} %get-tuple-element.231, f32[8,256]{1,0:T(8,128)S(1)} %get-tuple-element.232, pred[256,256]{1,0:T(8,128)(4,1)S(1)} %iota_compare_fusion.6, ...), kind=kOutput, calls=%fused_computation.8.clone.1 | convolution fusion | flops 404750336 | bytes 1401856 | tf_op jit(solution)/shard_map/while/body/eval_jaxpr/hts,shp->thp/dot_general | solution.py:211
  92.5 4.4 %fusion.79 = f32[256,40,64]{0,2,1:T(8,128)} fusion(f32[256,40,64]{0,2,1:T(8,128)} %get-tuple-element.244, s32[]{:T(128)S(6)} %select_n.58, f32[256,256]{1,0:T(8,128)S(1)} %get-tuple-element.258, f32[8,256]{1,0:T(8,128)S(1)} %get-tuple-element.231, f32[8,256]{1,0:T(8,128)S(1)} %get-tuple-element.232, pred[256,256]{1,0:T(8,128)(4,1)S(1)} %iota_compare_fusion.6, ...), kind=kOutput, calls=%fused_computation.8.clone.1 | convolution fusion | flops 404750336 | bytes 1401856 | tf_op jit(solution)/shard_map/while/body/eval_jaxpr/hts,shp->thp/dot_general | solution.py:211
  97.6 5.3 %shard_map.122 = f32[40,64,128]{2,1,0:T(8,128)} custom-call(f32[40,64,128]{2,1,0:T(8,128)} %fusion.38.local_ref, f32[40,1,128]{2,1,0:T(1,128)} %broadcast_in_dim.101.decay_ref), custom_call_target="tpu_custom_call" | custom-call | tf_op jit(solution)/shard_map/pallas_call | solution.py:167
  102.9 7.1 %multiply_reduce_fusion = (f32[256]{0:T(256)S(1)}, f32[256,40,64]{0,2,1:T(8,128)}) fusion(f32[256,40,64]{0,2,1:T(8,128)} %bitcast.193, f32[256,40,64]{0,2,1:T(8,128)} %get-tuple-element.267, f32[40]{0:T(128)S(1)} %copy-done.5, f32[256,40,64]{0,2,1:T(8,128)} %get-tuple-element.126, f32[40,64,128]{2,1,0:T(8,128)} %shard_map.122, ...), kind=kOutput, calls=%fused_computation.37 | convolution fusion | flops 1013841664 | bytes 11904512 | tf_op jit(solution)/shard_map/tn,hpn->thp/dot_general | solution.py:241
  109.9 3.3 %copy.78 = f32[1,256,2560]{2,1,0:T(8,128)} copy(f32[1,256,2560]{1,2,0:T(8,128)} %bitcast.192) | data formatting | bytes 5242880 | tf_op jit(solution)/shard_map/reshape | solution.py:245
  113.2 4.0 %convolution_multiply_fusion = f32[2560,128]{1,0:T(8,128)S(1)} fusion(f32[256,2560]{1,0:T(8,128)} %copy.83, bf16[256,2816]{1,0:T(8,128)(2,1)S(1)} %multiply_convert_fusion, f32[]{:T(128)S(6)} %sub.90), kind=kOutput, calls=%fused_computation.21 | convolution fusion | flops 1008271360 | bytes 5308420 | tf_op jit(solution)/shard_map/sk,sn->kn/dot_general | solution.py:293
  118.7 3.4 %copy.84 = f32[2,2,2,2,2,2,2,2,10,128]{9,8,7,6,5,4,3,2,1,0:T(8,128)} copy(f32[2,2,2,2,2,2,2,2,10,128]{9,8,0,1,2,3,4,5,6,7:T(8,128)} %bitcast.189) | data formatting | bytes 2621440 | tf_op jit(solution)/shard_map/transpose | solution.py:104
  122.1 68.0 %shard_map.123 = f32[1,10,128]{2,1,0:T(8,128)} custom-call(f32[256,10,128]{2,1,0:T(8,128)} %bitcast.190), custom_call_target="tpu_custom_call" | custom-call | tf_op jit(solution)/shard_map/pallas_call | solution.py:86
  190.1 3.4 %multiply_convert_fusion.1 = bf16[1,256,2560]{2,1,0:T(8,128)(2,1)} fusion(f32[1,256,2560]{2,1,0:T(8,128)S(1)} %copy-done.1, f32[2560]{0:T(1024)S(1)} %copy-done.3, f32[256]{0:T(256)S(1)} %add_rsqrt_fusion, bf16[1,256,2560]{2,1,0:T(8,128)(2,1)} %param.14), kind=kLoop, calls=%fused_computation.36 | loop fusion | flops 5898240 | bytes 5254144 | tf_op jit(solution)/shard_map/convert_element_type | solution.py:247
  (68 shorter events, 19.7 us)
Async XLA Ops:
  1.4 53.0 %collective-permute-start = (bf16[1,3,2816]{2,1,0:T(4,128)(2,1)S(1)}, bf16[1,3,2816]{2,1,0:T(4,128)(2,1)S(1)}, u32[]{:S(2)}, u32[]{:S(2)}) collective-permute-start(bf16[1,3,2816]{2,1,0:T(4,128)(2,1)S(1)} %slice.100), channel_id=1, source_target_pairs={{0,1},{1,2},{2,3},{3,4},{4,5},{5,6},{6,7},{8,9},{9,10},{10,11},{11... | collective-permute-start | bytes 50696 | tf_op jit(solution)/shard_map/ppermute | solution.py:188
  53.1 3.0 %copy-start.4 = (f32[2816]{0:T(1024)S(1)}, f32[2816]{0:T(1024)}, u32[]{:S(2)}) copy-start(f32[2816]{0:T(1024)} %param.17) | copy-start | bytes 33796
  58.0 2.7 %copy-start = (f32[256,2560]{1,0:T(8,128)S(1)}, f32[256,2560]{1,0:T(8,128)}, u32[]{:S(2)}) copy-start(f32[256,2560]{1,0:T(8,128)} %copy.76) | copy-start | bytes 7864324
  96.9 6.0 %copy-start.5 = (f32[40]{0:T(128)S(1)}, f32[40]{0:T(128)}, u32[]{:S(2)}) copy-start(f32[40]{0:T(128)} %param.20) | copy-start | bytes 484
  118.7 71.4 %copy-start.1 = (f32[1,256,2560]{2,1,0:T(8,128)S(1)}, f32[1,256,2560]{2,1,0:T(8,128)}, u32[]{:S(2)}) copy-start(f32[1,256,2560]{2,1,0:T(8,128)} %copy.78) | copy-start | bytes 7864324
  118.7 71.4 %copy-start.3 = (f32[2560]{0:T(1024)S(1)}, f32[2560]{0:T(1024)}, u32[]{:S(2)}) copy-start(f32[2560]{0:T(1024)} %param.21) | copy-start | bytes 30724
  190.1 3.4 %copy-start.2 = (f32[1,10,128]{2,1,0:T(8,128)S(1)}, f32[1,10,128]{2,1,0:T(8,128)}, u32[]{:S(2)}) copy-start(f32[1,10,128]{2,1,0:T(8,128)} %shard_map.123) | copy-start | bytes 15364

commit v4 on v3

--- a/solution.py
+++ b/solution.py
@@ -29,7 +29,7 @@
     return plan
 
 
-def _reduce_scatter_kernel(plan, in_ref, out_ref, acc, *rest):
+def _reduce_scatter_kernel(plan, in_ref, label_ref, out_ref, acc, label_buf, label_send, label_recv, *rest):
     rounds = len(plan)
     recv = rest[:rounds]
     send_sem, recv_sem = rest[rounds], rest[rounds + 1]
@@ -44,10 +44,30 @@
             return (partner_of(axis, bit), coords["seq"])
         return (coords["dp"], partner_of(axis, bit))
 
+    dp_count = lax.axis_size("dp")
+
+    def label_copy(shift):
+        return pltpu.make_async_remote_copy(
+            src_ref=label_ref,
+            dst_ref=label_buf.at[shift],
+            send_sem=label_send.at[shift],
+            recv_sem=label_recv.at[shift],
+            device_id=((coords["dp"] + shift) % dp_count, coords["seq"]),
+            device_id_type=MESH_ID,
+        )
+
     barrier = pltpu.get_barrier_semaphore()
-    for axis, bit in plan:
+    seq_rounds = [(axis, bit) for axis, bit in plan if axis == "seq"]
+    for axis, bit in seq_rounds:
         pl.semaphore_signal(barrier, inc=1, device_id=device_of(axis, bit), device_id_type=MESH_ID)
-    pl.semaphore_wait(barrier, rounds)
+    for shift in range(1, dp_count):
+        pl.semaphore_signal(
+            barrier, inc=1, device_id=((coords["dp"] + shift) % dp_count, coords["seq"]),
+            device_id_type=MESH_ID,
+        )
+    pl.semaphore_wait(barrier, len(seq_rounds) + dp_count - 1)
+    for shift in range(1, dp_count):
+        label_copy(shift).start()
 
     size = in_ref.shape[0]
     base = 0
@@ -57,6 +77,13 @@
         mine = (coords[axis] // bit) % 2
         keep = base + mine * half
         give = base + (1 - mine) * half
+        if index == len(seq_rounds):
+            for shift in range(1, dp_count):
+                label_copy(shift).wait_recv()
+            n_one = label_ref[...] + jnp.sum(label_buf[1:], axis=0)
+            own = label_ref[...]
+            weight = own / n_one - (1.0 - own) / (dp_count - n_one)
+            acc[pl.ds(base, size)] = acc[pl.ds(base, size)] * weight[None]
         source = in_ref if index == 0 else acc
         copy = pltpu.make_async_remote_copy(
             src_ref=source.at[pl.ds(give, half)],
@@ -75,9 +102,11 @@
     out_ref[...] = acc[pl.ds(base, 1)]
     for copy in copies:
         copy.wait_send()
-
-
-def reduce_scatter_blocks(blocks):
+    for shift in range(1, dp_count):
+        label_copy(shift).wait_send()
+
+
+def reduce_scatter_blocks(blocks, label):
     dp_count = lax.axis_size("dp")
     seq_count = lax.axis_size("seq")
     plan = _halving_plan(dp_count, seq_count)
@@ -86,14 +115,19 @@
     return pl.pallas_call(
         functools.partial(_reduce_scatter_kernel, plan),
         out_shape=jax.ShapeDtypeStruct((1, rows, cols), blocks.dtype),
-        in_specs=[pl.BlockSpec(memory_space=pltpu.VMEM)],
+        in_specs=[pl.BlockSpec(memory_space=pltpu.VMEM)] * 2,
         out_specs=pl.BlockSpec(memory_space=pltpu.VMEM),
-        scratch_shapes=[pltpu.VMEM((n_blocks, rows, cols), blocks.dtype)] + recv_shapes + [
+        scratch_shapes=[
+            pltpu.VMEM((n_blocks, rows, cols), blocks.dtype),
+            pltpu.VMEM((dp_count, 1, cols), jnp.float32),
+            pltpu.SemaphoreType.DMA((dp_count,)),
+            pltpu.SemaphoreType.DMA((dp_count,)),
+        ] + recv_shapes + [
             pltpu.SemaphoreType.DMA((len(plan),)),
             pltpu.SemaphoreType.DMA((len(plan),)),
         ],
         compiler_params=pltpu.CompilerParams(collective_id=1, has_side_effects=True),
-    )(blocks)
+    )(blocks, jnp.broadcast_to(label.astype(jnp.float32), (1, cols)))
 
 
 def to_halving_order(partial, dp_count, seq_count, rows):
@@ -263,7 +297,6 @@
     row_count = xbc.shape[1]
     seq_count = lax.axis_size("seq")
     me = lax.axis_index("seq")
-    n_one = jnp.sum(lax.all_gather(labels, "dp", tiled=True).astype(jnp.float32))
     edge_rows = from_behind(xbc[:, row_count - (KW - 1) :, :], "seq", 1)
     padded = jnp.concatenate([edge_rows, xbc], axis=1)[0].astype(jnp.float32)
     conv_sum = conv_bias
@@ -283,27 +316,18 @@
         readout[0],
         offset,
     )
-    scalars = lax.all_gather(jnp.stack([decay_total, carry_weight]), "seq")
-    coef_rows = [jnp.zeros_like(decay_total)]
-    for later in range(seq_count - 1, 0, -1):
-        coef_rows.append(scalars[later, 1] + scalars[later, 0] * coef_rows[-1])
-    coef_all = jnp.stack(coef_rows[::-1])
-    coef = jnp.sum(jnp.where((jnp.arange(seq_count) == me)[:, None], coef_all, 0.0), axis=0)
-    mean_weight = coef[None, :] * to_end + read_weight
-    mean_local = jnp.einsum(
+    h_in = carry_chain(local_state, decay_total)
+    read_local = jnp.einsum(
         "sk,sn->kn",
-        (mean_weight[:, :, None] * x_wide).reshape(row_count, H * P_SIZE),
+        (read_weight[:, :, None] * x_wide).reshape(row_count, H * P_SIZE),
         b_wide,
         precision=highest,
-    )
+    ).reshape(H, P_SIZE, N)
+    mean_state = (carry_weight[:, None, None] * h_in + read_local).reshape(H * P_SIZE, N)
     batch_count = lax.axis_size("dp")
-    class_value = labels[0].astype(jnp.float32)
-    class_weight = class_value / n_one - (1.0 - class_value) / (batch_count - n_one)
-    partial_value = class_weight * mean_local
-    block_rows = partial_value.shape[0] // (batch_count * seq_count)
-    blocks = to_halving_order(partial_value, batch_count, seq_count, block_rows)
-    steering = reduce_scatter_blocks(blocks)[0]
-    h_in = carry_chain(local_state, decay_total)
+    block_rows = mean_state.shape[0] // (batch_count * seq_count)
+    blocks = to_halving_order(mean_state, batch_count, seq_count, block_rows)
+    steering = reduce_scatter_blocks(blocks, labels[0])[0]
     layer_out = finish_block(
         diagonal_part, x_wide, c_wide, cumulative, h_in, gate_input[0], d_skip, norm_gain
     )

time: 195 us -> 170 us (0.87)
  blocking collectives: 32.2 us -> 0 us
  Pallas kernels: 73.2 us -> 79.5 us
    unnamed x1 -> x0, blocking collectives: 21.2 us -> none
    all_gather x1 -> x0, blocking collectives: 11 us -> none  [on_device(): scalars = lax.all_gather(jnp.stack([decay_total, carry_weight]), 'seq')]
    pallas_call x1, Pallas kernels: 68 us -> 72.4 us  [reduce_scatter_blocks(): pl.pallas_call(functools.partial(_reduce_scatter_kernel, plan), out_shape...]
    dynamic_slice x5, local copies, waits for them, and re-layouts: 0.01 us -> 3.69 us  [group_step(): dt_group = lax.dynamic_slice_in_dim(dt_heads, head_start, group_heads, 0)]
    dot_general x0 -> x1, local copies, waits for them, and re-layouts: none -> 3.29 us  [on_device(): jnp.einsum('sk,sn->kn', (read_weight[:, :, None] * x_wide).reshape(row_co...]
    unnamed x18 -> x21, local copies, waits for them, and re-layouts: 4.17 us -> 1.03 us
  transfers between devices with their start and end apart: 1 -> 1, of which waited for: 0 -> 0; matrix products, arithmetic and copies ran while one was open for 9% -> 8% of each run, Pallas kernels for 0% -> 0%
where the time goes in v4:
time: 170 us; the launch traced here: 169 us
  Pallas kernels  79.5 us (47%)
  matrix products  38.1 us (22%)
  local copies, waits for them, and re-layouts  32.5 us (19%)
  other arithmetic  15.7 us (9%)
  starting transfers between devices  1.74 us (1%)
    pallas_call x1, Pallas kernels, reduce_scatter_blocks(): pl.pallas_call(functools.partial(_reduce_scatter_kernel, plan), out_shape...  72.4 us
    dot_general x5, matrix products, group_step(): jnp.einsum('hts,shp->thp', weight, x_group, precision=highest)  21.8 us
    pallas_call x1, Pallas kernels, carry_chain(): pl.pallas_call(functools.partial(_chain_kernel, chunk), out_shape=jax.Sha...  7.14 us
    dot_general x1, matrix products, finish_block(): incoming = jnp.einsum('tn,hpn->thp', c_wide, h_in, precision=highest)  6.65 us
    dot_general x1, matrix products, on_device(): jnp.einsum('sk,sn->kn', (read_weight[:, :, None] * x_wide).reshape(row_co...  4.43 us
    dot_general x1, matrix products, local_terms(): jnp.einsum('sk,sn->kn', (to_end[:, :, None] * x_wide).reshape(row_count,...  4.06 us
    dynamic_slice x5, local copies, waits for them, and re-layouts, group_step(): dt_group = lax.dynamic_slice_in_dim(dt_heads, head_start, group_heads, 0)  3.69 us
  transfers between devices with their start and end apart: 1, of which 0 were waited for; matrix products, arithmetic and copies ran while one was open for 8% of the time, Pallas kernels for 0%

profile of v4, /device:TPU:6, one launch (start us, length us, event | category | flops | bytes accessed | tf_op | source)
XLA Modules:
  0.0 169.2 jit_solution(16107528862839965460)
XLA Ops:
  1.4 1.7 %collective-permute-start = (bf16[1,3,2816]{2,1,0:T(4,128)(2,1)S(1)}, bf16[1,3,2816]{2,1,0:T(4,128)(2,1)S(1)}, u32[]{:S(2)}, u32[]{:S(2)}) collective-permute-start(bf16[1,3,2816]{2,1,0:T(4,128)(2,1)S(1)} %slice.58), channel_id=1, source_target_pairs={{0,1},{1,2},{2,3},{3,4},{4,5},{5,6},{6,7},{8,9},{9,10},{10,11},{11... | collective-permute-start | bytes 50696 | tf_op jit(solution)/shard_map/ppermute | solution.py:222
  10.2 2.1 %copy.38 = f32[256,2560]{1,0:T(8,128)} copy(f32[256,2560]{0,1:T(8,128)S(1)} %bitcast.117) | data formatting | bytes 5242880 | tf_op jit(solution)/shard_map/mul | solution.py:256
  12.6 2.2 %copy.42 = f32[256,2560]{1,0:T(8,128)} copy(f32[256,2560]{0,1:T(8,128)S(1)} %bitcast.118) | data formatting | bytes 5242880 | tf_op jit(solution)/shard_map/mul | solution.py:322
  15.5 2.8 %copy.41 = f32[1,256,2560]{1,2,0:T(8,128)} copy(bf16[1,256,2560]{2,1,0:T(8,128)(2,1)} %param.14) | data formatting | bytes 3932160 | tf_op jit(solution)/shard_map/convert_element_type | solution.py:279
  19.0 1.9 %multiply_convert_fusion = bf16[256,2816]{1,0:T(8,128)(2,1)S(1)} fusion(f32[1,259,2816]{2,1,0:T(8,128)S(1)} %maximum_convert_fusion, f32[2816]{0:T(1024)S(1)} %get-tuple-element.149, f32[2816]{0:T(1024)S(1)} %get-tuple-element.150, f32[2816]{0:T(1024)S(1)} %get-tuple-element.148, f32[2816]{0:T(1024)S(1)} %get-tuple-element.147, f32[2816]{0:T(1024)S(1)} %copy-done.8), kind=kLoop, calls=%fused_computation.33 | loop fusion | flops 9371648 | bytes 13032448 | tf_op jit(solution)/shard_map/convert_element_type | solution.py:305
  20.9 1.8 %slice_convert_fusion = f32[256,2560]{1,0:T(8,128)} fusion(bf16[256,2816]{1,0:T(8,128)(2,1)S(1)} %multiply_convert_fusion), kind=kLoop, calls=%fused_computation.41 | loop fusion | flops 655360 | bytes 3932160 | tf_op jit(solution)/shard_map/convert_element_type | solution.py:227
  23.7 3.0 %multiply_bitcast_fusion = (f32[2560,256]{0,1:T(8,128)}, f32[2560,256]{0,1:T(8,128)}) fusion(f32[256,2560]{1,0:T(8,128)S(1)} %copy-done.1, bf16[256,2816]{1,0:T(8,128)(2,1)S(1)} %multiply_convert_fusion, f32[256,2560]{1,0:T(8,128)S(1)} %copy-done), kind=kLoop, calls=%fused_computation.34 | loop fusion | flops 1966080 | bytes 11796480 | tf_op jit(solution)/shard_map/sk,sn->kn/dot_general | solution.py:320
  26.7 3.2 %copy.39 = f32[2560,256]{1,0:T(8,128)} copy(f32[2560,256]{0,1:T(8,128)} %get-tuple-element.168) | data formatting | bytes 5242880 | tf_op jit(solution)/shard_map/sk,sn->kn/dot_general | solution.py:254
  29.9 4.1 %fusion.32.local_ref = f32[40,64,128]{2,1,0:T(8,128)} fusion(f32[40,64,256]{2,1,0:T(8,128)} %bitcast.119, bf16[256,2816]{1,0:T(8,128)(2,1)S(1)} %multiply_convert_fusion), kind=kOutput, calls=%fused_computation.45 | convolution fusion | flops 1006632960 | bytes 3997696 | tf_op jit(solution)/shard_map/sk,sn->kn/dot_general | solution.py:254
  34.0 3.3 %copy.43 = f32[2560,256]{1,0:T(8,128)} copy(f32[2560,256]{0,1:T(8,128)} %get-tuple-element.167) | data formatting | bytes 5242880 | tf_op jit(solution)/shard_map/sk,sn->kn/dot_general | solution.py:320
  38.0 7.1 %shard_map.122 = f32[40,64,128]{2,1,0:T(8,128)} custom-call(f32[40,64,128]{2,1,0:T(8,128)} %fusion.32.local_ref, f32[40,1,128]{2,1,0:T(1,128)} %broadcast_in_dim.86.decay_ref), custom_call_target="tpu_custom_call" | custom-call | tf_op jit(solution)/shard_map/pallas_call | solution.py:201
  45.1 4.4 %convolution_add_fusion = f32[40,64,128]{2,1,0:T(8,128)} fusion(f32[40,64,256]{2,1,0:T(8,128)} %bitcast.116, f32[40,64,128]{2,1,0:T(8,128)} %shard_map.122, f32[40]{0:T(128)S(1)} %broadcast_multiply_fusion, bf16[256,2816]{1,0:T(8,128)(2,1)S(1)} %multiply_convert_fusion), kind=kOutput, calls=%fused_computation.40 | convolution fusion | flops 1007288320 | bytes 5308928 | tf_op jit(solution)/shard_map/sk,sn->kn/dot_general | solution.py:320
  53.1 72.4 %shard_map.123 = f32[1,10,128]{2,1,0:T(8,128)} custom-call(f32[256,10,128]{2,1,0:T(8,128)} %bitcast.120, f32[1,128]{1,0:T(1,128)} %broadcast_in_dim.89.label_ref), custom_call_target="tpu_custom_call" | custom-call | tf_op jit(solution)/shard_map/pallas_call | solution.py:115
  125.5 3.2 %copy.35 = f32[256,2560]{0,1:T(8,128)} copy(f32[256,2560]{1,0:T(8,128)} %slice_convert_fusion) | data formatting | bytes 5242880 | tf_op jit(solution)/shard_map/convert_element_type | solution.py:227
  128.7 1.9 %broadcast_in_dim.85 = f32[256,40,64]{0,2,1:T(8,128)} broadcast(f32[]{:T(128)} %constant.61.clone.1), dimensions={} | broadcast | bytes 2621444 | tf_op jit(solution)/shard_map/broadcast_in_dim | solution.py:249
  130.6 25.7 %while.14 = (s32[]{:T(128)}, f32[256,40,64]{0,2,1:T(8,128)}, f32[256,40,64]{0,2,1:T(8,128)}, f32[40,256]{1,0:T(8,128)}, f32[40,256]{1,0:T(8,128)}, /*index=5*/f3...) while((s32[]{:T(128)}, f32[256,40,64]{0,2,1:T(8,128)}, ...), condition=%wide.region_3.4_spmd.clone, body=%wide.region_2.3_spmd.clone.sunk | while | flops 404815872 | bytes 1500311 | solution.py:248
  131.5 4.4 %fusion.59 = f32[256,40,64]{0,2,1:T(8,128)} fusion(f32[256,40,64]{0,2,1:T(8,128)} %get-tuple-element.231, s32[]{:T(128)S(6)} %select_n.56, f32[256,256]{1,0:T(8,128)S(1)} %get-tuple-element.245, f32[8,256]{1,0:T(8,128)S(1)} %get-tuple-element.218, f32[8,256]{1,0:T(8,128)S(1)} %get-tuple-element.219, pred[256,256]{1,0:T(8,128)(4,1)S(1)} %iota_compare_fusion.5, ...), kind=kOutput, calls=%fused_computation.8.clone.1 | convolution fusion | flops 404750336 | bytes 1401856 | tf_op jit(solution)/shard_map/while/body/eval_jaxpr/hts,shp->thp/dot_general | solution.py:245
  136.6 4.4 %fusion.59 = f32[256,40,64]{0,2,1:T(8,128)} fusion(f32[256,40,64]{0,2,1:T(8,128)} %get-tuple-element.231, s32[]{:T(128)S(6)} %select_n.56, f32[256,256]{1,0:T(8,128)S(1)} %get-tuple-element.245, f32[8,256]{1,0:T(8,128)S(1)} %get-tuple-element.218, f32[8,256]{1,0:T(8,128)S(1)} %get-tuple-element.219, pred[256,256]{1,0:T(8,128)(4,1)S(1)} %iota_compare_fusion.5, ...), kind=kOutput, calls=%fused_computation.8.clone.1 | convolution fusion | flops 404750336 | bytes 1401856 | tf_op jit(solution)/shard_map/while/body/eval_jaxpr/hts,shp->thp/dot_general | solution.py:245
  141.7 4.4 %fusion.59 = f32[256,40,64]{0,2,1:T(8,128)} fusion(f32[256,40,64]{0,2,1:T(8,128)} %get-tuple-element.231, s32[]{:T(128)S(6)} %select_n.56, f32[256,256]{1,0:T(8,128)S(1)} %get-tuple-element.245, f32[8,256]{1,0:T(8,128)S(1)} %get-tuple-element.218, f32[8,256]{1,0:T(8,128)S(1)} %get-tuple-element.219, pred[256,256]{1,0:T(8,128)(4,1)S(1)} %iota_compare_fusion.5, ...), kind=kOutput, calls=%fused_computation.8.clone.1 | convolution fusion | flops 404750336 | bytes 1401856 | tf_op jit(solution)/shard_map/while/body/eval_jaxpr/hts,shp->thp/dot_general | solution.py:245
  146.9 4.3 %fusion.59 = f32[256,40,64]{0,2,1:T(8,128)} fusion(f32[256,40,64]{0,2,1:T(8,128)} %get-tuple-element.231, s32[]{:T(128)S(6)} %select_n.56, f32[256,256]{1,0:T(8,128)S(1)} %get-tuple-element.245, f32[8,256]{1,0:T(8,128)S(1)} %get-tuple-element.218, f32[8,256]{1,0:T(8,128)S(1)} %get-tuple-element.219, pred[256,256]{1,0:T(8,128)(4,1)S(1)} %iota_compare_fusion.5, ...), kind=kOutput, calls=%fused_computation.8.clone.1 | convolution fusion | flops 404750336 | bytes 1401856 | tf_op jit(solution)/shard_map/while/body/eval_jaxpr/hts,shp->thp/dot_general | solution.py:245
  152.0 4.3 %fusion.59 = f32[256,40,64]{0,2,1:T(8,128)} fusion(f32[256,40,64]{0,2,1:T(8,128)} %get-tuple-element.231, s32[]{:T(128)S(6)} %select_n.56, f32[256,256]{1,0:T(8,128)S(1)} %get-tuple-element.245, f32[8,256]{1,0:T(8,128)S(1)} %get-tuple-element.218, f32[8,256]{1,0:T(8,128)S(1)} %get-tuple-element.219, pred[256,256]{1,0:T(8,128)(4,1)S(1)} %iota_compare_fusion.5, ...), kind=kOutput, calls=%fused_computation.8.clone.1 | convolution fusion | flops 404750336 | bytes 1401856 | tf_op jit(solution)/shard_map/while/body/eval_jaxpr/hts,shp->thp/dot_general | solution.py:245
  156.3 6.7 %multiply_reduce_fusion = (f32[256]{0:T(256)S(1)}, f32[256,40,64]{0,2,1:T(8,128)}) fusion(f32[256,40,64]{0,2,1:T(8,128)} %bitcast.124, f32[256,40,64]{0,2,1:T(8,128)} %get-tuple-element.254, f32[40]{0:T(128)S(1)} %copy-done.9, f32[256,40,64]{0,2,1:T(8,128)} %get-tuple-element.126, f32[40,64,128]{2,1,0:T(8,128)S(1)} %copy-done.2, ...), kind=kOutput, calls=%fused_computation.36 | convolution fusion | flops 1013841664 | bytes 11904512 | tf_op jit(solution)/shard_map/tn,hpn->thp/dot_general | solution.py:275
  163.0 2.2 %copy.40 = f32[1,256,2560]{2,1,0:T(8,128)S(1)} copy(f32[1,256,2560]{1,2,0:T(8,128)} %bitcast.123) | data formatting | bytes 5242880 | tf_op jit(solution)/shard_map/reshape | solution.py:279
  165.2 3.4 %multiply_convert_fusion.1 = bf16[1,256,2560]{2,1,0:T(8,128)(2,1)} fusion(f32[1,256,2560]{2,1,0:T(8,128)S(1)} %copy.40, f32[2560]{0:T(1024)S(1)} %copy-done.7, f32[256]{0:T(256)S(1)} %add_rsqrt_fusion, bf16[1,256,2560]{2,1,0:T(8,128)(2,1)} %param.14), kind=kLoop, calls=%fused_computation.35 | loop fusion | flops 5898240 | bytes 5254144 | tf_op jit(solution)/shard_map/convert_element_type | solution.py:281
  (58 shorter events, 18.3 us)
Async XLA Ops:
  1.4 16.9 %collective-permute-start = (bf16[1,3,2816]{2,1,0:T(4,128)(2,1)S(1)}, bf16[1,3,2816]{2,1,0:T(4,128)(2,1)S(1)}, u32[]{:S(2)}, u32[]{:S(2)}) collective-permute-start(bf16[1,3,2816]{2,1,0:T(4,128)(2,1)S(1)} %slice.58), channel_id=1, source_target_pairs={{0,1},{1,2},{2,3},{3,4},{4,5},{5,6},{6,7},{8,9},{9,10},{10,11},{11... | collective-permute-start | bytes 50696 | tf_op jit(solution)/shard_map/ppermute | solution.py:222
  14.7 3.6 %copy-start.3 = (bf16[1,256,2816]{2,1,0:T(8,128)(2,1)S(1)}, bf16[1,256,2816]{2,1,0:T(8,128)(2,1)}, u32[]{:S(2)}) copy-start(bf16[1,256,2816]{2,1,0:T(8,128)(2,1)} %param.13) | copy-start | bytes 4325380
  18.3 0.7 copy-start.8
  19.0 4.6 %copy-start.1 = (f32[256,2560]{1,0:T(8,128)S(1)}, f32[256,2560]{1,0:T(8,128)}, u32[]{:S(2)}) copy-start(f32[256,2560]{1,0:T(8,128)} %copy.42) | copy-start | bytes 7864324
  20.9 2.8 %copy-start = (f32[256,2560]{1,0:T(8,128)S(1)}, f32[256,2560]{1,0:T(8,128)}, u32[]{:S(2)}) copy-start(f32[256,2560]{1,0:T(8,128)} %copy.38) | copy-start | bytes 7864324
  128.7 1.9 %copy-start.4 = (f32[256,256]{1,0:T(8,128)S(1)}, f32[256,256]{1,0:T(8,128)}, u32[]{:S(2)}) copy-start(f32[256,256]{1,0:T(8,128)} %fusion.36) | copy-start | bytes 786436
  130.6 25.7 %copy-start.2 = (f32[40,64,128]{2,1,0:T(8,128)S(1)}, f32[40,64,128]{2,1,0:T(8,128)}, u32[]{:S(2)}) copy-start(f32[40,64,128]{2,1,0:T(8,128)} %shard_map.122) | copy-start | bytes 3932164
  130.6 25.7 %copy-start.5 = (f32[256,40]{0,1:T(8,128)S(1)}, f32[256,40]{0,1:T(8,128)}, u32[]{:S(2)}) copy-start(f32[256,40]{0,1:T(8,128)} %get-tuple-element.169) | copy-start | bytes 122884
  130.6 25.7 %copy-start.9 = (f32[40]{0:T(128)S(1)}, f32[40]{0:T(128)}, u32[]{:S(2)}) copy-start(f32[40]{0:T(128)} %param.20) | copy-start | bytes 484
  163.0 2.2 %copy-start.7 = (f32[2560]{0:T(1024)S(1)}, f32[2560]{0:T(1024)}, u32[]{:S(2)}) copy-start(f32[2560]{0:T(1024)} %param.21) | copy-start | bytes 30724
  165.2 3.4 %copy-start.6 = (f32[1,10,128]{2,1,0:T(8,128)S(1)}, f32[1,10,128]{2,1,0:T(8,128)}, u32[]{:S(2)}) copy-start(f32[1,10,128]{2,1,0:T(8,128)} %shard_map.123) | copy-start | bytes 15364

commit v5 on v4

--- a/solution.py
+++ b/solution.py
@@ -194,7 +194,7 @@
             link(send_buf, piece).wait_send()
 
 
-def carry_chain(local_state, decay_total, pieces=8):
+def carry_chain(local_state, decay_total, pieces=20):
     heads = local_state.shape[0]
     chunk = heads // pieces
     decay = jnp.broadcast_to(decay_total[:, None, None], (heads, 1, local_state.shape[2]))

time: 170 us -> 168 us (0.988)
  Pallas kernels: 79.5 us -> 77 us
    pallas_call x1, Pallas kernels: 72.4 us -> 69.7 us  [reduce_scatter_blocks(): pl.pallas_call(functools.partial(_reduce_scatter_kernel, plan), out_shape...]
  transfers between devices with their start and end apart: 1 -> 1, of which waited for: 0 -> 0; matrix products, arithmetic and copies ran while one was open for 8% -> 9% of each run, Pallas kernels for 0% -> 0%
where the time goes in v5:
time: 168 us; the launch traced here: 167 us
  Pallas kernels  77 us (46%)
  matrix products  38.1 us (23%)
  local copies, waits for them, and re-layouts  32.5 us (19%)
  other arithmetic  15.7 us (9%)
  starting transfers between devices  1.74 us (1%)
    pallas_call x1, Pallas kernels, reduce_scatter_blocks(): pl.pallas_call(functools.partial(_reduce_scatter_kernel, plan), out_shape...  69.7 us
    dot_general x5, matrix products, group_step(): jnp.einsum('hts,shp->thp', weight, x_group, precision=highest)  21.8 us
    pallas_call x1, Pallas kernels, carry_chain(): pl.pallas_call(functools.partial(_chain_kernel, chunk), out_shape=jax.Sha...  7.36 us
    dot_general x1, matrix products, finish_block(): incoming = jnp.einsum('tn,hpn->thp', c_wide, h_in, precision=highest)  6.64 us
    dot_general x1, matrix products, on_device(): jnp.einsum('sk,sn->kn', (read_weight[:, :, None] * x_wide).reshape(row_co...  4.43 us
    dot_general x1, matrix products, local_terms(): jnp.einsum('sk,sn->kn', (to_end[:, :, None] * x_wide).reshape(row_count,...  4.06 us
    dynamic_slice x5, local copies, waits for them, and re-layouts, group_step(): dt_group = lax.dynamic_slice_in_dim(dt_heads, head_start, group_heads, 0)  3.69 us
    convert_element_type x1, other arithmetic, finish_block(): return (gated_out * inv_rms * norm_gain).astype(jnp.bfloat16)  3.38 us
  transfers between devices with their start and end apart: 1, of which 0 were waited for; matrix products, arithmetic and copies ran while one was open for 9% of the time, Pallas kernels for 0%

profile of v5, /device:TPU:6, one launch (start us, length us, event | category | flops | bytes accessed | tf_op | source)
XLA Modules:
  0.0 166.6 jit_solution(15149935906699024803)
XLA Ops:
  1.4 1.7 %collective-permute-start = (bf16[1,3,2816]{2,1,0:T(4,128)(2,1)S(1)}, bf16[1,3,2816]{2,1,0:T(4,128)(2,1)S(1)}, u32[]{:S(2)}, u32[]{:S(2)}) collective-permute-start(bf16[1,3,2816]{2,1,0:T(4,128)(2,1)S(1)} %slice.58), channel_id=1, source_target_pairs={{0,1},{1,2},{2,3},{3,4},{4,5},{5,6},{6,7},{8,9},{9,10},{10,11},{11... | collective-permute-start | bytes 50696 | tf_op jit(solution)/shard_map/ppermute | solution.py:222
  10.2 2.1 %copy.38 = f32[256,2560]{1,0:T(8,128)} copy(f32[256,2560]{0,1:T(8,128)S(1)} %bitcast.117) | data formatting | bytes 5242880 | tf_op jit(solution)/shard_map/mul | solution.py:256
  12.6 2.2 %copy.42 = f32[256,2560]{1,0:T(8,128)} copy(f32[256,2560]{0,1:T(8,128)S(1)} %bitcast.118) | data formatting | bytes 5242880 | tf_op jit(solution)/shard_map/mul | solution.py:322
  15.5 2.8 %copy.41 = f32[1,256,2560]{1,2,0:T(8,128)} copy(bf16[1,256,2560]{2,1,0:T(8,128)(2,1)} %param.14) | data formatting | bytes 3932160 | tf_op jit(solution)/shard_map/convert_element_type | solution.py:279
  19.0 1.9 %multiply_convert_fusion = bf16[256,2816]{1,0:T(8,128)(2,1)S(1)} fusion(f32[1,259,2816]{2,1,0:T(8,128)S(1)} %maximum_convert_fusion, f32[2816]{0:T(1024)S(1)} %get-tuple-element.149, f32[2816]{0:T(1024)S(1)} %get-tuple-element.150, f32[2816]{0:T(1024)S(1)} %get-tuple-element.148, f32[2816]{0:T(1024)S(1)} %get-tuple-element.147, f32[2816]{0:T(1024)S(1)} %copy-done.8), kind=kLoop, calls=%fused_computation.33 | loop fusion | flops 9371648 | bytes 13032448 | tf_op jit(solution)/shard_map/convert_element_type | solution.py:305
  20.9 1.8 %slice_convert_fusion = f32[256,2560]{1,0:T(8,128)} fusion(bf16[256,2816]{1,0:T(8,128)(2,1)S(1)} %multiply_convert_fusion), kind=kLoop, calls=%fused_computation.41 | loop fusion | flops 655360 | bytes 3932160 | tf_op jit(solution)/shard_map/convert_element_type | solution.py:227
  23.7 3.0 %multiply_bitcast_fusion = (f32[2560,256]{0,1:T(8,128)}, f32[2560,256]{0,1:T(8,128)}) fusion(f32[256,2560]{1,0:T(8,128)S(1)} %copy-done.1, bf16[256,2816]{1,0:T(8,128)(2,1)S(1)} %multiply_convert_fusion, f32[256,2560]{1,0:T(8,128)S(1)} %copy-done), kind=kLoop, calls=%fused_computation.34 | loop fusion | flops 1966080 | bytes 11796480 | tf_op jit(solution)/shard_map/sk,sn->kn/dot_general | solution.py:320
  26.7 3.2 %copy.39 = f32[2560,256]{1,0:T(8,128)} copy(f32[2560,256]{0,1:T(8,128)} %get-tuple-element.168) | data formatting | bytes 5242880 | tf_op jit(solution)/shard_map/sk,sn->kn/dot_general | solution.py:254
  29.9 4.1 %fusion.32.local_ref = f32[40,64,128]{2,1,0:T(8,128)} fusion(f32[40,64,256]{2,1,0:T(8,128)} %bitcast.119, bf16[256,2816]{1,0:T(8,128)(2,1)S(1)} %multiply_convert_fusion), kind=kOutput, calls=%fused_computation.45 | convolution fusion | flops 1006632960 | bytes 3997696 | tf_op jit(solution)/shard_map/sk,sn->kn/dot_general | solution.py:254
  34.0 3.3 %copy.43 = f32[2560,256]{1,0:T(8,128)} copy(f32[2560,256]{0,1:T(8,128)} %get-tuple-element.167) | data formatting | bytes 5242880 | tf_op jit(solution)/shard_map/sk,sn->kn/dot_general | solution.py:320
  38.0 7.4 %shard_map.122 = f32[40,64,128]{2,1,0:T(8,128)} custom-call(f32[40,64,128]{2,1,0:T(8,128)} %fusion.32.local_ref, f32[40,1,128]{2,1,0:T(1,128)} %broadcast_in_dim.86.decay_ref), custom_call_target="tpu_custom_call" | custom-call | tf_op jit(solution)/shard_map/pallas_call | solution.py:201
  45.3 4.4 %convolution_add_fusion = f32[40,64,128]{2,1,0:T(8,128)} fusion(f32[40,64,256]{2,1,0:T(8,128)} %bitcast.116, f32[40,64,128]{2,1,0:T(8,128)} %shard_map.122, f32[40]{0:T(128)S(1)} %broadcast_multiply_fusion, bf16[256,2816]{1,0:T(8,128)(2,1)S(1)} %multiply_convert_fusion), kind=kOutput, calls=%fused_computation.40 | convolution fusion | flops 1007288320 | bytes 5308928 | tf_op jit(solution)/shard_map/sk,sn->kn/dot_general | solution.py:320
  53.3 69.7 %shard_map.123 = f32[1,10,128]{2,1,0:T(8,128)} custom-call(f32[256,10,128]{2,1,0:T(8,128)} %bitcast.120, f32[1,128]{1,0:T(1,128)} %broadcast_in_dim.89.label_ref), custom_call_target="tpu_custom_call" | custom-call | tf_op jit(solution)/shard_map/pallas_call | solution.py:115
  123.0 3.2 %copy.35 = f32[256,2560]{0,1:T(8,128)} copy(f32[256,2560]{1,0:T(8,128)} %slice_convert_fusion) | data formatting | bytes 5242880 | tf_op jit(solution)/shard_map/convert_element_type | solution.py:227
  126.2 1.9 %broadcast_in_dim.85 = f32[256,40,64]{0,2,1:T(8,128)} broadcast(f32[]{:T(128)} %constant.61.clone.1), dimensions={} | broadcast | bytes 2621444 | tf_op jit(solution)/shard_map/broadcast_in_dim | solution.py:249
  128.1 25.7 %while.14 = (s32[]{:T(128)}, f32[256,40,64]{0,2,1:T(8,128)}, f32[256,40,64]{0,2,1:T(8,128)}, f32[40,256]{1,0:T(8,128)}, f32[40,256]{1,0:T(8,128)}, /*index=5*/f3...) while((s32[]{:T(128)}, f32[256,40,64]{0,2,1:T(8,128)}, ...), condition=%wide.region_3.4_spmd.clone, body=%wide.region_2.3_spmd.clone.sunk | while | flops 404815872 | bytes 1500311 | solution.py:248
  129.0 4.4 %fusion.59 = f32[256,40,64]{0,2,1:T(8,128)} fusion(f32[256,40,64]{0,2,1:T(8,128)} %get-tuple-element.231, s32[]{:T(128)S(6)} %select_n.56, f32[256,256]{1,0:T(8,128)S(1)} %get-tuple-element.245, f32[8,256]{1,0:T(8,128)S(1)} %get-tuple-element.218, f32[8,256]{1,0:T(8,128)S(1)} %get-tuple-element.219, pred[256,256]{1,0:T(8,128)(4,1)S(1)} %iota_compare_fusion.5, ...), kind=kOutput, calls=%fused_computation.8.clone.1 | convolution fusion | flops 404750336 | bytes 1401856 | tf_op jit(solution)/shard_map/while/body/eval_jaxpr/hts,shp->thp/dot_general | solution.py:245
  134.1 4.4 %fusion.59 = f32[256,40,64]{0,2,1:T(8,128)} fusion(f32[256,40,64]{0,2,1:T(8,128)} %get-tuple-element.231, s32[]{:T(128)S(6)} %select_n.56, f32[256,256]{1,0:T(8,128)S(1)} %get-tuple-element.245, f32[8,256]{1,0:T(8,128)S(1)} %get-tuple-element.218, f32[8,256]{1,0:T(8,128)S(1)} %get-tuple-element.219, pred[256,256]{1,0:T(8,128)(4,1)S(1)} %iota_compare_fusion.5, ...), kind=kOutput, calls=%fused_computation.8.clone.1 | convolution fusion | flops 404750336 | bytes 1401856 | tf_op jit(solution)/shard_map/while/body/eval_jaxpr/hts,shp->thp/dot_general | solution.py:245
  139.2 4.4 %fusion.59 = f32[256,40,64]{0,2,1:T(8,128)} fusion(f32[256,40,64]{0,2,1:T(8,128)} %get-tuple-element.231, s32[]{:T(128)S(6)} %select_n.56, f32[256,256]{1,0:T(8,128)S(1)} %get-tuple-element.245, f32[8,256]{1,0:T(8,128)S(1)} %get-tuple-element.218, f32[8,256]{1,0:T(8,128)S(1)} %get-tuple-element.219, pred[256,256]{1,0:T(8,128)(4,1)S(1)} %iota_compare_fusion.5, ...), kind=kOutput, calls=%fused_computation.8.clone.1 | convolution fusion | flops 404750336 | bytes 1401856 | tf_op jit(solution)/shard_map/while/body/eval_jaxpr/hts,shp->thp/dot_general | solution.py:245
  144.4 4.3 %fusion.59 = f32[256,40,64]{0,2,1:T(8,128)} fusion(f32[256,40,64]{0,2,1:T(8,128)} %get-tuple-element.231, s32[]{:T(128)S(6)} %select_n.56, f32[256,256]{1,0:T(8,128)S(1)} %get-tuple-element.245, f32[8,256]{1,0:T(8,128)S(1)} %get-tuple-element.218, f32[8,256]{1,0:T(8,128)S(1)} %get-tuple-element.219, pred[256,256]{1,0:T(8,128)(4,1)S(1)} %iota_compare_fusion.5, ...), kind=kOutput, calls=%fused_computation.8.clone.1 | convolution fusion | flops 404750336 | bytes 1401856 | tf_op jit(solution)/shard_map/while/body/eval_jaxpr/hts,shp->thp/dot_general | solution.py:245
  149.5 4.3 %fusion.59 = f32[256,40,64]{0,2,1:T(8,128)} fusion(f32[256,40,64]{0,2,1:T(8,128)} %get-tuple-element.231, s32[]{:T(128)S(6)} %select_n.56, f32[256,256]{1,0:T(8,128)S(1)} %get-tuple-element.245, f32[8,256]{1,0:T(8,128)S(1)} %get-tuple-element.218, f32[8,256]{1,0:T(8,128)S(1)} %get-tuple-element.219, pred[256,256]{1,0:T(8,128)(4,1)S(1)} %iota_compare_fusion.5, ...), kind=kOutput, calls=%fused_computation.8.clone.1 | convolution fusion | flops 404750336 | bytes 1401856 | tf_op jit(solution)/shard_map/while/body/eval_jaxpr/hts,shp->thp/dot_general | solution.py:245
  153.8 6.6 %multiply_reduce_fusion = (f32[256]{0:T(256)S(1)}, f32[256,40,64]{0,2,1:T(8,128)}) fusion(f32[256,40,64]{0,2,1:T(8,128)} %bitcast.124, f32[256,40,64]{0,2,1:T(8,128)} %get-tuple-element.254, f32[40]{0:T(128)S(1)} %copy-done.9, f32[256,40,64]{0,2,1:T(8,128)} %get-tuple-element.126, f32[40,64,128]{2,1,0:T(8,128)S(1)} %copy-done.2, ...), kind=kOutput, calls=%fused_computation.36 | convolution fusion | flops 1013841664 | bytes 11904512 | tf_op jit(solution)/shard_map/tn,hpn->thp/dot_general | solution.py:275
  160.5 2.2 %copy.40 = f32[1,256,2560]{2,1,0:T(8,128)S(1)} copy(f32[1,256,2560]{1,2,0:T(8,128)} %bitcast.123) | data formatting | bytes 5242880 | tf_op jit(solution)/shard_map/reshape | solution.py:279
  162.7 3.4 %multiply_convert_fusion.1 = bf16[1,256,2560]{2,1,0:T(8,128)(2,1)} fusion(f32[1,256,2560]{2,1,0:T(8,128)S(1)} %copy.40, f32[2560]{0:T(1024)S(1)} %copy-done.7, f32[256]{0:T(256)S(1)} %add_rsqrt_fusion, bf16[1,256,2560]{2,1,0:T(8,128)(2,1)} %param.14), kind=kLoop, calls=%fused_computation.35 | loop fusion | flops 5898240 | bytes 5254144 | tf_op jit(solution)/shard_map/convert_element_type | solution.py:281
  (58 shorter events, 18.3 us)
Async XLA Ops:
  1.4 16.9 %collective-permute-start = (bf16[1,3,2816]{2,1,0:T(4,128)(2,1)S(1)}, bf16[1,3,2816]{2,1,0:T(4,128)(2,1)S(1)}, u32[]{:S(2)}, u32[]{:S(2)}) collective-permute-start(bf16[1,3,2816]{2,1,0:T(4,128)(2,1)S(1)} %slice.58), channel_id=1, source_target_pairs={{0,1},{1,2},{2,3},{3,4},{4,5},{5,6},{6,7},{8,9},{9,10},{10,11},{11... | collective-permute-start | bytes 50696 | tf_op jit(solution)/shard_map/ppermute | solution.py:222
  14.7 3.6 %copy-start.3 = (bf16[1,256,2816]{2,1,0:T(8,128)(2,1)S(1)}, bf16[1,256,2816]{2,1,0:T(8,128)(2,1)}, u32[]{:S(2)}) copy-start(bf16[1,256,2816]{2,1,0:T(8,128)(2,1)} %param.13) | copy-start | bytes 4325380
  18.3 0.7 copy-start.8
  19.0 4.6 %copy-start.1 = (f32[256,2560]{1,0:T(8,128)S(1)}, f32[256,2560]{1,0:T(8,128)}, u32[]{:S(2)}) copy-start(f32[256,2560]{1,0:T(8,128)} %copy.42) | copy-start | bytes 7864324
  20.9 2.8 %copy-start = (f32[256,2560]{1,0:T(8,128)S(1)}, f32[256,2560]{1,0:T(8,128)}, u32[]{:S(2)}) copy-start(f32[256,2560]{1,0:T(8,128)} %copy.38) | copy-start | bytes 7864324
  126.2 1.9 %copy-start.4 = (f32[256,256]{1,0:T(8,128)S(1)}, f32[256,256]{1,0:T(8,128)}, u32[]{:S(2)}) copy-start(f32[256,256]{1,0:T(8,128)} %fusion.36) | copy-start | bytes 786436
  128.1 25.7 %copy-start.2 = (f32[40,64,128]{2,1,0:T(8,128)S(1)}, f32[40,64,128]{2,1,0:T(8,128)}, u32[]{:S(2)}) copy-start(f32[40,64,128]{2,1,0:T(8,128)} %shard_map.122) | copy-start | bytes 3932164
  128.1 25.7 %copy-start.5 = (f32[256,40]{0,1:T(8,128)S(1)}, f32[256,40]{0,1:T(8,128)}, u32[]{:S(2)}) copy-start(f32[256,40]{0,1:T(8,128)} %get-tuple-element.169) | copy-start | bytes 122884
  128.1 25.7 %copy-start.9 = (f32[40]{0:T(128)S(1)}, f32[40]{0:T(128)}, u32[]{:S(2)}) copy-start(f32[40]{0:T(128)} %param.20) | copy-start | bytes 484
  160.5 2.2 %copy-start.7 = (f32[2560]{0:T(1024)S(1)}, f32[2560]{0:T(1024)}, u32[]{:S(2)}) copy-start(f32[2560]{0:T(1024)} %param.21) | copy-start | bytes 30724
  162.6 3.4 %copy-start.6 = (f32[1,10,128]{2,1,0:T(8,128)S(1)}, f32[1,10,128]{2,1,0:T(8,128)}, u32[]{:S(2)}) copy-start(f32[1,10,128]{2,1,0:T(8,128)} %shard_map.123) | copy-start | bytes 15364

commit v6 on v5

--- a/solution.py
+++ b/solution.py
@@ -146,7 +146,7 @@
     has_right = (2 * count - 2 - me) // count
     left = me - has_left
     right = me + has_right
-    pieces = local_ref.shape[0] // chunk
+    pieces = local_ref.shape[1] // chunk
 
     barrier = pltpu.get_barrier_semaphore()
 
@@ -161,10 +161,10 @@
     pl.semaphore_wait(barrier, has_left + has_right)
 
     def link(source, piece):
-        rows = pl.ds(piece * chunk, chunk)
+        cols = pl.ds(piece * chunk, chunk)
         return pltpu.make_async_remote_copy(
-            src_ref=source.at[rows],
-            dst_ref=hin_ref.at[rows],
+            src_ref=source.at[:, cols],
+            dst_ref=hin_ref.at[:, cols],
             send_sem=send_sem.at[piece],
             recv_sem=recv_sem.at[piece],
             device_id=(row_id, right),
@@ -180,12 +180,12 @@
     @pl.when(has_left == 1)
     def _():
         for piece in range(pieces):
-            rows = pl.ds(piece * chunk, chunk)
+            cols = pl.ds(piece * chunk, chunk)
             link(send_buf, piece).wait_recv()
 
             @pl.when(has_right == 1)
             def _():
-                send_buf[rows] = decay_ref[rows] * hin_ref[rows] + local_ref[rows]
+                send_buf[:, cols] = decay_ref[:, cols] * hin_ref[:, cols] + local_ref[:, cols]
                 link(send_buf, piece).start()
 
     @pl.when(has_right == 1)
@@ -194,10 +194,8 @@
             link(send_buf, piece).wait_send()
 
 
-def carry_chain(local_state, decay_total, pieces=20):
-    heads = local_state.shape[0]
-    chunk = heads // pieces
-    decay = jnp.broadcast_to(decay_total[:, None, None], (heads, 1, local_state.shape[2]))
+def carry_chain(local_state, decay, pieces=20):
+    chunk = local_state.shape[1] // pieces
     return pl.pallas_call(
         functools.partial(_chain_kernel, chunk),
         out_shape=jax.ShapeDtypeStruct(local_state.shape, local_state.dtype),
@@ -222,6 +220,16 @@
     return lax.ppermute(block, axis, route)
 
 
+def state_product(weight, x_wide, b_wide):
+    row_count = x_wide.shape[0]
+    return lax.dot_general(
+        b_wide,
+        (weight[:, :, None] * x_wide).reshape(row_count, H * P_SIZE),
+        (((0,), (0,)), ((), ())),
+        precision=highest,
+    )
+
+
 def local_terms(x_vals, b_vals, c_vals, dt_vals, cumulative, points, offset):
     row_count = x_vals.shape[0]
     x_wide = x_vals.astype(jnp.float32).reshape(row_count, H, P_SIZE)
@@ -251,12 +259,7 @@
     final_log = cumulative[row_count - 1]
     to_end = jnp.exp(final_log[None, :] - cumulative) * dt_vals
     decay_total = jnp.exp(final_log)
-    local_state = jnp.einsum(
-        "sk,sn->kn",
-        (to_end[:, :, None] * x_wide).reshape(row_count, H * P_SIZE),
-        b_wide,
-        precision=highest,
-    ).reshape(H, P_SIZE, N)
+    local_state = state_product(to_end, x_wide, b_wide)
     local_index = points - offset
     owned_flag = ((local_index >= 0) & (local_index < row_count)).astype(jnp.float32)
     one_hot = (positions[None, :] == local_index[:, None]).astype(jnp.float32)
@@ -272,7 +275,7 @@
 
 def finish_block(diagonal_part, x_wide, c_wide, cumulative, h_in, gate_rows, d_skip, norm_gain):
     row_count = x_wide.shape[0]
-    incoming = jnp.einsum("tn,hpn->thp", c_wide, h_in, precision=highest)
+    incoming = jnp.dot(c_wide, h_in, precision=highest).reshape(row_count, H, P_SIZE)
     ssm_out = (
         diagonal_part + jnp.exp(cumulative)[:, :, None] * incoming + d_skip[None, :, None] * x_wide
     )
@@ -316,14 +319,9 @@
         readout[0],
         offset,
     )
-    h_in = carry_chain(local_state, decay_total)
-    read_local = jnp.einsum(
-        "sk,sn->kn",
-        (read_weight[:, :, None] * x_wide).reshape(row_count, H * P_SIZE),
-        b_wide,
-        precision=highest,
-    ).reshape(H, P_SIZE, N)
-    mean_state = (carry_weight[:, None, None] * h_in + read_local).reshape(H * P_SIZE, N)
+    h_in = carry_chain(local_state, jnp.repeat(decay_total, P_SIZE)[None])
+    read_local = state_product(read_weight, x_wide, b_wide)
+    mean_state = (jnp.repeat(carry_weight, P_SIZE)[None] * h_in + read_local).T
     batch_count = lax.axis_size("dp")
     block_rows = mean_state.shape[0] // (batch_count * seq_count)
     blocks = to_halving_order(mean_state, batch_count, seq_count, block_rows)

time: 168 us -> 157 us (0.935)
  local copies, waits for them, and re-layouts: 32.5 us -> 22.7 us
  matrix products: 38.1 us -> 32.4 us
  other arithmetic: 15.7 us -> 20.6 us
    dot_general x2 -> x0, local copies, waits for them, and re-layouts: 6.53 us -> none  [the longest x1 3.29 us: on_device(): jnp.einsum('sk,sn->kn', (read_weight[:, :, None] * x_wide).reshape(row_co...]
    convert_element_type x2 -> x0, local copies, waits for them, and re-layouts: 6.07 us -> none  [the longest x1 3.23 us: local_terms(): x_wide = x_vals.astype(jnp.float32).reshape(row_count, H, P_SIZE)]
    dot_general x3, matrix products: 15.1 us -> 9.51 us  [the longest x2 5.28 us: state_product(): lax.dot_general(b_wide, (weight[:, :, None] * x_wide).reshape(row_count,...]
    reduce_sum x0 -> x1, other arithmetic: none -> 4.66 us  [finish_block(): jnp.mean(gated_out * gated_out, axis=-1, keepdims=True) + 1e-05]
    unnamed x21 -> x30, local copies, waits for them, and re-layouts: 1.03 us -> 5.51 us
    mul x4 -> x1, local copies, waits for them, and re-layouts: 4.67 us -> 0.67 us  [on_device(): mean_state = (jnp.repeat(carry_weight, P_SIZE)[None] * h_in + read_local).T]
    dot_general x1 -> x0, other arithmetic: 3.01 us -> none  [on_device(): jnp.einsum('sk,sn->kn', (read_weight[:, :, None] * x_wide).reshape(row_co...]
    convert_element_type x1, other arithmetic: 1.86 us -> 4.8 us  [on_device(): activated = jax.nn.silu(conv_sum).astype(jnp.bfloat16)]
  transfers between devices with their start and end apart: 1 -> 1, of which waited for: 0 -> 0; matrix products, arithmetic and copies ran while one was open for 9% -> 8% of each run, Pallas kernels for 0% -> 0%
where the time goes in v6:
time: 157 us; the launch traced here: 156 us
  Pallas kernels  76.5 us (49%)
  matrix products  32.4 us (21%)
  local copies, waits for them, and re-layouts  22.7 us (14%)
  other arithmetic  20.6 us (13%)
  starting transfers between devices  2.33 us (1%)
    pallas_call x1, Pallas kernels, reduce_scatter_blocks(): pl.pallas_call(functools.partial(_reduce_scatter_kernel, plan), out_shape...  69.7 us
    dot_general x5, matrix products, group_step(): jnp.einsum('hts,shp->thp', weight, x_group, precision=highest)  21.7 us
    pallas_call x1, Pallas kernels, carry_chain(): pl.pallas_call(functools.partial(_chain_kernel, chunk), out_shape=jax.Sha...  6.87 us
    unnamed x30, local copies, waits for them, and re-layouts  5.51 us
    dot_general x2, matrix products, state_product(): lax.dot_general(b_wide, (weight[:, :, None] * x_wide).reshape(row_count,...  5.28 us
    convert_element_type x1, other arithmetic, on_device(): activated = jax.nn.silu(conv_sum).astype(jnp.bfloat16)  4.8 us
    reduce_sum x1, other arithmetic, finish_block(): jnp.mean(gated_out * gated_out, axis=-1, keepdims=True) + 1e-05  4.66 us
    dot_general x1, matrix products, finish_block(): jnp.dot(c_wide, h_in, precision=highest).reshape(row_count, H, P_SIZE)  4.23 us
  transfers between devices with their start and end apart: 1, of which 0 were waited for; matrix products, arithmetic and copies ran while one was open for 8% of the time, Pallas kernels for 0%

profile of v6, /device:TPU:6, one launch (start us, length us, event | category | flops | bytes accessed | tf_op | source)
XLA Modules:
  0.0 156.2 jit_solution(18305721993181598091)
XLA Ops:
  1.4 2.3 %collective-permute-start = (bf16[1,3,2816]{2,1,0:T(4,128)(2,1)S(1)}, bf16[1,3,2816]{2,1,0:T(4,128)(2,1)}, u32[]{:S(2)}, u32[]{:S(2)}) collective-permute-start(bf16[1,3,2816]{2,1,0:T(4,128)(2,1)S(1)} %slice.58), channel_id=1, source_target_pairs={{0,1},{1,2},{2,3},{3,4},{4,5},{5,6},{6,7},{8,9},{9,10},{10,11},{11... | collective-permute-start | bytes 50696 | tf_op jit(solution)/shard_map/ppermute | solution.py:220
  8.1 1.5 bitcast_exponential_fusion
  9.6 1.7 %slice_reduce_fusion.5 = (f32[2816]{0:T(1024)}, f32[2816]{0:T(1024)}, f32[2816]{0:T(1024)}, f32[2816]{0:T(1024)}) fusion(f32[4,2816]{1,0:T(4,128)} %param.16), kind=kLoop, calls=%fused_computation.74 | loop fusion | bytes 90112 | tf_op jit(solution)/shard_map/slice | solution.py:307
  11.2 1.7 %copy.44 = bf16[1,256,2816]{1,2,0:T(8,128)(2,1)S(1)} copy(bf16[1,256,2816]{2,1,0:T(8,128)(2,1)} %param.13) | data formatting | bytes 2883584 | tf_op args[0]
  15.1 1.6 %copy.48 = bf16[1,256,2560]{1,2,0:T(8,128)(2,1)S(1)} copy(bf16[1,256,2560]{2,1,0:T(8,128)(2,1)} %param.14) | data formatting | bytes 2621440 | tf_op args[1]
  18.9 4.8 %multiply_convert_fusion = bf16[256,2816]{0,1:T(8,128)(2,1)S(1)} fusion(f32[1,259,2816]{1,2,0:T(8,128)S(1)} %maximum_convert_fusion, f32[2816]{0:T(1024)S(1)} %copy-done.7, f32[2816]{0:T(1024)S(1)} %copy-done.8, f32[2816]{0:T(1024)S(1)} %copy-done.6, f32[2816]{0:T(1024)S(1)} %copy-done.5, f32[2816]{0:T(1024)S(1)} %copy-done.11), kind=kLoop, calls=%fused_computation.35 | loop fusion | flops 9371648 | bytes 13032448 | tf_op jit(solution)/shard_map/convert_element_type | solution.py:308
  23.7 1.7 %slice_convert_fusion = f32[256,2560]{0,1:T(8,128)} fusion(bf16[256,2816]{0,1:T(8,128)(2,1)S(1)} %multiply_convert_fusion), kind=kLoop, calls=%fused_computation.45 | loop fusion | flops 655360 | bytes 3932160 | tf_op jit(solution)/shard_map/convert_element_type | solution.py:235
  26.3 1.8 %bitcast_multiply_fusion = (f32[256,2560]{0,1:T(8,128)}, f32[256,2560]{0,1:T(8,128)S(1)}) fusion(f32[256,40]{0,1:T(8,128)S(1)} %get-tuple-element.175, bf16[256,2816]{0,1:T(8,128)(2,1)S(1)} %multiply_convert_fusion, f32[256,40]{0,1:T(8,128)S(1)} %get-tuple-element.172), kind=kLoop, calls=%fused_computation.36 | loop fusion | flops 1966080 | bytes 6635520 | tf_op jit(solution)/shard_map/mul | solution.py:227
  28.1 2.6 %fusion.40.local_ref = f32[128,2560]{1,0:T(8,128)} fusion(f32[256,2560]{0,1:T(8,128)S(1)} %get-tuple-element.170, bf16[256,2816]{0,1:T(8,128)(2,1)S(1)} %multiply_convert_fusion), kind=kOutput, calls=%fused_computation.53 | convolution fusion | flops 1006632960 | bytes 3997696 | tf_op jit(solution)/shard_map/dot_general | solution.py:225
  30.8 6.9 %shard_map.122 = f32[128,2560]{1,0:T(8,128)} custom-call(f32[128,2560]{1,0:T(8,128)} %fusion.40.local_ref, f32[1,2560]{1,0:T(1,128)} %broadcast_in_dim_reshape.4.decay_ref), custom_call_target="tpu_custom_call" | custom-call | tf_op jit(solution)/shard_map/pallas_call | solution.py:199
  37.7 4.2 %fusion.35 = f32[256,2560]{0,1:T(8,128)} fusion(f32[128,2560]{1,0:T(8,128)} %shard_map.122, bf16[256,2816]{0,1:T(8,128)(2,1)S(1)} %multiply_convert_fusion), kind=kOutput, calls=%fused_computation.48 | convolution fusion | flops 1006632960 | bytes 3997696 | tf_op jit(solution)/shard_map/dot_general | solution.py:278
  41.9 2.7 %fusion.23 = f32[2560,128]{0,1:T(8,128)} fusion(f32[256,2560]{0,1:T(8,128)S(1)} %copy-done.1, f32[128,2560]{1,0:T(8,128)S(1)} %copy-done, f32[2560]{0:T(1024)S(1)} %copy-done.4, bf16[256,2816]{0,1:T(8,128)(2,1)S(1)} %multiply_convert_fusion), kind=kOutput, calls=%fused_computation.22 | convolution fusion | flops 1007288320 | bytes 5320704 | tf_op jit(solution)/shard_map/dot_general | solution.py:225
  44.6 2.8 %copy.49 = f32[2560,128]{1,0:T(8,128)} copy(f32[2560,128]{0,1:T(8,128)} %fusion.23) | data formatting | bytes 2621440 | tf_op jit(solution)/shard_map/transpose | solution.py:324
  48.7 1.7 %copy.50 = f32[2,2,2,2,2,2,2,2,10,128]{9,8,7,6,5,4,3,2,1,0:T(8,128)} copy(f32[2,2,2,2,2,2,2,2,10,128]{9,8,0,1,2,3,4,5,6,7:T(8,128)S(1)} %bitcast.117) | data formatting | bytes 2621440 | tf_op jit(solution)/shard_map/transpose | solution.py:138
  50.9 69.7 %shard_map.123 = f32[1,10,128]{2,1,0:T(8,128)} custom-call(f32[256,10,128]{2,1,0:T(8,128)} %bitcast.116, f32[1,128]{1,0:T(1,128)} %broadcast_in_dim.89.label_ref), custom_call_target="tpu_custom_call" | custom-call | tf_op jit(solution)/shard_map/pallas_call | solution.py:115
  120.6 1.8 %broadcast_in_dim.84 = f32[256,40,64]{0,2,1:T(8,128)} broadcast(f32[]{:T(128)} %constant.61.clone.1), dimensions={} | broadcast | bytes 2621444 | tf_op jit(solution)/shard_map/broadcast_in_dim | solution.py:257
  122.5 25.5 %while.14 = (s32[]{:T(128)}, f32[256,40,64]{0,2,1:T(8,128)}, f32[256,40,64]{0,2,1:T(8,128)}, f32[40,256]{1,0:T(8,128)}, f32[40,256]{1,0:T(8,128)}, /*index=5*/f3...) while((s32[]{:T(128)}, f32[256,40,64]{0,2,1:T(8,128)}, ...), condition=%wide.region_3.4_spmd.clone, body=%wide.region_2.3_spmd.clone.sunk | while | flops 404815872 | bytes 1500311 | solution.py:256
  123.2 4.3 %fusion.61 = f32[256,40,64]{0,2,1:T(8,128)} fusion(f32[256,40,64]{0,2,1:T(8,128)} %get-tuple-element.231, s32[]{:T(128)S(6)} %select_n.56, f32[256,256]{1,0:T(8,128)S(1)} %get-tuple-element.245, f32[8,256]{1,0:T(8,128)S(1)} %get-tuple-element.218, f32[8,256]{1,0:T(8,128)S(1)} %get-tuple-element.219, pred[256,256]{1,0:T(8,128)(4,1)S(1)} %iota_compare_fusion.5, ...), kind=kOutput, calls=%fused_computation.8.clone.1 | convolution fusion | flops 404750336 | bytes 1401856 | tf_op jit(solution)/shard_map/while/body/eval_jaxpr/hts,shp->thp/dot_general | solution.py:253
  128.3 4.4 %fusion.61 = f32[256,40,64]{0,2,1:T(8,128)} fusion(f32[256,40,64]{0,2,1:T(8,128)} %get-tuple-element.231, s32[]{:T(128)S(6)} %select_n.56, f32[256,256]{1,0:T(8,128)S(1)} %get-tuple-element.245, f32[8,256]{1,0:T(8,128)S(1)} %get-tuple-element.218, f32[8,256]{1,0:T(8,128)S(1)} %get-tuple-element.219, pred[256,256]{1,0:T(8,128)(4,1)S(1)} %iota_compare_fusion.5, ...), kind=kOutput, calls=%fused_computation.8.clone.1 | convolution fusion | flops 404750336 | bytes 1401856 | tf_op jit(solution)/shard_map/while/body/eval_jaxpr/hts,shp->thp/dot_general | solution.py:253
  133.4 4.4 %fusion.61 = f32[256,40,64]{0,2,1:T(8,128)} fusion(f32[256,40,64]{0,2,1:T(8,128)} %get-tuple-element.231, s32[]{:T(128)S(6)} %select_n.56, f32[256,256]{1,0:T(8,128)S(1)} %get-tuple-element.245, f32[8,256]{1,0:T(8,128)S(1)} %get-tuple-element.218, f32[8,256]{1,0:T(8,128)S(1)} %get-tuple-element.219, pred[256,256]{1,0:T(8,128)(4,1)S(1)} %iota_compare_fusion.5, ...), kind=kOutput, calls=%fused_computation.8.clone.1 | convolution fusion | flops 404750336 | bytes 1401856 | tf_op jit(solution)/shard_map/while/body/eval_jaxpr/hts,shp->thp/dot_general | solution.py:253
  138.5 4.4 %fusion.61 = f32[256,40,64]{0,2,1:T(8,128)} fusion(f32[256,40,64]{0,2,1:T(8,128)} %get-tuple-element.231, s32[]{:T(128)S(6)} %select_n.56, f32[256,256]{1,0:T(8,128)S(1)} %get-tuple-element.245, f32[8,256]{1,0:T(8,128)S(1)} %get-tuple-element.218, f32[8,256]{1,0:T(8,128)S(1)} %get-tuple-element.219, pred[256,256]{1,0:T(8,128)(4,1)S(1)} %iota_compare_fusion.5, ...), kind=kOutput, calls=%fused_computation.8.clone.1 | convolution fusion | flops 404750336 | bytes 1401856 | tf_op jit(solution)/shard_map/while/body/eval_jaxpr/hts,shp->thp/dot_general | solution.py:253
  143.6 4.3 %fusion.61 = f32[256,40,64]{0,2,1:T(8,128)} fusion(f32[256,40,64]{0,2,1:T(8,128)} %get-tuple-element.231, s32[]{:T(128)S(6)} %select_n.56, f32[256,256]{1,0:T(8,128)S(1)} %get-tuple-element.245, f32[8,256]{1,0:T(8,128)S(1)} %get-tuple-element.218, f32[8,256]{1,0:T(8,128)S(1)} %get-tuple-element.219, pred[256,256]{1,0:T(8,128)(4,1)S(1)} %iota_compare_fusion.5, ...), kind=kOutput, calls=%fused_computation.8.clone.1 | convolution fusion | flops 404750336 | bytes 1401856 | tf_op jit(solution)/shard_map/while/body/eval_jaxpr/hts,shp->thp/dot_general | solution.py:253
  147.9 4.7 %multiply_reduce_fusion = (f32[256]{0:T(256)S(1)}, f32[256,40,64]{0,2,1:T(8,128)S(1)}) fusion(f32[256,40,64]{0,2,1:T(8,128)} %get-tuple-element.254, f32[40]{0:T(128)S(1)} %copy-done.12, f32[256,40,64]{0,2,1:T(8,128)} %get-tuple-element.126, f32[256,40,64]{0,2,1:T(8,128)} %bitcast.115, f32[256,40]{0,1:T(8,128)S(1)} %copy-done.3, ...), kind=kLoop, calls=%fused_computation.42 | loop fusion | flops 7864064 | bytes 11838624 | tf_op jit(solution)/shard_map/reduce_sum | solution.py:283
  154.0 1.6 %copy.51 = bf16[1,256,2560]{2,1,0:T(8,128)(2,1)} copy(bf16[1,256,2560]{1,2,0:T(8,128)(2,1)S(1)} %fusion.34) | data formatting | bytes 2621440
  (64 shorter events, 17.2 us)
Async XLA Ops:
  1.4 15.2 %collective-permute-start = (bf16[1,3,2816]{2,1,0:T(4,128)(2,1)S(1)}, bf16[1,3,2816]{2,1,0:T(4,128)(2,1)}, u32[]{:S(2)}, u32[]{:S(2)}) collective-permute-start(bf16[1,3,2816]{2,1,0:T(4,128)(2,1)S(1)} %slice.58), channel_id=1, source_target_pairs={{0,1},{1,2},{2,3},{3,4},{4,5},{5,6},{6,7},{8,9},{9,10},{10,11},{11... | collective-permute-start | bytes 50696 | tf_op jit(solution)/shard_map/ppermute | solution.py:220
  17.8 1.0 copy-start.5
  17.8 1.0 copy-start.6
  17.8 1.0 copy-start.7
  17.8 1.0 copy-start.8
  17.9 1.0 copy-start.11
  37.6 4.3 %copy-start = (f32[128,2560]{1,0:T(8,128)S(1)}, f32[128,2560]{1,0:T(8,128)}, u32[]{:S(2)}) copy-start(f32[128,2560]{1,0:T(8,128)} %shard_map.122) | copy-start | bytes 3932164
  37.7 4.3 %copy-start.1 = (f32[256,2560]{0,1:T(8,128)S(1)}, f32[256,2560]{0,1:T(8,128)}, u32[]{:S(2)}) copy-start(f32[256,2560]{0,1:T(8,128)} %get-tuple-element.169) | copy-start | bytes 7864324
  37.7 4.2 %copy-start.4 = (f32[2560]{0:T(1024)S(1)}, f32[2560]{0:T(1024)}, u32[]{:S(2)}) copy-start(f32[2560]{0:T(1024)} %mul.248) | copy-start | bytes 30724
  50.4 72.0 %copy-start.2 = (f32[256,256]{1,0:T(8,128)S(1)}, f32[256,256]{1,0:T(8,128)}, u32[]{:S(2)}) copy-start(f32[256,256]{1,0:T(8,128)} %fusion.37) | copy-start | bytes 786436
  122.5 25.5 %copy-start.3 = (f32[256,40]{0,1:T(8,128)S(1)}, f32[256,40]{0,1:T(8,128)}, u32[]{:S(2)}) copy-start(f32[256,40]{0,1:T(8,128)} %get-tuple-element.171) | copy-start | bytes 122884
  122.5 25.5 %copy-start.12 = (f32[40]{0:T(128)S(1)}, f32[40]{0:T(128)}, u32[]{:S(2)}) copy-start(f32[40]{0:T(128)} %param.20) | copy-start | bytes 484
  147.9 4.7 %copy-start.10 = (f32[2560]{0:T(1024)S(1)}, f32[2560]{0:T(1024)}, u32[]{:S(2)}) copy-start(f32[2560]{0:T(1024)} %param.21) | copy-start | bytes 30724
  154.0 1.6 %copy-start.9 = (f32[1,10,128]{2,1,0:T(8,128)S(1)}, f32[1,10,128]{2,1,0:T(8,128)}, u32[]{:S(2)}) copy-start(f32[1,10,128]{2,1,0:T(8,128)} %shard_map.123) | copy-start | bytes 15364

commit v7 on v6

--- a/solution.py
+++ b/solution.py
@@ -240,22 +240,12 @@
     )
     positions = jnp.arange(row_count, dtype=jnp.int32)
     causal = positions[:, None] >= positions[None, :]
-    cum_heads = cumulative.T
-    dt_heads = dt_vals.T
-
-    def group_step(group_index, buffer):
-        head_start = group_index * group_heads
-        cum_group = lax.dynamic_slice_in_dim(cum_heads, head_start, group_heads, 0)
-        dt_group = lax.dynamic_slice_in_dim(dt_heads, head_start, group_heads, 0)
-        x_group = lax.dynamic_slice_in_dim(x_wide, head_start, group_heads, 1)
-        spread = jnp.where(causal[None], cum_group[:, :, None] - cum_group[:, None, :], -1e30)
-        weight = jnp.exp(spread) * dt_group[:, None, :] * scores[None]
-        partial_value = jnp.einsum("hts,shp->thp", weight, x_group, precision=highest)
-        return lax.dynamic_update_slice_in_dim(buffer, partial_value, head_start, 1)
-
-    diagonal_part = lax.fori_loop(
-        0, H // group_heads, group_step, jnp.zeros((row_count, H, P_SIZE), jnp.float32)
-    )
+    masked_scores = jnp.where(causal, scores, 0.0)
+    grow = jnp.exp(-cumulative) * dt_vals
+    shrink = jnp.exp(cumulative)
+    scaled_x = (grow[:, :, None] * x_wide).reshape(row_count, H * P_SIZE)
+    mixed = jnp.dot(masked_scores, scaled_x, precision=highest).reshape(row_count, H, P_SIZE)
+    diagonal_part = shrink[:, :, None] * mixed
     final_log = cumulative[row_count - 1]
     to_end = jnp.exp(final_log[None, :] - cumulative) * dt_vals
     decay_total = jnp.exp(final_log)

time: 157 us -> 132 us (0.84)
  matrix products: 32.4 us -> 19.3 us
  local copies, waits for them, and re-layouts: 22.7 us -> 13.9 us
  other arithmetic: 20.6 us -> 17.6 us
    dot_general x5 -> x1, matrix products: 21.7 us -> 8.6 us  [local_terms(): jnp.dot(masked_scores, scaled_x, precision=highest)]
    reduce_sum x1 -> x0, other arithmetic: 4.66 us -> none  [finish_block(): jnp.mean(gated_out * gated_out, axis=-1, keepdims=True) + 1e-05]
    dynamic_slice x5 -> x0, local copies, waits for them, and re-layouts: 3.59 us -> none  [group_step(): dt_group = lax.dynamic_slice_in_dim(dt_heads, head_start, group_heads, 0)]
    unnamed x30 -> x18, local copies, waits for them, and re-layouts: 5.51 us -> 2.32 us
    reshape x0 -> x1, local copies, waits for them, and re-layouts: none -> 2.16 us  [finish_block(): ssm_out.reshape(row_count, H * P_SIZE)]
    convert_element_type x1, other arithmetic: 1.37 us -> 3.38 us  [finish_block(): return (gated_out * inv_rms * norm_gain).astype(jnp.bfloat16)]
    convert_element_type x0 -> x1, local copies, waits for them, and re-layouts: none -> 1.86 us  [finish_block(): gate_rows.astype(jnp.float32)]
    broadcast_in_dim x1 -> x0, local copies, waits for them, and re-layouts: 1.82 us -> none  [local_terms(): jnp.zeros((row_count, H, P_SIZE), jnp.float32)]
where the time goes in v7:
time: 132 us; the launch traced here: 131 us
  Pallas kernels  77 us (58%)
  matrix products  19.3 us (15%)
  other arithmetic  17.6 us (13%)
  local copies, waits for them, and re-layouts  13.9 us (11%)
  starting transfers between devices  1.74 us (1%)
  between operations  1.52 us (1%)
    pallas_call x1, Pallas kernels, reduce_scatter_blocks(): pl.pallas_call(functools.partial(_reduce_scatter_kernel, plan), out_shape...  69.7 us
    dot_general x1, matrix products, local_terms(): jnp.dot(masked_scores, scaled_x, precision=highest)  8.6 us
    pallas_call x1, Pallas kernels, carry_chain(): pl.pallas_call(functools.partial(_chain_kernel, chunk), out_shape=jax.Sha...  7.34 us
    dot_general x2, matrix products, state_product(): lax.dot_general(b_wide, (weight[:, :, None] * x_wide).reshape(row_count,...  5.28 us
    convert_element_type x1, other arithmetic, on_device(): activated = jax.nn.silu(conv_sum).astype(jnp.bfloat16)  4.8 us
    dot_general x1, matrix products, finish_block(): jnp.dot(c_wide, h_in, precision=highest).reshape(row_count, H, P_SIZE)  4.26 us
    convert_element_type x1, other arithmetic, finish_block(): return (gated_out * inv_rms * norm_gain).astype(jnp.bfloat16)  3.38 us
    mul x1, other arithmetic, state_product(): weight[:, :, None] * x_wide  2.87 us
  transfers between devices with their start and end apart: 1, of which 0 were waited for; matrix products, arithmetic and copies ran while one was open for 8% of the time, Pallas kernels for 0%

profile of v7, /device:TPU:6, one launch (start us, length us, event | category | flops | bytes accessed | tf_op | source)
XLA Modules:
  0.0 131.1 jit_solution(15211861725697755660)
XLA Ops:
  0.6 0.9 slice.60
  1.6 1.7 %collective-permute-start = (bf16[1,3,2816]{2,1,0:T(4,128)(2,1)S(1)}, bf16[1,3,2816]{2,1,0:T(4,128)(2,1)S(1)}, u32[]{:S(2)}, u32[]{:S(2)}) collective-permute-start(bf16[1,3,2816]{2,1,0:T(4,128)(2,1)S(1)} %slice.60), channel_id=1, source_target_pairs={{0,1},{1,2},{2,3},{3,4},{4,5},{5,6},{6,7},{8,9},{9,10},{10,11},{11... | collective-permute-start | bytes 50696 | tf_op jit(solution)/shard_map/ppermute | solution.py:220
  4.0 0.8 copy_bitcast_fusion
  5.7 0.7 and_convert_fusion
  7.0 0.9 exponential_multiply_fusion.1
  7.8 1.1 slice_reduce_fusion.5
  8.9 1.7 %copy.45 = bf16[1,256,2816]{1,2,0:T(8,128)(2,1)S(1)} copy(bf16[1,256,2816]{2,1,0:T(8,128)(2,1)} %param.11) | data formatting | bytes 2883584 | tf_op args[0]
  10.7 0.7 broadcast_in_dim_reshape.4.decay_ref
  12.2 1.9 %copy.50 = f32[1,256,2560]{1,2,0:T(8,128)} copy(bf16[1,256,2560]{2,1,0:T(8,128)(2,1)S(1)} %copy-done.2) | data formatting | bytes 3932160 | tf_op jit(solution)/shard_map/convert_element_type | solution.py:272
  14.4 0.9 maximum_convert_fusion
  15.4 4.8 %multiply_convert_fusion = bf16[256,2816]{0,1:T(8,128)(2,1)S(1)} fusion(f32[1,259,2816]{1,2,0:T(8,128)S(1)} %maximum_convert_fusion, f32[2816]{0:T(1024)S(1)} %get-tuple-element.4, f32[2816]{0:T(1024)S(1)} %get-tuple-element.5, f32[2816]{0:T(1024)S(1)} %get-tuple-element.3, f32[2816]{0:T(1024)S(1)} %get-tuple-element.2, f32[2816]{0:T(1024)S(1)} %copy-done.6), kind=kLoop, calls=%fused_computation.14 | loop fusion | flops 9371648 | bytes 13032448 | tf_op jit(solution)/shard_map/convert_element_type | solution.py:298
  20.2 1.7 %slice_convert_fusion = f32[256,2560]{0,1:T(8,128)} fusion(bf16[256,2816]{0,1:T(8,128)(2,1)S(1)} %multiply_convert_fusion), kind=kLoop, calls=%fused_computation.24 | loop fusion | flops 655360 | bytes 3932160 | tf_op jit(solution)/shard_map/convert_element_type | solution.py:235
  21.9 0.9 fusion.9
  22.9 2.9 %bitcast_multiply_fusion = (f32[256,2560]{0,1:T(8,128)}, f32[256,2560]{0,1:T(8,128)S(1)}, f32[256,2560]{0,1:T(8,128)}) fusion(f32[256,40]{0,1:T(8,128)S(1)} %get-tuple-element.14, bf16[256,2816]{0,1:T(8,128)(2,1)S(1)} %multiply_convert_fusion, f32[256,40]{0,1:T(8,128)S(1)} %get-tuple-element.12, f32[256,40]{0,1:T(8,128)S(1)} %get-tuple-element.11), kind=kLoop, calls=%fused_computation.15 | loop fusion | flops 2621440 | bytes 9297920 | tf_op jit(solution)/shard_map/mul | solution.py:227
  25.7 2.6 %fusion.14.local_ref = f32[128,2560]{1,0:T(8,128)} fusion(f32[256,2560]{0,1:T(8,128)S(1)} %get-tuple-element.9, bf16[256,2816]{0,1:T(8,128)(2,1)S(1)} %multiply_convert_fusion), kind=kOutput, calls=%fused_computation.32 | convolution fusion | flops 1006632960 | bytes 3997696 | tf_op jit(solution)/shard_map/dot_general | solution.py:225
  28.3 7.3 %shard_map.122 = f32[128,2560]{1,0:T(8,128)} custom-call(f32[128,2560]{1,0:T(8,128)} %fusion.14.local_ref, f32[1,2560]{1,0:T(1,128)} %broadcast_in_dim_reshape.4.decay_ref), custom_call_target="tpu_custom_call" | custom-call | tf_op jit(solution)/shard_map/pallas_call | solution.py:199
  35.7 4.3 %fusion.10 = f32[256,2560]{0,1:T(8,128)} fusion(f32[128,2560]{1,0:T(8,128)} %shard_map.122, bf16[256,2816]{0,1:T(8,128)(2,1)S(1)} %multiply_convert_fusion), kind=kOutput, calls=%fused_computation.28 | convolution fusion | flops 1006632960 | bytes 3997696 | tf_op jit(solution)/shard_map/dot_general | solution.py:268
  40.0 2.7 %fusion = f32[2560,128]{0,1:T(8,128)} fusion(f32[256,2560]{0,1:T(8,128)S(1)} %copy-done.1, f32[128,2560]{1,0:T(8,128)S(1)} %copy-done, f32[2560]{0:T(1024)S(1)} %mul.226, bf16[256,2816]{0,1:T(8,128)(2,1)S(1)} %multiply_convert_fusion), kind=kOutput, calls=%fused_computation.1 | convolution fusion | flops 1007288320 | bytes 5320704 | tf_op jit(solution)/shard_map/dot_general | solution.py:225
  42.6 1.7 %copy.51 = f32[2560,128]{1,0:T(8,128)S(1)} copy(f32[2560,128]{0,1:T(8,128)} %fusion) | data formatting | bytes 2621440 | tf_op jit(solution)/shard_map/transpose | solution.py:314
  44.5 1.6 %copy.52 = f32[2,2,2,2,2,2,2,2,10,128]{9,8,7,6,5,4,3,2,1,0:T(8,128)} copy(f32[2,2,2,2,2,2,2,2,10,128]{9,8,0,1,2,3,4,5,6,7:T(8,128)S(1)} %bitcast.112) | data formatting | bytes 2621440 | tf_op jit(solution)/shard_map/transpose | solution.py:138
  46.7 69.7 %shard_map.123 = f32[1,10,128]{2,1,0:T(8,128)} custom-call(f32[256,10,128]{2,1,0:T(8,128)} %bitcast.111, f32[1,128]{1,0:T(1,128)} %broadcast_in_dim.27.label_ref), custom_call_target="tpu_custom_call" | custom-call | tf_op jit(solution)/shard_map/pallas_call | solution.py:115
  116.4 8.6 %multiply_reduce_fusion = (f32[256]{0:T(256)S(1)}, f32[256,40,64]{0,2,1:T(8,128)}) fusion(f32[256,40,64]{0,2,1:T(8,128)} %bitcast.114, f32[256,40,64]{0,2,1:T(8,128)} %bitcast.115, f32[40]{0:T(128)S(1)} %copy-done.7, f32[256,40]{0,1:T(8,128)S(1)} %get-tuple-element.13, f32[256,40,64]{0,2,1:T(8,128)} %bitcast.116, f32[256,256,1]{1,0,2:T(8,128)S(1)} %copy-done.3, ...), kind=kOutput, calls=%fused_computation.20 | convolution fusion | flops 2020474624 | bytes 13411488 | tf_op jit(solution)/shard_map/dot_general | solution.py:247
  125.0 2.2 %copy.49 = f32[1,256,2560]{2,1,0:T(8,128)S(1)} copy(f32[1,256,2560]{1,2,0:T(8,128)} %bitcast.113) | data formatting | bytes 5242880 | tf_op jit(solution)/shard_map/reshape | solution.py:272
  127.2 3.4 %multiply_convert_fusion.1 = bf16[1,256,2560]{2,1,0:T(8,128)(2,1)} fusion(f32[1,256,2560]{2,1,0:T(8,128)S(1)} %copy.49, f32[2560]{0:T(1024)S(1)} %copy-done.5, f32[256]{0:T(256)S(1)} %add_rsqrt_fusion, bf16[1,256,2560]{2,1,0:T(8,128)(2,1)} %param.12), kind=kLoop, calls=%fused_computation.19 | loop fusion | flops 5898240 | bytes 5254144 | tf_op jit(solution)/shard_map/convert_element_type | solution.py:274
  (37 shorter events, 4.0 us)
Async XLA Ops:
  0.6 11.5 %copy-start.2 = (bf16[1,256,2560]{2,1,0:T(8,128)(2,1)S(1)}, bf16[1,256,2560]{2,1,0:T(8,128)(2,1)}, u32[]{:S(2)}) copy-start(bf16[1,256,2560]{2,1,0:T(8,128)(2,1)} %param.12) | copy-start | bytes 3932164
  1.6 12.5 %collective-permute-start = (bf16[1,3,2816]{2,1,0:T(4,128)(2,1)S(1)}, bf16[1,3,2816]{2,1,0:T(4,128)(2,1)S(1)}, u32[]{:S(2)}, u32[]{:S(2)}) collective-permute-start(bf16[1,3,2816]{2,1,0:T(4,128)(2,1)S(1)} %slice.60), channel_id=1, source_target_pairs={{0,1},{1,2},{2,3},{3,4},{4,5},{5,6},{6,7},{8,9},{9,10},{10,11},{11... | collective-permute-start | bytes 50696 | tf_op jit(solution)/shard_map/ppermute | solution.py:220
  14.4 0.9 copy-start.6
  35.7 4.3 %copy-start = (f32[128,2560]{1,0:T(8,128)S(1)}, f32[128,2560]{1,0:T(8,128)}, u32[]{:S(2)}) copy-start(f32[128,2560]{1,0:T(8,128)} %shard_map.122) | copy-start | bytes 3932164
  35.7 4.3 %copy-start.1 = (f32[256,2560]{0,1:T(8,128)S(1)}, f32[256,2560]{0,1:T(8,128)}, u32[]{:S(2)}) copy-start(f32[256,2560]{0,1:T(8,128)} %get-tuple-element.8) | copy-start | bytes 7864324
  44.5 71.8 %copy-start.3 = (f32[256,256,1]{1,0,2:T(8,128)S(1)}, f32[256,256,1]{1,0,2:T(8,128)}, u32[]{:S(2)}) copy-start(f32[256,256,1]{1,0,2:T(8,128)} %fusion.9) | copy-start | bytes 786436
  44.5 71.8 %copy-start.7 = (f32[40]{0:T(128)S(1)}, f32[40]{0:T(128)}, u32[]{:S(2)}) copy-start(f32[40]{0:T(128)} %param.18) | copy-start | bytes 484
  125.0 2.2 %copy-start.5 = (f32[2560]{0:T(1024)S(1)}, f32[2560]{0:T(1024)}, u32[]{:S(2)}) copy-start(f32[2560]{0:T(1024)} %param.19) | copy-start | bytes 30724
  127.2 3.4 %copy-start.4 = (f32[1,10,128]{2,1,0:T(8,128)S(1)}, f32[1,10,128]{2,1,0:T(8,128)}, u32[]{:S(2)}) copy-start(f32[1,10,128]{2,1,0:T(8,128)} %shard_map.123) | copy-start | bytes 15364

commit v8 on v7

--- a/solution.py
+++ b/solution.py
@@ -35,9 +35,22 @@
     send_sem, recv_sem = rest[rounds], rest[rounds + 1]
     coords = {"dp": lax.axis_index("dp"), "seq": lax.axis_index("seq")}
 
+    y_count = lax.axis_size("seq") // 2
+    core = coords["seq"] % 2
+    y_virtual = (coords["seq"] // 2 + (y_count - 1) * core) % y_count
+
     def partner_of(axis, bit):
         me = coords[axis]
+        if axis == "seq" and bit > 1:
+            virtual = 2 * y_virtual + core
+            other = virtual + bit - 2 * bit * ((virtual // bit) % 2)
+            return 2 * ((other // 2 + y_count - (y_count - 1) * core) % y_count) + core
         return me + bit - 2 * bit * ((me // bit) % 2)
+
+    def bit_of(axis, bit):
+        if axis == "seq" and bit > 1:
+            return ((2 * y_virtual + core) // bit) % 2
+        return (coords[axis] // bit) % 2
 
     def device_of(axis, bit):
         if axis == "dp":
@@ -74,7 +87,7 @@
     copies = []
     for index, (axis, bit) in enumerate(plan):
         half = size // 2
-        mine = (coords[axis] // bit) % 2
+        mine = bit_of(axis, bit)
         keep = base + mine * half
         give = base + (1 - mine) * half
         if index == len(seq_rounds):
@@ -314,7 +327,9 @@
     mean_state = (jnp.repeat(carry_weight, P_SIZE)[None] * h_in + read_local).T
     batch_count = lax.axis_size("dp")
     block_rows = mean_state.shape[0] // (batch_count * seq_count)
-    blocks = to_halving_order(mean_state, batch_count, seq_count, block_rows)
+    by_chip = mean_state.reshape(batch_count, seq_count // 2, 2, block_rows, N)
+    by_chip = jnp.stack([by_chip[:, :, 0], jnp.roll(by_chip[:, :, 1], -1, axis=1)], axis=2)
+    blocks = to_halving_order(by_chip.reshape(-1, N), batch_count, seq_count, block_rows)
     steering = reduce_scatter_blocks(blocks, labels[0])[0]
     layer_out = finish_block(
         diagonal_part, x_wide, c_wide, cumulative, h_in, gate_input[0], d_skip, norm_gain

time: 132 us -> 133 us (level)
  local copies, waits for them, and re-layouts: 13.9 us -> 17.4 us
  Pallas kernels: 77 us -> 74.7 us
  matrix products: 19.3 us -> 17.4 us
  other arithmetic: 17.6 us -> 19.2 us
    pallas_call x1, Pallas kernels: 69.7 us -> 67.2 us  [reduce_scatter_blocks(): pl.pallas_call(functools.partial(_reduce_scatter_kernel, plan), out_shape...]
    dot_general x1, matrix products: 4.26 us -> 2.81 us  [finish_block(): jnp.dot(c_wide, h_in, precision=highest).reshape(row_count, H, P_SIZE)]
where the time goes in v8:
time: 133 us; the launch traced here: 132 us
  Pallas kernels  74.7 us (56%)
  other arithmetic  19.2 us (14%)
  local copies, waits for them, and re-layouts  17.4 us (13%)
  matrix products  17.4 us (13%)
  starting transfers between devices  1.74 us (1%)
  between operations  1.58 us (1%)
    pallas_call x1, Pallas kernels, reduce_scatter_blocks(): pl.pallas_call(functools.partial(_reduce_scatter_kernel, plan), out_shape...  67.2 us
    dot_general x1, matrix products, local_terms(): jnp.dot(masked_scores, scaled_x, precision=highest)  7.87 us
    pallas_call x1, Pallas kernels, carry_chain(): pl.pallas_call(functools.partial(_chain_kernel, chunk), out_shape=jax.Sha...  7.44 us
    dot_general x2, matrix products, state_product(): lax.dot_general(b_wide, (weight[:, :, None] * x_wide).reshape(row_count,...  6.29 us
    convert_element_type x1, other arithmetic, on_device(): activated = jax.nn.silu(conv_sum).astype(jnp.bfloat16)  4.8 us
    convert_element_type x1, other arithmetic, finish_block(): return (gated_out * inv_rms * norm_gain).astype(jnp.bfloat16)  3.38 us
    unnamed x18, local copies, waits for them, and re-layouts  3.27 us
    mul x1, other arithmetic, state_product(): weight[:, :, None] * x_wide  2.82 us
  transfers between devices with their start and end apart: 1, of which 0 were waited for; matrix products, arithmetic and copies ran while one was open for 8% of the time, Pallas kernels for 0%

profile of v8, /device:TPU:6, one launch (start us, length us, event | category | flops | bytes accessed | tf_op | source)
XLA Modules:
  0.0 132.0 jit_solution(8894874115444119731)
XLA Ops:
  0.6 0.9 slice.74
  1.6 1.7 %collective-permute-start = (bf16[1,3,2816]{2,1,0:T(4,128)(2,1)S(1)}, bf16[1,3,2816]{2,1,0:T(4,128)(2,1)S(1)}, u32[]{:S(2)}, u32[]{:S(2)}) collective-permute-start(bf16[1,3,2816]{2,1,0:T(4,128)(2,1)S(1)} %slice.74), channel_id=1, source_target_pairs={{0,1},{1,2},{2,3},{3,4},{4,5},{5,6},{6,7},{8,9},{9,10},{10,11},{11... | collective-permute-start | bytes 50696 | tf_op jit(solution)/shard_map/ppermute | solution.py:233
  4.0 0.8 copy_bitcast_fusion
  7.0 1.5 %exponential_multiply_fusion.1 = (f32[256,40]{0,1:T(8,128)S(1)}, f32[256,40]{0,1:T(8,128)S(1)}, f32[256,40]{0,1:T(8,128)}, f32[256,40]{0,1:T(8,128)S(1)}) fusion(f32[40]{0:T(128)} %param.16, bf16[1,256,40]{1,2,0:T(8,128)(2,1)} %param.13, f32[40]{0:T(128)S(1)} %slice_reduce_fusion.1, f32[256,40]{0,1:T(8,128)S(1)} %multiply_reduce_fusion.1, ...), kind=kLoop, calls=%fused_computation.52 | loop fusion | flops 153600 | bytes 266880 | tf_op jit(solution)/shard_map/mul | solution.py:257
  8.4 1.1 slice_reduce_fusion.5
  9.5 1.7 %copy.48 = bf16[1,256,2816]{1,2,0:T(8,128)(2,1)S(1)} copy(bf16[1,256,2816]{2,1,0:T(8,128)(2,1)} %param.11) | data formatting | bytes 2883584 | tf_op args[0]
  12.8 1.9 %copy.53 = f32[1,256,2560]{1,2,0:T(8,128)} copy(bf16[1,256,2560]{2,1,0:T(8,128)(2,1)S(1)} %copy-done.1) | data formatting | bytes 3932160 | tf_op jit(solution)/shard_map/convert_element_type | solution.py:285
  15.1 0.9 maximum_convert_fusion
  16.0 4.8 %multiply_convert_fusion = bf16[256,2816]{0,1:T(8,128)(2,1)S(1)} fusion(f32[1,259,2816]{1,2,0:T(8,128)S(1)} %maximum_convert_fusion, f32[2816]{0:T(1024)S(1)} %get-tuple-element.4, f32[2816]{0:T(1024)S(1)} %get-tuple-element.5, f32[2816]{0:T(1024)S(1)} %get-tuple-element.3, f32[2816]{0:T(1024)S(1)} %get-tuple-element.2, f32[2816]{0:T(1024)S(1)} %copy-done.6), kind=kLoop, calls=%fused_computation.14 | loop fusion | flops 9371648 | bytes 13032448 | tf_op jit(solution)/shard_map/convert_element_type | solution.py:311
  20.8 2.8 %bitcast_multiply_fusion = (f32[256,2560]{0,1:T(8,128)}, f32[256,2560]{0,1:T(8,128)S(1)}, f32[256,2560]{0,1:T(8,128)}) fusion(f32[256,40]{0,1:T(8,128)S(1)} %get-tuple-element.16, bf16[256,2816]{0,1:T(8,128)(2,1)S(1)} %multiply_convert_fusion, f32[256,40]{0,1:T(8,128)S(1)} %get-tuple-element.14, f32[256,40]{0,1:T(8,128)S(1)} %get-tuple-element.13), kind=kLoop, calls=%fused_computation.15 | loop fusion | flops 2621440 | bytes 9297920 | tf_op jit(solution)/shard_map/mul | solution.py:240
  23.6 2.6 %fusion.14.local_ref = f32[128,2560]{1,0:T(8,128)} fusion(f32[256,2560]{0,1:T(8,128)S(1)} %get-tuple-element.11, bf16[256,2816]{0,1:T(8,128)(2,1)S(1)} %multiply_convert_fusion), kind=kOutput, calls=%fused_computation.35 | convolution fusion | flops 1006632960 | bytes 3997696 | tf_op jit(solution)/shard_map/dot_general | solution.py:238
  26.3 7.4 %shard_map.122 = f32[128,2560]{1,0:T(8,128)} custom-call(f32[128,2560]{1,0:T(8,128)} %fusion.14.local_ref, f32[1,2560]{1,0:T(1,128)} %broadcast_in_dim_reshape.4.decay_ref), custom_call_target="tpu_custom_call" | custom-call | tf_op jit(solution)/shard_map/pallas_call | solution.py:212
  33.7 3.7 %fusion = f32[2560,128]{0,1:T(8,128)S(1)} fusion(f32[256,2560]{0,1:T(8,128)} %get-tuple-element.10, f32[128,2560]{1,0:T(8,128)} %shard_map.122, f32[2560]{0:T(1024)S(1)} %mul.226, bf16[256,2816]{0,1:T(8,128)(2,1)S(1)} %multiply_convert_fusion), kind=kOutput, calls=%fused_computation.1 | convolution fusion | flops 1007288320 | bytes 5320704 | tf_op jit(solution)/shard_map/dot_general | solution.py:238
  37.4 1.5 %copy.54 = f32[2560,128]{1,0:T(8,128)} copy(f32[2560,128]{0,1:T(8,128)S(1)} %fusion) | data formatting | bytes 2621440 | tf_op jit(solution)/shard_map/transpose | solution.py:327
  38.9 1.3 %reshape.159 = f32[32,4,2,10,128]{4,3,2,1,0:T(8,128)S(1)} reshape(f32[2560,128]{1,0:T(8,128)} %copy.54) | data formatting | bytes 2621440 | tf_op jit(solution)/shard_map/reshape | solution.py:330
  40.6 1.0 copy-done
  41.5 2.8 %fusion.10 = f32[256,2560]{0,1:T(8,128)} fusion(f32[128,2560]{1,0:T(8,128)S(1)} %copy-done, bf16[256,2816]{0,1:T(8,128)(2,1)S(1)} %multiply_convert_fusion), kind=kOutput, calls=%fused_computation.31 | convolution fusion | flops 1006632960 | bytes 3997696 | tf_op jit(solution)/shard_map/dot_general | solution.py:281
  44.3 1.7 %slice_convert_fusion = f32[256,2560]{0,1:T(8,128)} fusion(bf16[256,2816]{0,1:T(8,128)(2,1)S(1)} %multiply_convert_fusion), kind=kLoop, calls=%fused_computation.27 | loop fusion | flops 655360 | bytes 3932160 | tf_op jit(solution)/shard_map/convert_element_type | solution.py:248
  47.1 0.9 maximum_bitcast_fusion
  48.1 2.1 %copy.57 = f32[2,2,2,2,2,2,2,2,10,128]{9,8,7,6,5,4,3,2,1,0:T(8,128)} copy(f32[2,2,2,2,2,2,2,2,10,128]{9,3,4,5,6,7,8,1,2,0:T(2,128)S(1)} %maximum_bitcast_fusion) | data formatting | bytes 2621440 | tf_op jit(solution)/shard_map/transpose | solution.py:151
  50.7 67.2 %shard_map.123 = f32[1,10,128]{2,1,0:T(8,128)} custom-call(f32[256,10,128]{2,1,0:T(8,128)} %bitcast.116, f32[1,128]{1,0:T(1,128)} %broadcast_in_dim.27.label_ref), custom_call_target="tpu_custom_call" | custom-call | tf_op jit(solution)/shard_map/pallas_call | solution.py:128
  117.9 7.9 %multiply_reduce_fusion = (f32[256]{0:T(256)S(1)}, f32[256,40,64]{0,2,1:T(8,128)}) fusion(f32[256,40,64]{0,2,1:T(8,128)S(1)} %bitcast.120, f32[256,40,64]{0,2,1:T(8,128)} %bitcast.122, f32[40]{0:T(128)S(1)} %copy-done.7, f32[256,40]{0,1:T(8,128)S(1)} %copy-done.3, f32[256,40,64]{0,2,1:T(8,128)} %bitcast.121, f32[256,256,1]{1,0,2:T(8,128)S(1)} %fusion.9, ...), kind=kOutput, calls=%fused_computation.20 | convolution fusion | flops 2020474624 | bytes 13411488 | tf_op jit(solution)/shard_map/dot_general | solution.py:260
  125.8 2.2 %copy.52 = f32[1,256,2560]{2,1,0:T(8,128)S(1)} copy(f32[1,256,2560]{1,2,0:T(8,128)} %bitcast.119) | data formatting | bytes 5242880 | tf_op jit(solution)/shard_map/reshape | solution.py:285
  128.0 3.4 %multiply_convert_fusion.1 = bf16[1,256,2560]{2,1,0:T(8,128)(2,1)} fusion(f32[1,256,2560]{2,1,0:T(8,128)S(1)} %copy.52, f32[2560]{0:T(1024)S(1)} %copy-done.5, f32[256]{0:T(256)S(1)} %add_rsqrt_fusion, bf16[1,256,2560]{2,1,0:T(8,128)(2,1)} %param.12), kind=kLoop, calls=%fused_computation.19 | loop fusion | flops 5898240 | bytes 5254144 | tf_op jit(solution)/shard_map/convert_element_type | solution.py:287
  (44 shorter events, 6.6 us)
Async XLA Ops:
  0.6 12.1 %copy-start.1 = (bf16[1,256,2560]{2,1,0:T(8,128)(2,1)S(1)}, bf16[1,256,2560]{2,1,0:T(8,128)(2,1)}, u32[]{:S(2)}) copy-start(bf16[1,256,2560]{2,1,0:T(8,128)(2,1)} %param.12) | copy-start | bytes 3932164
  1.6 13.1 %collective-permute-start = (bf16[1,3,2816]{2,1,0:T(4,128)(2,1)S(1)}, bf16[1,3,2816]{2,1,0:T(4,128)(2,1)S(1)}, u32[]{:S(2)}, u32[]{:S(2)}) collective-permute-start(bf16[1,3,2816]{2,1,0:T(4,128)(2,1)S(1)} %slice.74), channel_id=1, source_target_pairs={{0,1},{1,2},{2,3},{3,4},{4,5},{5,6},{6,7},{8,9},{9,10},{10,11},{11... | collective-permute-start | bytes 50696 | tf_op jit(solution)/shard_map/ppermute | solution.py:233
  15.1 0.9 copy-start.6
  40.2 1.3 copy-start
  48.1 69.9 %copy-start.2 = (f32[1,256,2560]{1,2,0:T(8,128)S(1)}, f32[1,256,2560]{1,2,0:T(8,128)}, u32[]{:S(2)}) copy-start(f32[1,256,2560]{1,2,0:T(8,128)} %copy.53) | copy-start | bytes 7864324
  48.1 69.9 %copy-start.3 = (f32[256,40]{0,1:T(8,128)S(1)}, f32[256,40]{0,1:T(8,128)}, u32[]{:S(2)}) copy-start(f32[256,40]{0,1:T(8,128)} %get-tuple-element.15) | copy-start | bytes 122884
  48.1 69.9 %copy-start.7 = (f32[40]{0:T(128)S(1)}, f32[40]{0:T(128)}, u32[]{:S(2)}) copy-start(f32[40]{0:T(128)} %param.18) | copy-start | bytes 484
  125.8 2.2 %copy-start.5 = (f32[2560]{0:T(1024)S(1)}, f32[2560]{0:T(1024)}, u32[]{:S(2)}) copy-start(f32[2560]{0:T(1024)} %param.19) | copy-start | bytes 30724
  128.0 3.4 %copy-start.4 = (f32[1,10,128]{2,1,0:T(8,128)S(1)}, f32[1,10,128]{2,1,0:T(8,128)}, u32[]{:S(2)}) copy-start(f32[1,10,128]{2,1,0:T(8,128)} %shard_map.123) | copy-start | bytes 15364

commit v9 on v7

--- a/solution.py
+++ b/solution.py
@@ -244,7 +244,7 @@
     grow = jnp.exp(-cumulative) * dt_vals
     shrink = jnp.exp(cumulative)
     scaled_x = (grow[:, :, None] * x_wide).reshape(row_count, H * P_SIZE)
-    mixed = jnp.dot(masked_scores, scaled_x, precision=highest).reshape(row_count, H, P_SIZE)
+    mixed = jnp.dot(masked_scores, scaled_x, precision=lax.Precision.HIGH).reshape(row_count, H, P_SIZE)
     diagonal_part = shrink[:, :, None] * mixed
     final_log = cumulative[row_count - 1]
     to_end = jnp.exp(final_log[None, :] - cumulative) * dt_vals
@@ -265,7 +265,7 @@
 
 def finish_block(diagonal_part, x_wide, c_wide, cumulative, h_in, gate_rows, d_skip, norm_gain):
     row_count = x_wide.shape[0]
-    incoming = jnp.dot(c_wide, h_in, precision=highest).reshape(row_count, H, P_SIZE)
+    incoming = jnp.dot(c_wide, h_in, precision=lax.Precision.HIGH).reshape(row_count, H, P_SIZE)
     ssm_out = (
         diagonal_part + jnp.exp(cumulative)[:, :, None] * incoming + d_skip[None, :, None] * x_wide
     )

time: 132 us -> 130 us (0.985)
  matrix products: 19.3 us -> 17.8 us
    dot_general x2, matrix products: 12.9 us -> 11.4 us  [the longest x1 7.51 us: local_terms(): jnp.dot(masked_scores, scaled_x, precision=lax.Precision.HIGH)]
where the time goes in v9:
time: 130 us
  Pallas kernels  77 us (59%)
  matrix products  17.8 us (14%)
  other arithmetic  17.6 us (14%)
  local copies, waits for them, and re-layouts  13.9 us (11%)
  starting transfers between devices  1.74 us (1%)
  between operations  1.52 us (1%)
    pallas_call x1, Pallas kernels, reduce_scatter_blocks(): pl.pallas_call(functools.partial(_reduce_scatter_kernel, plan), out_shape...  69.7 us
    dot_general x1, matrix products, local_terms(): jnp.dot(masked_scores, scaled_x, precision=lax.Precision.HIGH)  7.51 us
    pallas_call x1, Pallas kernels, carry_chain(): pl.pallas_call(functools.partial(_chain_kernel, chunk), out_shape=jax.Sha...  7.34 us
    dot_general x2, matrix products, state_product(): lax.dot_general(b_wide, (weight[:, :, None] * x_wide).reshape(row_count,...  5.28 us
    convert_element_type x1, other arithmetic, on_device(): activated = jax.nn.silu(conv_sum).astype(jnp.bfloat16)  4.8 us
    dot_general x1, matrix products, finish_block(): jnp.dot(c_wide, h_in, precision=lax.Precision.HIGH)  3.91 us
    convert_element_type x1, other arithmetic, finish_block(): return (gated_out * inv_rms * norm_gain).astype(jnp.bfloat16)  3.38 us
    mul x1, other arithmetic, state_product(): weight[:, :, None] * x_wide  2.87 us
  transfers between devices with their start and end apart: 1, of which 0 were waited for; matrix products, arithmetic and copies ran while one was open for 8% of the time, Pallas kernels for 0%

profile of v9, /device:TPU:6, one launch (start us, length us, event | category | flops | bytes accessed | tf_op | source)
XLA Modules:
  0.0 129.7 jit_solution(16844421562670880430)
XLA Ops:
  0.6 0.9 slice.60
  1.6 1.7 %collective-permute-start = (bf16[1,3,2816]{2,1,0:T(4,128)(2,1)S(1)}, bf16[1,3,2816]{2,1,0:T(4,128)(2,1)S(1)}, u32[]{:S(2)}, u32[]{:S(2)}) collective-permute-start(bf16[1,3,2816]{2,1,0:T(4,128)(2,1)S(1)} %slice.60), channel_id=1, source_target_pairs={{0,1},{1,2},{2,3},{3,4},{4,5},{5,6},{6,7},{8,9},{9,10},{10,11},{11... | collective-permute-start | bytes 50696 | tf_op jit(solution)/shard_map/ppermute | solution.py:220
  4.0 0.8 copy_bitcast_fusion
  5.7 0.7 and_convert_fusion
  7.0 0.9 exponential_multiply_fusion.1
  7.8 1.1 slice_reduce_fusion.5
  8.9 1.7 %copy.45 = bf16[1,256,2816]{1,2,0:T(8,128)(2,1)S(1)} copy(bf16[1,256,2816]{2,1,0:T(8,128)(2,1)} %param.11) | data formatting | bytes 2883584 | tf_op args[0]
  10.7 0.7 broadcast_in_dim_reshape.4.decay_ref
  12.2 1.9 %copy.50 = f32[1,256,2560]{1,2,0:T(8,128)} copy(bf16[1,256,2560]{2,1,0:T(8,128)(2,1)S(1)} %copy-done.2) | data formatting | bytes 3932160 | tf_op jit(solution)/shard_map/convert_element_type | solution.py:272
  14.4 0.9 maximum_convert_fusion
  15.4 4.8 %multiply_convert_fusion = bf16[256,2816]{0,1:T(8,128)(2,1)S(1)} fusion(f32[1,259,2816]{1,2,0:T(8,128)S(1)} %maximum_convert_fusion, f32[2816]{0:T(1024)S(1)} %get-tuple-element.4, f32[2816]{0:T(1024)S(1)} %get-tuple-element.5, f32[2816]{0:T(1024)S(1)} %get-tuple-element.3, f32[2816]{0:T(1024)S(1)} %get-tuple-element.2, f32[2816]{0:T(1024)S(1)} %copy-done.6), kind=kLoop, calls=%fused_computation.14 | loop fusion | flops 9371648 | bytes 13032448 | tf_op jit(solution)/shard_map/convert_element_type | solution.py:298
  20.2 1.7 %slice_convert_fusion = f32[256,2560]{0,1:T(8,128)} fusion(bf16[256,2816]{0,1:T(8,128)(2,1)S(1)} %multiply_convert_fusion), kind=kLoop, calls=%fused_computation.24 | loop fusion | flops 655360 | bytes 3932160 | tf_op jit(solution)/shard_map/convert_element_type | solution.py:235
  21.9 0.9 fusion.9
  22.9 2.9 %bitcast_multiply_fusion = (f32[256,2560]{0,1:T(8,128)}, f32[256,2560]{0,1:T(8,128)S(1)}, f32[256,2560]{0,1:T(8,128)}) fusion(f32[256,40]{0,1:T(8,128)S(1)} %get-tuple-element.14, bf16[256,2816]{0,1:T(8,128)(2,1)S(1)} %multiply_convert_fusion, f32[256,40]{0,1:T(8,128)S(1)} %get-tuple-element.12, f32[256,40]{0,1:T(8,128)S(1)} %get-tuple-element.11), kind=kLoop, calls=%fused_computation.15 | loop fusion | flops 2621440 | bytes 9297920 | tf_op jit(solution)/shard_map/mul | solution.py:227
  25.7 2.6 %fusion.14.local_ref = f32[128,2560]{1,0:T(8,128)} fusion(f32[256,2560]{0,1:T(8,128)S(1)} %get-tuple-element.9, bf16[256,2816]{0,1:T(8,128)(2,1)S(1)} %multiply_convert_fusion), kind=kOutput, calls=%fused_computation.32 | convolution fusion | flops 1006632960 | bytes 3997696 | tf_op jit(solution)/shard_map/dot_general | solution.py:225
  28.3 7.3 %shard_map.122 = f32[128,2560]{1,0:T(8,128)} custom-call(f32[128,2560]{1,0:T(8,128)} %fusion.14.local_ref, f32[1,2560]{1,0:T(1,128)} %broadcast_in_dim_reshape.4.decay_ref), custom_call_target="tpu_custom_call" | custom-call | tf_op jit(solution)/shard_map/pallas_call | solution.py:199
  35.7 3.9 %fusion.10 = f32[256,2560]{0,1:T(8,128)} fusion(f32[128,2560]{1,0:T(8,128)} %shard_map.122, bf16[256,2816]{0,1:T(8,128)(2,1)S(1)} %multiply_convert_fusion), kind=kOutput, calls=%fused_computation.28 | convolution fusion | flops 503316480 | bytes 3997696 | tf_op jit(solution)/shard_map/dot_general | solution.py:268
  39.6 2.7 %fusion = f32[2560,128]{0,1:T(8,128)} fusion(f32[256,2560]{0,1:T(8,128)S(1)} %copy-done.1, f32[128,2560]{1,0:T(8,128)S(1)} %copy-done, f32[2560]{0:T(1024)S(1)} %mul.226, bf16[256,2816]{0,1:T(8,128)(2,1)S(1)} %multiply_convert_fusion), kind=kOutput, calls=%fused_computation.1 | convolution fusion | flops 1007288320 | bytes 5320704 | tf_op jit(solution)/shard_map/dot_general | solution.py:225
  42.3 1.7 %copy.51 = f32[2560,128]{1,0:T(8,128)S(1)} copy(f32[2560,128]{0,1:T(8,128)} %fusion) | data formatting | bytes 2621440 | tf_op jit(solution)/shard_map/transpose | solution.py:314
  44.2 1.6 %copy.52 = f32[2,2,2,2,2,2,2,2,10,128]{9,8,7,6,5,4,3,2,1,0:T(8,128)} copy(f32[2,2,2,2,2,2,2,2,10,128]{9,8,0,1,2,3,4,5,6,7:T(8,128)S(1)} %bitcast.112) | data formatting | bytes 2621440 | tf_op jit(solution)/shard_map/transpose | solution.py:138
  46.3 69.7 %shard_map.123 = f32[1,10,128]{2,1,0:T(8,128)} custom-call(f32[256,10,128]{2,1,0:T(8,128)} %bitcast.111, f32[1,128]{1,0:T(1,128)} %broadcast_in_dim.27.label_ref), custom_call_target="tpu_custom_call" | custom-call | tf_op jit(solution)/shard_map/pallas_call | solution.py:115
  116.0 7.5 %multiply_reduce_fusion = (f32[256]{0:T(256)S(1)}, f32[256,40,64]{0,2,1:T(8,128)}) fusion(f32[256,40,64]{0,2,1:T(8,128)} %bitcast.114, f32[256,40,64]{0,2,1:T(8,128)} %bitcast.115, f32[40]{0:T(128)S(1)} %copy-done.7, f32[256,40]{0,1:T(8,128)S(1)} %get-tuple-element.13, f32[256,40,64]{0,2,1:T(8,128)} %bitcast.116, f32[256,256,1]{1,0,2:T(8,128)S(1)} %copy-done.3, ...), kind=kOutput, calls=%fused_computation.20 | convolution fusion | flops 1013841664 | bytes 13411488 | tf_op jit(solution)/shard_map/dot_general | solution.py:247
  123.5 2.2 %copy.49 = f32[1,256,2560]{2,1,0:T(8,128)S(1)} copy(f32[1,256,2560]{1,2,0:T(8,128)} %bitcast.113) | data formatting | bytes 5242880 | tf_op jit(solution)/shard_map/reshape | solution.py:272
  125.7 3.4 %multiply_convert_fusion.1 = bf16[1,256,2560]{2,1,0:T(8,128)(2,1)} fusion(f32[1,256,2560]{2,1,0:T(8,128)S(1)} %copy.49, f32[2560]{0:T(1024)S(1)} %copy-done.5, f32[256]{0:T(256)S(1)} %add_rsqrt_fusion, bf16[1,256,2560]{2,1,0:T(8,128)(2,1)} %param.12), kind=kLoop, calls=%fused_computation.19 | loop fusion | flops 5898240 | bytes 5254144 | tf_op jit(solution)/shard_map/convert_element_type | solution.py:274
  (37 shorter events, 4.0 us)
Async XLA Ops:
  0.6 11.5 %copy-start.2 = (bf16[1,256,2560]{2,1,0:T(8,128)(2,1)S(1)}, bf16[1,256,2560]{2,1,0:T(8,128)(2,1)}, u32[]{:S(2)}) copy-start(bf16[1,256,2560]{2,1,0:T(8,128)(2,1)} %param.12) | copy-start | bytes 3932164
  1.6 12.5 %collective-permute-start = (bf16[1,3,2816]{2,1,0:T(4,128)(2,1)S(1)}, bf16[1,3,2816]{2,1,0:T(4,128)(2,1)S(1)}, u32[]{:S(2)}, u32[]{:S(2)}) collective-permute-start(bf16[1,3,2816]{2,1,0:T(4,128)(2,1)S(1)} %slice.60), channel_id=1, source_target_pairs={{0,1},{1,2},{2,3},{3,4},{4,5},{5,6},{6,7},{8,9},{9,10},{10,11},{11... | collective-permute-start | bytes 50696 | tf_op jit(solution)/shard_map/ppermute | solution.py:220
  14.4 0.9 copy-start.6
  35.7 3.9 %copy-start = (f32[128,2560]{1,0:T(8,128)S(1)}, f32[128,2560]{1,0:T(8,128)}, u32[]{:S(2)}) copy-start(f32[128,2560]{1,0:T(8,128)} %shard_map.122) | copy-start | bytes 3932164
  35.7 3.9 %copy-start.1 = (f32[256,2560]{0,1:T(8,128)S(1)}, f32[256,2560]{0,1:T(8,128)}, u32[]{:S(2)}) copy-start(f32[256,2560]{0,1:T(8,128)} %get-tuple-element.8) | copy-start | bytes 7864324
  44.1 71.8 %copy-start.3 = (f32[256,256,1]{1,0,2:T(8,128)S(1)}, f32[256,256,1]{1,0,2:T(8,128)}, u32[]{:S(2)}) copy-start(f32[256,256,1]{1,0,2:T(8,128)} %fusion.9) | copy-start | bytes 786436
  44.2 71.8 %copy-start.7 = (f32[40]{0:T(128)S(1)}, f32[40]{0:T(128)}, u32[]{:S(2)}) copy-start(f32[40]{0:T(128)} %param.18) | copy-start | bytes 484
  123.5 2.2 %copy-start.5 = (f32[2560]{0:T(1024)S(1)}, f32[2560]{0:T(1024)}, u32[]{:S(2)}) copy-start(f32[2560]{0:T(1024)} %param.19) | copy-start | bytes 30724
  125.7 3.4 %copy-start.4 = (f32[1,10,128]{2,1,0:T(8,128)S(1)}, f32[1,10,128]{2,1,0:T(8,128)}, u32[]{:S(2)}) copy-start(f32[1,10,128]{2,1,0:T(8,128)} %shard_map.123) | copy-start | bytes 15364

commit v10 on v9

--- a/solution.py
+++ b/solution.py
@@ -226,7 +226,7 @@
         b_wide,
         (weight[:, :, None] * x_wide).reshape(row_count, H * P_SIZE),
         (((0,), (0,)), ((), ())),
-        precision=highest,
+        precision=lax.Precision.HIGH,
     )
 
 

time: 130 us -> 129 us (level)
  no operation moved by 1% of the time
where the time goes in v10:
time: 129 us
  Pallas kernels  77 us (60%)
  other arithmetic  17.6 us (14%)
  matrix products  16.7 us (13%)
  local copies, waits for them, and re-layouts  13.9 us (11%)
  starting transfers between devices  1.74 us (1%)
  between operations  1.52 us (1%)
    pallas_call x1, Pallas kernels, reduce_scatter_blocks(): pl.pallas_call(functools.partial(_reduce_scatter_kernel, plan), out_shape...  69.7 us
    dot_general x1, matrix products, local_terms(): jnp.dot(masked_scores, scaled_x, precision=lax.Precision.HIGH)  7.51 us
    pallas_call x1, Pallas kernels, carry_chain(): pl.pallas_call(functools.partial(_chain_kernel, chunk), out_shape=jax.Sha...  7.34 us
    convert_element_type x1, other arithmetic, on_device(): activated = jax.nn.silu(conv_sum).astype(jnp.bfloat16)  4.8 us
    dot_general x2, matrix products, state_product(): lax.dot_general(b_wide, (weight[:, :, None] * x_wide).reshape(row_count,...  4.16 us
    dot_general x1, matrix products, finish_block(): jnp.dot(c_wide, h_in, precision=lax.Precision.HIGH)  3.91 us
    convert_element_type x1, other arithmetic, finish_block(): return (gated_out * inv_rms * norm_gain).astype(jnp.bfloat16)  3.38 us
    mul x1, other arithmetic, state_product(): weight[:, :, None] * x_wide  2.87 us
  transfers between devices with their start and end apart: 1, of which 0 were waited for; matrix products, arithmetic and copies ran while one was open for 8% of the time, Pallas kernels for 0%

profile of v10, /device:TPU:6, one launch (start us, length us, event | category | flops | bytes accessed | tf_op | source)
XLA Modules:
  0.0 128.6 jit_solution(15954578908207860072)
XLA Ops:
  0.6 0.9 slice.60
  1.6 1.7 %collective-permute-start = (bf16[1,3,2816]{2,1,0:T(4,128)(2,1)S(1)}, bf16[1,3,2816]{2,1,0:T(4,128)(2,1)S(1)}, u32[]{:S(2)}, u32[]{:S(2)}) collective-permute-start(bf16[1,3,2816]{2,1,0:T(4,128)(2,1)S(1)} %slice.60), channel_id=1, source_target_pairs={{0,1},{1,2},{2,3},{3,4},{4,5},{5,6},{6,7},{8,9},{9,10},{10,11},{11... | collective-permute-start | bytes 50696 | tf_op jit(solution)/shard_map/ppermute | solution.py:220
  4.0 0.8 copy_bitcast_fusion
  5.7 0.7 and_convert_fusion
  7.0 0.9 exponential_multiply_fusion.1
  7.8 1.1 slice_reduce_fusion.5
  8.9 1.7 %copy.45 = bf16[1,256,2816]{1,2,0:T(8,128)(2,1)S(1)} copy(bf16[1,256,2816]{2,1,0:T(8,128)(2,1)} %param.11) | data formatting | bytes 2883584 | tf_op args[0]
  10.7 0.7 broadcast_in_dim_reshape.4.decay_ref
  12.2 1.9 %copy.50 = f32[1,256,2560]{1,2,0:T(8,128)} copy(bf16[1,256,2560]{2,1,0:T(8,128)(2,1)S(1)} %copy-done.2) | data formatting | bytes 3932160 | tf_op jit(solution)/shard_map/convert_element_type | solution.py:272
  14.4 0.9 maximum_convert_fusion
  15.4 4.8 %multiply_convert_fusion = bf16[256,2816]{0,1:T(8,128)(2,1)S(1)} fusion(f32[1,259,2816]{1,2,0:T(8,128)S(1)} %maximum_convert_fusion, f32[2816]{0:T(1024)S(1)} %get-tuple-element.4, f32[2816]{0:T(1024)S(1)} %get-tuple-element.5, f32[2816]{0:T(1024)S(1)} %get-tuple-element.3, f32[2816]{0:T(1024)S(1)} %get-tuple-element.2, f32[2816]{0:T(1024)S(1)} %copy-done.6), kind=kLoop, calls=%fused_computation.14 | loop fusion | flops 9371648 | bytes 13032448 | tf_op jit(solution)/shard_map/convert_element_type | solution.py:298
  20.2 1.7 %slice_convert_fusion = f32[256,2560]{0,1:T(8,128)} fusion(bf16[256,2816]{0,1:T(8,128)(2,1)S(1)} %multiply_convert_fusion), kind=kLoop, calls=%fused_computation.24 | loop fusion | flops 655360 | bytes 3932160 | tf_op jit(solution)/shard_map/convert_element_type | solution.py:235
  21.9 0.9 fusion.9
  22.9 2.9 %bitcast_multiply_fusion = (f32[256,2560]{0,1:T(8,128)}, f32[256,2560]{0,1:T(8,128)S(1)}, f32[256,2560]{0,1:T(8,128)}) fusion(f32[256,40]{0,1:T(8,128)S(1)} %get-tuple-element.14, bf16[256,2816]{0,1:T(8,128)(2,1)S(1)} %multiply_convert_fusion, f32[256,40]{0,1:T(8,128)S(1)} %get-tuple-element.12, f32[256,40]{0,1:T(8,128)S(1)} %get-tuple-element.11), kind=kLoop, calls=%fused_computation.15 | loop fusion | flops 2621440 | bytes 9297920 | tf_op jit(solution)/shard_map/mul | solution.py:227
  25.7 2.1 %fusion.14.local_ref = f32[128,2560]{1,0:T(8,128)} fusion(f32[256,2560]{0,1:T(8,128)S(1)} %get-tuple-element.9, bf16[256,2816]{0,1:T(8,128)(2,1)S(1)} %multiply_convert_fusion), kind=kOutput, calls=%fused_computation.32 | convolution fusion | flops 503316480 | bytes 3997696 | tf_op jit(solution)/shard_map/dot_general | solution.py:225
  27.8 7.3 %shard_map.122 = f32[128,2560]{1,0:T(8,128)} custom-call(f32[128,2560]{1,0:T(8,128)} %fusion.14.local_ref, f32[1,2560]{1,0:T(1,128)} %broadcast_in_dim_reshape.4.decay_ref), custom_call_target="tpu_custom_call" | custom-call | tf_op jit(solution)/shard_map/pallas_call | solution.py:199
  35.2 3.9 %fusion.10 = f32[256,2560]{0,1:T(8,128)} fusion(f32[128,2560]{1,0:T(8,128)} %shard_map.122, bf16[256,2816]{0,1:T(8,128)(2,1)S(1)} %multiply_convert_fusion), kind=kOutput, calls=%fused_computation.28 | convolution fusion | flops 503316480 | bytes 3997696 | tf_op jit(solution)/shard_map/dot_general | solution.py:268
  39.1 2.1 %fusion = f32[2560,128]{0,1:T(8,128)} fusion(f32[256,2560]{0,1:T(8,128)S(1)} %copy-done.1, f32[128,2560]{1,0:T(8,128)S(1)} %copy-done, f32[2560]{0:T(1024)S(1)} %mul.226, bf16[256,2816]{0,1:T(8,128)(2,1)S(1)} %multiply_convert_fusion), kind=kOutput, calls=%fused_computation.1 | convolution fusion | flops 503971840 | bytes 5320704 | tf_op jit(solution)/shard_map/dot_general | solution.py:225
  41.2 1.7 %copy.51 = f32[2560,128]{1,0:T(8,128)S(1)} copy(f32[2560,128]{0,1:T(8,128)} %fusion) | data formatting | bytes 2621440 | tf_op jit(solution)/shard_map/transpose | solution.py:314
  43.1 1.6 %copy.52 = f32[2,2,2,2,2,2,2,2,10,128]{9,8,7,6,5,4,3,2,1,0:T(8,128)} copy(f32[2,2,2,2,2,2,2,2,10,128]{9,8,0,1,2,3,4,5,6,7:T(8,128)S(1)} %bitcast.112) | data formatting | bytes 2621440 | tf_op jit(solution)/shard_map/transpose | solution.py:138
  45.2 69.7 %shard_map.123 = f32[1,10,128]{2,1,0:T(8,128)} custom-call(f32[256,10,128]{2,1,0:T(8,128)} %bitcast.111, f32[1,128]{1,0:T(1,128)} %broadcast_in_dim.27.label_ref), custom_call_target="tpu_custom_call" | custom-call | tf_op jit(solution)/shard_map/pallas_call | solution.py:115
  114.9 7.5 %multiply_reduce_fusion = (f32[256]{0:T(256)S(1)}, f32[256,40,64]{0,2,1:T(8,128)}) fusion(f32[256,40,64]{0,2,1:T(8,128)} %bitcast.114, f32[256,40,64]{0,2,1:T(8,128)} %bitcast.115, f32[40]{0:T(128)S(1)} %copy-done.7, f32[256,40]{0,1:T(8,128)S(1)} %get-tuple-element.13, f32[256,40,64]{0,2,1:T(8,128)} %bitcast.116, f32[256,256,1]{1,0,2:T(8,128)S(1)} %copy-done.3, ...), kind=kOutput, calls=%fused_computation.20 | convolution fusion | flops 1013841664 | bytes 13411488 | tf_op jit(solution)/shard_map/dot_general | solution.py:247
  122.4 2.2 %copy.49 = f32[1,256,2560]{2,1,0:T(8,128)S(1)} copy(f32[1,256,2560]{1,2,0:T(8,128)} %bitcast.113) | data formatting | bytes 5242880 | tf_op jit(solution)/shard_map/reshape | solution.py:272
  124.6 3.4 %multiply_convert_fusion.1 = bf16[1,256,2560]{2,1,0:T(8,128)(2,1)} fusion(f32[1,256,2560]{2,1,0:T(8,128)S(1)} %copy.49, f32[2560]{0:T(1024)S(1)} %copy-done.5, f32[256]{0:T(256)S(1)} %add_rsqrt_fusion, bf16[1,256,2560]{2,1,0:T(8,128)(2,1)} %param.12), kind=kLoop, calls=%fused_computation.19 | loop fusion | flops 5898240 | bytes 5254144 | tf_op jit(solution)/shard_map/convert_element_type | solution.py:274
  (37 shorter events, 4.0 us)
Async XLA Ops:
  0.6 11.5 %copy-start.2 = (bf16[1,256,2560]{2,1,0:T(8,128)(2,1)S(1)}, bf16[1,256,2560]{2,1,0:T(8,128)(2,1)}, u32[]{:S(2)}) copy-start(bf16[1,256,2560]{2,1,0:T(8,128)(2,1)} %param.12) | copy-start | bytes 3932164
  1.6 12.5 %collective-permute-start = (bf16[1,3,2816]{2,1,0:T(4,128)(2,1)S(1)}, bf16[1,3,2816]{2,1,0:T(4,128)(2,1)S(1)}, u32[]{:S(2)}, u32[]{:S(2)}) collective-permute-start(bf16[1,3,2816]{2,1,0:T(4,128)(2,1)S(1)} %slice.60), channel_id=1, source_target_pairs={{0,1},{1,2},{2,3},{3,4},{4,5},{5,6},{6,7},{8,9},{9,10},{10,11},{11... | collective-permute-start | bytes 50696 | tf_op jit(solution)/shard_map/ppermute | solution.py:220
  14.4 0.9 copy-start.6
  35.1 3.9 %copy-start = (f32[128,2560]{1,0:T(8,128)S(1)}, f32[128,2560]{1,0:T(8,128)}, u32[]{:S(2)}) copy-start(f32[128,2560]{1,0:T(8,128)} %shard_map.122) | copy-start | bytes 3932164
  35.1 3.9 %copy-start.1 = (f32[256,2560]{0,1:T(8,128)S(1)}, f32[256,2560]{0,1:T(8,128)}, u32[]{:S(2)}) copy-start(f32[256,2560]{0,1:T(8,128)} %get-tuple-element.8) | copy-start | bytes 7864324
  43.0 71.8 %copy-start.3 = (f32[256,256,1]{1,0,2:T(8,128)S(1)}, f32[256,256,1]{1,0,2:T(8,128)}, u32[]{:S(2)}) copy-start(f32[256,256,1]{1,0,2:T(8,128)} %fusion.9) | copy-start | bytes 786436
  43.0 71.8 %copy-start.7 = (f32[40]{0:T(128)S(1)}, f32[40]{0:T(128)}, u32[]{:S(2)}) copy-start(f32[40]{0:T(128)} %param.18) | copy-start | bytes 484
  122.4 2.2 %copy-start.5 = (f32[2560]{0:T(1024)S(1)}, f32[2560]{0:T(1024)}, u32[]{:S(2)}) copy-start(f32[2560]{0:T(1024)} %param.19) | copy-start | bytes 30724
  124.6 3.4 %copy-start.4 = (f32[1,10,128]{2,1,0:T(8,128)S(1)}, f32[1,10,128]{2,1,0:T(8,128)}, u32[]{:S(2)}) copy-start(f32[1,10,128]{2,1,0:T(8,128)} %shard_map.123) | copy-start | bytes 15364

commit v11 on v10

--- a/solution.py
+++ b/solution.py
@@ -146,7 +146,7 @@
     has_right = (2 * count - 2 - me) // count
     left = me - has_left
     right = me + has_right
-    pieces = local_ref.shape[1] // chunk
+    pieces = local_ref.shape[0] // chunk
 
     barrier = pltpu.get_barrier_semaphore()
 
@@ -163,8 +163,8 @@
     def link(source, piece):
         cols = pl.ds(piece * chunk, chunk)
         return pltpu.make_async_remote_copy(
-            src_ref=source.at[:, cols],
-            dst_ref=hin_ref.at[:, cols],
+            src_ref=source.at[cols],
+            dst_ref=hin_ref.at[cols],
             send_sem=send_sem.at[piece],
             recv_sem=recv_sem.at[piece],
             device_id=(row_id, right),
@@ -185,7 +185,7 @@
 
             @pl.when(has_right == 1)
             def _():
-                send_buf[:, cols] = decay_ref[:, cols] * hin_ref[:, cols] + local_ref[:, cols]
+                send_buf[cols] = decay_ref[...] * hin_ref[cols] + local_ref[cols]
                 link(send_buf, piece).start()
 
     @pl.when(has_right == 1)
@@ -194,8 +194,8 @@
             link(send_buf, piece).wait_send()
 
 
-def carry_chain(local_state, decay, pieces=20):
-    chunk = local_state.shape[1] // pieces
+def carry_chain(local_state, decay, pieces=16):
+    chunk = local_state.shape[0] // pieces
     return pl.pallas_call(
         functools.partial(_chain_kernel, chunk),
         out_shape=jax.ShapeDtypeStruct(local_state.shape, local_state.dtype),

time: 129 us -> 129 us (level)
  no operation moved by 1% of the time
where the time goes in v11:
time: 129 us
  Pallas kernels  77.4 us (60%)
  other arithmetic  17.6 us (14%)
  matrix products  16.7 us (13%)
  local copies, waits for them, and re-layouts  13.9 us (11%)
  starting transfers between devices  1.74 us (1%)
  between operations  1.52 us (1%)
    pallas_call x1, Pallas kernels, reduce_scatter_blocks(): pl.pallas_call(functools.partial(_reduce_scatter_kernel, plan), out_shape...  70.1 us
    dot_general x1, matrix products, local_terms(): jnp.dot(masked_scores, scaled_x, precision=lax.Precision.HIGH)  7.51 us
    pallas_call x1, Pallas kernels, carry_chain(): pl.pallas_call(functools.partial(_chain_kernel, chunk), out_shape=jax.Sha...  7.27 us
    convert_element_type x1, other arithmetic, on_device(): activated = jax.nn.silu(conv_sum).astype(jnp.bfloat16)  4.8 us
    dot_general x2, matrix products, state_product(): lax.dot_general(b_wide, (weight[:, :, None] * x_wide).reshape(row_count,...  4.16 us
    dot_general x1, matrix products, finish_block(): jnp.dot(c_wide, h_in, precision=lax.Precision.HIGH)  3.92 us
    convert_element_type x1, other arithmetic, finish_block(): return (gated_out * inv_rms * norm_gain).astype(jnp.bfloat16)  3.38 us
    mul x1, other arithmetic, state_product(): weight[:, :, None] * x_wide  2.87 us
  transfers between devices with their start and end apart: 1, of which 0 were waited for; matrix products, arithmetic and copies ran while one was open for 8% of the time, Pallas kernels for 0%

profile of v11, /device:TPU:6, one launch (start us, length us, event | category | flops | bytes accessed | tf_op | source)
XLA Modules:
  0.0 129.0 jit_solution(7785009697877410412)
XLA Ops:
  0.6 0.9 slice.60
  1.6 1.7 %collective-permute-start = (bf16[1,3,2816]{2,1,0:T(4,128)(2,1)S(1)}, bf16[1,3,2816]{2,1,0:T(4,128)(2,1)S(1)}, u32[]{:S(2)}, u32[]{:S(2)}) collective-permute-start(bf16[1,3,2816]{2,1,0:T(4,128)(2,1)S(1)} %slice.60), channel_id=1, source_target_pairs={{0,1},{1,2},{2,3},{3,4},{4,5},{5,6},{6,7},{8,9},{9,10},{10,11},{11... | collective-permute-start | bytes 50696 | tf_op jit(solution)/shard_map/ppermute | solution.py:220
  4.0 0.8 copy_bitcast_fusion
  5.7 0.7 and_convert_fusion
  7.0 0.9 exponential_multiply_fusion.1
  7.8 1.1 slice_reduce_fusion.5
  8.9 1.7 %copy.45 = bf16[1,256,2816]{1,2,0:T(8,128)(2,1)S(1)} copy(bf16[1,256,2816]{2,1,0:T(8,128)(2,1)} %param.11) | data formatting | bytes 2883584 | tf_op args[0]
  10.7 0.7 broadcast_in_dim_reshape.4.decay_ref
  12.2 1.9 %copy.50 = f32[1,256,2560]{1,2,0:T(8,128)} copy(bf16[1,256,2560]{2,1,0:T(8,128)(2,1)S(1)} %copy-done.2) | data formatting | bytes 3932160 | tf_op jit(solution)/shard_map/convert_element_type | solution.py:272
  14.4 0.9 maximum_convert_fusion
  15.4 4.8 %multiply_convert_fusion = bf16[256,2816]{0,1:T(8,128)(2,1)S(1)} fusion(f32[1,259,2816]{1,2,0:T(8,128)S(1)} %maximum_convert_fusion, f32[2816]{0:T(1024)S(1)} %get-tuple-element.4, f32[2816]{0:T(1024)S(1)} %get-tuple-element.5, f32[2816]{0:T(1024)S(1)} %get-tuple-element.3, f32[2816]{0:T(1024)S(1)} %get-tuple-element.2, f32[2816]{0:T(1024)S(1)} %copy-done.6), kind=kLoop, calls=%fused_computation.14 | loop fusion | flops 9371648 | bytes 13032448 | tf_op jit(solution)/shard_map/convert_element_type | solution.py:298
  20.2 1.7 %slice_convert_fusion = f32[256,2560]{0,1:T(8,128)} fusion(bf16[256,2816]{0,1:T(8,128)(2,1)S(1)} %multiply_convert_fusion), kind=kLoop, calls=%fused_computation.24 | loop fusion | flops 655360 | bytes 3932160 | tf_op jit(solution)/shard_map/convert_element_type | solution.py:235
  21.9 0.9 fusion.9
  22.9 2.9 %bitcast_multiply_fusion = (f32[256,2560]{0,1:T(8,128)}, f32[256,2560]{0,1:T(8,128)S(1)}, f32[256,2560]{0,1:T(8,128)}) fusion(f32[256,40]{0,1:T(8,128)S(1)} %get-tuple-element.14, bf16[256,2816]{0,1:T(8,128)(2,1)S(1)} %multiply_convert_fusion, f32[256,40]{0,1:T(8,128)S(1)} %get-tuple-element.12, f32[256,40]{0,1:T(8,128)S(1)} %get-tuple-element.11), kind=kLoop, calls=%fused_computation.15 | loop fusion | flops 2621440 | bytes 9297920 | tf_op jit(solution)/shard_map/mul | solution.py:227
  25.7 2.1 %fusion.14.local_ref = f32[128,2560]{1,0:T(8,128)} fusion(f32[256,2560]{0,1:T(8,128)S(1)} %get-tuple-element.9, bf16[256,2816]{0,1:T(8,128)(2,1)S(1)} %multiply_convert_fusion), kind=kOutput, calls=%fused_computation.32 | convolution fusion | flops 503316480 | bytes 3997696 | tf_op jit(solution)/shard_map/dot_general | solution.py:225
  27.8 7.3 %shard_map.122 = f32[128,2560]{1,0:T(8,128)} custom-call(f32[128,2560]{1,0:T(8,128)} %fusion.14.local_ref, f32[1,2560]{1,0:T(1,128)} %broadcast_in_dim_reshape.4.decay_ref), custom_call_target="tpu_custom_call" | custom-call | tf_op jit(solution)/shard_map/pallas_call | solution.py:199
  35.1 3.9 %fusion.10 = f32[256,2560]{0,1:T(8,128)} fusion(f32[128,2560]{1,0:T(8,128)} %shard_map.122, bf16[256,2816]{0,1:T(8,128)(2,1)S(1)} %multiply_convert_fusion), kind=kOutput, calls=%fused_computation.28 | convolution fusion | flops 503316480 | bytes 3997696 | tf_op jit(solution)/shard_map/dot_general | solution.py:268
  39.0 2.1 %fusion = f32[2560,128]{0,1:T(8,128)} fusion(f32[256,2560]{0,1:T(8,128)S(1)} %copy-done.1, f32[128,2560]{1,0:T(8,128)S(1)} %copy-done, f32[2560]{0:T(1024)S(1)} %mul.226, bf16[256,2816]{0,1:T(8,128)(2,1)S(1)} %multiply_convert_fusion), kind=kOutput, calls=%fused_computation.1 | convolution fusion | flops 503971840 | bytes 5320704 | tf_op jit(solution)/shard_map/dot_general | solution.py:225
  41.1 1.7 %copy.51 = f32[2560,128]{1,0:T(8,128)S(1)} copy(f32[2560,128]{0,1:T(8,128)} %fusion) | data formatting | bytes 2621440 | tf_op jit(solution)/shard_map/transpose | solution.py:314
  43.0 1.6 %copy.52 = f32[2,2,2,2,2,2,2,2,10,128]{9,8,7,6,5,4,3,2,1,0:T(8,128)} copy(f32[2,2,2,2,2,2,2,2,10,128]{9,8,0,1,2,3,4,5,6,7:T(8,128)S(1)} %bitcast.112) | data formatting | bytes 2621440 | tf_op jit(solution)/shard_map/transpose | solution.py:138
  45.1 70.1 %shard_map.123 = f32[1,10,128]{2,1,0:T(8,128)} custom-call(f32[256,10,128]{2,1,0:T(8,128)} %bitcast.111, f32[1,128]{1,0:T(1,128)} %broadcast_in_dim.27.label_ref), custom_call_target="tpu_custom_call" | custom-call | tf_op jit(solution)/shard_map/pallas_call | solution.py:115
  115.3 7.5 %multiply_reduce_fusion = (f32[256]{0:T(256)S(1)}, f32[256,40,64]{0,2,1:T(8,128)}) fusion(f32[256,40,64]{0,2,1:T(8,128)} %bitcast.114, f32[256,40,64]{0,2,1:T(8,128)} %bitcast.115, f32[40]{0:T(128)S(1)} %copy-done.7, f32[256,40]{0,1:T(8,128)S(1)} %get-tuple-element.13, f32[256,40,64]{0,2,1:T(8,128)} %bitcast.116, f32[256,256,1]{1,0,2:T(8,128)S(1)} %copy-done.3, ...), kind=kOutput, calls=%fused_computation.20 | convolution fusion | flops 1013841664 | bytes 13411488 | tf_op jit(solution)/shard_map/dot_general | solution.py:247
  122.8 2.2 %copy.49 = f32[1,256,2560]{2,1,0:T(8,128)S(1)} copy(f32[1,256,2560]{1,2,0:T(8,128)} %bitcast.113) | data formatting | bytes 5242880 | tf_op jit(solution)/shard_map/reshape | solution.py:272
  125.0 3.4 %multiply_convert_fusion.1 = bf16[1,256,2560]{2,1,0:T(8,128)(2,1)} fusion(f32[1,256,2560]{2,1,0:T(8,128)S(1)} %copy.49, f32[2560]{0:T(1024)S(1)} %copy-done.5, f32[256]{0:T(256)S(1)} %add_rsqrt_fusion, bf16[1,256,2560]{2,1,0:T(8,128)(2,1)} %param.12), kind=kLoop, calls=%fused_computation.19 | loop fusion | flops 5898240 | bytes 5254144 | tf_op jit(solution)/shard_map/convert_element_type | solution.py:274
  (37 shorter events, 4.0 us)
Async XLA Ops:
  0.6 11.5 %copy-start.2 = (bf16[1,256,2560]{2,1,0:T(8,128)(2,1)S(1)}, bf16[1,256,2560]{2,1,0:T(8,128)(2,1)}, u32[]{:S(2)}) copy-start(bf16[1,256,2560]{2,1,0:T(8,128)(2,1)} %param.12) | copy-start | bytes 3932164
  1.6 12.5 %collective-permute-start = (bf16[1,3,2816]{2,1,0:T(4,128)(2,1)S(1)}, bf16[1,3,2816]{2,1,0:T(4,128)(2,1)S(1)}, u32[]{:S(2)}, u32[]{:S(2)}) collective-permute-start(bf16[1,3,2816]{2,1,0:T(4,128)(2,1)S(1)} %slice.60), channel_id=1, source_target_pairs={{0,1},{1,2},{2,3},{3,4},{4,5},{5,6},{6,7},{8,9},{9,10},{10,11},{11... | collective-permute-start | bytes 50696 | tf_op jit(solution)/shard_map/ppermute | solution.py:220
  14.4 0.9 copy-start.6
  35.1 3.9 %copy-start = (f32[128,2560]{1,0:T(8,128)S(1)}, f32[128,2560]{1,0:T(8,128)}, u32[]{:S(2)}) copy-start(f32[128,2560]{1,0:T(8,128)} %shard_map.122) | copy-start | bytes 3932164
  35.1 3.9 %copy-start.1 = (f32[256,2560]{0,1:T(8,128)S(1)}, f32[256,2560]{0,1:T(8,128)}, u32[]{:S(2)}) copy-start(f32[256,2560]{0,1:T(8,128)} %get-tuple-element.8) | copy-start | bytes 7864324
  43.0 72.3 %copy-start.3 = (f32[256,256,1]{1,0,2:T(8,128)S(1)}, f32[256,256,1]{1,0,2:T(8,128)}, u32[]{:S(2)}) copy-start(f32[256,256,1]{1,0,2:T(8,128)} %fusion.9) | copy-start | bytes 786436
  43.0 72.3 %copy-start.7 = (f32[40]{0:T(128)S(1)}, f32[40]{0:T(128)}, u32[]{:S(2)}) copy-start(f32[40]{0:T(128)} %param.18) | copy-start | bytes 484
  122.8 2.2 %copy-start.5 = (f32[2560]{0:T(1024)S(1)}, f32[2560]{0:T(1024)}, u32[]{:S(2)}) copy-start(f32[2560]{0:T(1024)} %param.19) | copy-start | bytes 30724
  125.0 3.4 %copy-start.4 = (f32[1,10,128]{2,1,0:T(8,128)S(1)}, f32[1,10,128]{2,1,0:T(8,128)}, u32[]{:S(2)}) copy-start(f32[1,10,128]{2,1,0:T(8,128)} %shard_map.123) | copy-start | bytes 15364

commit v12 on v10

--- a/solution.py
+++ b/solution.py
@@ -173,9 +173,9 @@
 
     @pl.when(has_left == 0)
     def _():
-        hin_ref[...] = jnp.zeros_like(hin_ref)
         for piece in range(pieces):
             link(local_ref, piece).start()
+        hin_ref[...] = jnp.zeros_like(hin_ref)
 
     @pl.when(has_left == 1)
     def _():

time: 129 us -> 129 us (level)
  no operation moved by 1% of the time
where the time goes in v12:
time: 129 us
  Pallas kernels  76.9 us (60%)
  other arithmetic  17.6 us (14%)
  matrix products  16.7 us (13%)
  local copies, waits for them, and re-layouts  13.9 us (11%)
  starting transfers between devices  1.74 us (1%)
  between operations  1.52 us (1%)
    pallas_call x1, Pallas kernels, reduce_scatter_blocks(): pl.pallas_call(functools.partial(_reduce_scatter_kernel, plan), out_shape...  69.7 us
    dot_general x1, matrix products, local_terms(): jnp.dot(masked_scores, scaled_x, precision=lax.Precision.HIGH)  7.51 us
    pallas_call x1, Pallas kernels, carry_chain(): pl.pallas_call(functools.partial(_chain_kernel, chunk), out_shape=jax.Sha...  7.26 us
    convert_element_type x1, other arithmetic, on_device(): activated = jax.nn.silu(conv_sum).astype(jnp.bfloat16)  4.8 us
    dot_general x2, matrix products, state_product(): lax.dot_general(b_wide, (weight[:, :, None] * x_wide).reshape(row_count,...  4.16 us
    dot_general x1, matrix products, finish_block(): jnp.dot(c_wide, h_in, precision=lax.Precision.HIGH)  3.91 us
    convert_element_type x1, other arithmetic, finish_block(): return (gated_out * inv_rms * norm_gain).astype(jnp.bfloat16)  3.38 us
    mul x1, other arithmetic, state_product(): weight[:, :, None] * x_wide  2.87 us
  transfers between devices with their start and end apart: 1, of which 0 were waited for; matrix products, arithmetic and copies ran while one was open for 8% of the time, Pallas kernels for 0%

profile of v12, /device:TPU:6, one launch (start us, length us, event | category | flops | bytes accessed | tf_op | source)
XLA Modules:
  0.0 128.5 jit_solution(15018475131397284933)
XLA Ops:
  0.6 0.9 slice.60
  1.6 1.7 %collective-permute-start = (bf16[1,3,2816]{2,1,0:T(4,128)(2,1)S(1)}, bf16[1,3,2816]{2,1,0:T(4,128)(2,1)S(1)}, u32[]{:S(2)}, u32[]{:S(2)}) collective-permute-start(bf16[1,3,2816]{2,1,0:T(4,128)(2,1)S(1)} %slice.60), channel_id=1, source_target_pairs={{0,1},{1,2},{2,3},{3,4},{4,5},{5,6},{6,7},{8,9},{9,10},{10,11},{11... | collective-permute-start | bytes 50696 | tf_op jit(solution)/shard_map/ppermute | solution.py:220
  4.0 0.8 copy_bitcast_fusion
  5.7 0.7 and_convert_fusion
  7.0 0.9 exponential_multiply_fusion.1
  7.8 1.1 slice_reduce_fusion.5
  8.9 1.7 %copy.45 = bf16[1,256,2816]{1,2,0:T(8,128)(2,1)S(1)} copy(bf16[1,256,2816]{2,1,0:T(8,128)(2,1)} %param.11) | data formatting | bytes 2883584 | tf_op args[0]
  10.7 0.7 broadcast_in_dim_reshape.4.decay_ref
  12.2 1.9 %copy.50 = f32[1,256,2560]{1,2,0:T(8,128)} copy(bf16[1,256,2560]{2,1,0:T(8,128)(2,1)S(1)} %copy-done.2) | data formatting | bytes 3932160 | tf_op jit(solution)/shard_map/convert_element_type | solution.py:272
  14.4 0.9 maximum_convert_fusion
  15.4 4.8 %multiply_convert_fusion = bf16[256,2816]{0,1:T(8,128)(2,1)S(1)} fusion(f32[1,259,2816]{1,2,0:T(8,128)S(1)} %maximum_convert_fusion, f32[2816]{0:T(1024)S(1)} %get-tuple-element.4, f32[2816]{0:T(1024)S(1)} %get-tuple-element.5, f32[2816]{0:T(1024)S(1)} %get-tuple-element.3, f32[2816]{0:T(1024)S(1)} %get-tuple-element.2, f32[2816]{0:T(1024)S(1)} %copy-done.6), kind=kLoop, calls=%fused_computation.14 | loop fusion | flops 9371648 | bytes 13032448 | tf_op jit(solution)/shard_map/convert_element_type | solution.py:298
  20.2 1.7 %slice_convert_fusion = f32[256,2560]{0,1:T(8,128)} fusion(bf16[256,2816]{0,1:T(8,128)(2,1)S(1)} %multiply_convert_fusion), kind=kLoop, calls=%fused_computation.24 | loop fusion | flops 655360 | bytes 3932160 | tf_op jit(solution)/shard_map/convert_element_type | solution.py:235
  21.9 0.9 fusion.9
  22.9 2.9 %bitcast_multiply_fusion = (f32[256,2560]{0,1:T(8,128)}, f32[256,2560]{0,1:T(8,128)S(1)}, f32[256,2560]{0,1:T(8,128)}) fusion(f32[256,40]{0,1:T(8,128)S(1)} %get-tuple-element.14, bf16[256,2816]{0,1:T(8,128)(2,1)S(1)} %multiply_convert_fusion, f32[256,40]{0,1:T(8,128)S(1)} %get-tuple-element.12, f32[256,40]{0,1:T(8,128)S(1)} %get-tuple-element.11), kind=kLoop, calls=%fused_computation.15 | loop fusion | flops 2621440 | bytes 9297920 | tf_op jit(solution)/shard_map/mul | solution.py:227
  25.7 2.1 %fusion.14.local_ref = f32[128,2560]{1,0:T(8,128)} fusion(f32[256,2560]{0,1:T(8,128)S(1)} %get-tuple-element.9, bf16[256,2816]{0,1:T(8,128)(2,1)S(1)} %multiply_convert_fusion), kind=kOutput, calls=%fused_computation.32 | convolution fusion | flops 503316480 | bytes 3997696 | tf_op jit(solution)/shard_map/dot_general | solution.py:225
  27.8 7.3 %shard_map.122 = f32[128,2560]{1,0:T(8,128)} custom-call(f32[128,2560]{1,0:T(8,128)} %fusion.14.local_ref, f32[1,2560]{1,0:T(1,128)} %broadcast_in_dim_reshape.4.decay_ref), custom_call_target="tpu_custom_call" | custom-call | tf_op jit(solution)/shard_map/pallas_call | solution.py:199
  35.1 3.9 %fusion.10 = f32[256,2560]{0,1:T(8,128)} fusion(f32[128,2560]{1,0:T(8,128)} %shard_map.122, bf16[256,2816]{0,1:T(8,128)(2,1)S(1)} %multiply_convert_fusion), kind=kOutput, calls=%fused_computation.28 | convolution fusion | flops 503316480 | bytes 3997696 | tf_op jit(solution)/shard_map/dot_general | solution.py:268
  39.0 2.1 %fusion = f32[2560,128]{0,1:T(8,128)} fusion(f32[256,2560]{0,1:T(8,128)S(1)} %copy-done.1, f32[128,2560]{1,0:T(8,128)S(1)} %copy-done, f32[2560]{0:T(1024)S(1)} %mul.226, bf16[256,2816]{0,1:T(8,128)(2,1)S(1)} %multiply_convert_fusion), kind=kOutput, calls=%fused_computation.1 | convolution fusion | flops 503971840 | bytes 5320704 | tf_op jit(solution)/shard_map/dot_general | solution.py:225
  41.1 1.7 %copy.51 = f32[2560,128]{1,0:T(8,128)S(1)} copy(f32[2560,128]{0,1:T(8,128)} %fusion) | data formatting | bytes 2621440 | tf_op jit(solution)/shard_map/transpose | solution.py:314
  43.0 1.6 %copy.52 = f32[2,2,2,2,2,2,2,2,10,128]{9,8,7,6,5,4,3,2,1,0:T(8,128)} copy(f32[2,2,2,2,2,2,2,2,10,128]{9,8,0,1,2,3,4,5,6,7:T(8,128)S(1)} %bitcast.112) | data formatting | bytes 2621440 | tf_op jit(solution)/shard_map/transpose | solution.py:138
  45.1 69.7 %shard_map.123 = f32[1,10,128]{2,1,0:T(8,128)} custom-call(f32[256,10,128]{2,1,0:T(8,128)} %bitcast.111, f32[1,128]{1,0:T(1,128)} %broadcast_in_dim.27.label_ref), custom_call_target="tpu_custom_call" | custom-call | tf_op jit(solution)/shard_map/pallas_call | solution.py:115
  114.8 7.5 %multiply_reduce_fusion = (f32[256]{0:T(256)S(1)}, f32[256,40,64]{0,2,1:T(8,128)}) fusion(f32[256,40,64]{0,2,1:T(8,128)} %bitcast.114, f32[256,40,64]{0,2,1:T(8,128)} %bitcast.115, f32[40]{0:T(128)S(1)} %copy-done.7, f32[256,40]{0,1:T(8,128)S(1)} %get-tuple-element.13, f32[256,40,64]{0,2,1:T(8,128)} %bitcast.116, f32[256,256,1]{1,0,2:T(8,128)S(1)} %copy-done.3, ...), kind=kOutput, calls=%fused_computation.20 | convolution fusion | flops 1013841664 | bytes 13411488 | tf_op jit(solution)/shard_map/dot_general | solution.py:247
  122.3 2.2 %copy.49 = f32[1,256,2560]{2,1,0:T(8,128)S(1)} copy(f32[1,256,2560]{1,2,0:T(8,128)} %bitcast.113) | data formatting | bytes 5242880 | tf_op jit(solution)/shard_map/reshape | solution.py:272
  124.5 3.4 %multiply_convert_fusion.1 = bf16[1,256,2560]{2,1,0:T(8,128)(2,1)} fusion(f32[1,256,2560]{2,1,0:T(8,128)S(1)} %copy.49, f32[2560]{0:T(1024)S(1)} %copy-done.5, f32[256]{0:T(256)S(1)} %add_rsqrt_fusion, bf16[1,256,2560]{2,1,0:T(8,128)(2,1)} %param.12), kind=kLoop, calls=%fused_computation.19 | loop fusion | flops 5898240 | bytes 5254144 | tf_op jit(solution)/shard_map/convert_element_type | solution.py:274
  (37 shorter events, 4.0 us)
Async XLA Ops:
  0.6 11.5 %copy-start.2 = (bf16[1,256,2560]{2,1,0:T(8,128)(2,1)S(1)}, bf16[1,256,2560]{2,1,0:T(8,128)(2,1)}, u32[]{:S(2)}) copy-start(bf16[1,256,2560]{2,1,0:T(8,128)(2,1)} %param.12) | copy-start | bytes 3932164
  1.6 12.5 %collective-permute-start = (bf16[1,3,2816]{2,1,0:T(4,128)(2,1)S(1)}, bf16[1,3,2816]{2,1,0:T(4,128)(2,1)S(1)}, u32[]{:S(2)}, u32[]{:S(2)}) collective-permute-start(bf16[1,3,2816]{2,1,0:T(4,128)(2,1)S(1)} %slice.60), channel_id=1, source_target_pairs={{0,1},{1,2},{2,3},{3,4},{4,5},{5,6},{6,7},{8,9},{9,10},{10,11},{11... | collective-permute-start | bytes 50696 | tf_op jit(solution)/shard_map/ppermute | solution.py:220
  14.4 0.9 copy-start.6
  35.0 3.9 %copy-start = (f32[128,2560]{1,0:T(8,128)S(1)}, f32[128,2560]{1,0:T(8,128)}, u32[]{:S(2)}) copy-start(f32[128,2560]{1,0:T(8,128)} %shard_map.122) | copy-start | bytes 3932164
  35.1 3.9 %copy-start.1 = (f32[256,2560]{0,1:T(8,128)S(1)}, f32[256,2560]{0,1:T(8,128)}, u32[]{:S(2)}) copy-start(f32[256,2560]{0,1:T(8,128)} %get-tuple-element.8) | copy-start | bytes 7864324
  43.0 71.8 %copy-start.3 = (f32[256,256,1]{1,0,2:T(8,128)S(1)}, f32[256,256,1]{1,0,2:T(8,128)}, u32[]{:S(2)}) copy-start(f32[256,256,1]{1,0,2:T(8,128)} %fusion.9) | copy-start | bytes 786436
  43.0 71.8 %copy-start.7 = (f32[40]{0:T(128)S(1)}, f32[40]{0:T(128)}, u32[]{:S(2)}) copy-start(f32[40]{0:T(128)} %param.18) | copy-start | bytes 484
  122.3 2.2 %copy-start.5 = (f32[2560]{0:T(1024)S(1)}, f32[2560]{0:T(1024)}, u32[]{:S(2)}) copy-start(f32[2560]{0:T(1024)} %param.19) | copy-start | bytes 30724
  124.5 3.4 %copy-start.4 = (f32[1,10,128]{2,1,0:T(8,128)S(1)}, f32[1,10,128]{2,1,0:T(8,128)}, u32[]{:S(2)}) copy-start(f32[1,10,128]{2,1,0:T(8,128)} %shard_map.123) | copy-start | bytes 15364

commit v13 on v11

--- a/solution.py
+++ b/solution.py
@@ -194,7 +194,7 @@
             link(send_buf, piece).wait_send()
 
 
-def carry_chain(local_state, decay, pieces=16):
+def carry_chain(local_state, decay, pieces=32):
     chunk = local_state.shape[0] // pieces
     return pl.pallas_call(
         functools.partial(_chain_kernel, chunk),

time: 129 us -> 129 us (level)
  no operation moved by 1% of the time
where the time goes in v13:
time: 129 us; the launch traced here: 128 us
  Pallas kernels  76.6 us (59%)
  other arithmetic  17.6 us (14%)
  matrix products  16.7 us (13%)
  local copies, waits for them, and re-layouts  13.9 us (11%)
  starting transfers between devices  1.74 us (1%)
  between operations  1.52 us (1%)
    pallas_call x1, Pallas kernels, reduce_scatter_blocks(): pl.pallas_call(functools.partial(_reduce_scatter_kernel, plan), out_shape...  69 us
    pallas_call x1, Pallas kernels, carry_chain(): pl.pallas_call(functools.partial(_chain_kernel, chunk), out_shape=jax.Sha...  7.56 us
    dot_general x1, matrix products, local_terms(): jnp.dot(masked_scores, scaled_x, precision=lax.Precision.HIGH)  7.51 us
    convert_element_type x1, other arithmetic, on_device(): activated = jax.nn.silu(conv_sum).astype(jnp.bfloat16)  4.8 us
    dot_general x2, matrix products, state_product(): lax.dot_general(b_wide, (weight[:, :, None] * x_wide).reshape(row_count,...  4.16 us
    dot_general x1, matrix products, finish_block(): jnp.dot(c_wide, h_in, precision=lax.Precision.HIGH)  3.92 us
    convert_element_type x1, other arithmetic, finish_block(): return (gated_out * inv_rms * norm_gain).astype(jnp.bfloat16)  3.38 us
    mul x1, other arithmetic, state_product(): weight[:, :, None] * x_wide  2.87 us
  transfers between devices with their start and end apart: 1, of which 0 were waited for; matrix products, arithmetic and copies ran while one was open for 8% of the time, Pallas kernels for 0%

profile of v13, /device:TPU:6, one launch (start us, length us, event | category | flops | bytes accessed | tf_op | source)
XLA Modules:
  0.0 128.2 jit_solution(16403458949019645465)
XLA Ops:
  0.6 0.9 slice.60
  1.6 1.7 %collective-permute-start = (bf16[1,3,2816]{2,1,0:T(4,128)(2,1)S(1)}, bf16[1,3,2816]{2,1,0:T(4,128)(2,1)S(1)}, u32[]{:S(2)}, u32[]{:S(2)}) collective-permute-start(bf16[1,3,2816]{2,1,0:T(4,128)(2,1)S(1)} %slice.60), channel_id=1, source_target_pairs={{0,1},{1,2},{2,3},{3,4},{4,5},{5,6},{6,7},{8,9},{9,10},{10,11},{11... | collective-permute-start | bytes 50696 | tf_op jit(solution)/shard_map/ppermute | solution.py:220
  4.0 0.8 copy_bitcast_fusion
  5.7 0.7 and_convert_fusion
  7.0 0.9 exponential_multiply_fusion.1
  7.8 1.1 slice_reduce_fusion.5
  8.9 1.7 %copy.45 = bf16[1,256,2816]{1,2,0:T(8,128)(2,1)S(1)} copy(bf16[1,256,2816]{2,1,0:T(8,128)(2,1)} %param.11) | data formatting | bytes 2883584 | tf_op args[0]
  10.7 0.7 broadcast_in_dim_reshape.4.decay_ref
  12.2 1.9 %copy.50 = f32[1,256,2560]{1,2,0:T(8,128)} copy(bf16[1,256,2560]{2,1,0:T(8,128)(2,1)S(1)} %copy-done.2) | data formatting | bytes 3932160 | tf_op jit(solution)/shard_map/convert_element_type | solution.py:272
  14.4 0.9 maximum_convert_fusion
  15.4 4.8 %multiply_convert_fusion = bf16[256,2816]{0,1:T(8,128)(2,1)S(1)} fusion(f32[1,259,2816]{1,2,0:T(8,128)S(1)} %maximum_convert_fusion, f32[2816]{0:T(1024)S(1)} %get-tuple-element.4, f32[2816]{0:T(1024)S(1)} %get-tuple-element.5, f32[2816]{0:T(1024)S(1)} %get-tuple-element.3, f32[2816]{0:T(1024)S(1)} %get-tuple-element.2, f32[2816]{0:T(1024)S(1)} %copy-done.6), kind=kLoop, calls=%fused_computation.14 | loop fusion | flops 9371648 | bytes 13032448 | tf_op jit(solution)/shard_map/convert_element_type | solution.py:298
  20.2 1.7 %slice_convert_fusion = f32[256,2560]{0,1:T(8,128)} fusion(bf16[256,2816]{0,1:T(8,128)(2,1)S(1)} %multiply_convert_fusion), kind=kLoop, calls=%fused_computation.24 | loop fusion | flops 655360 | bytes 3932160 | tf_op jit(solution)/shard_map/convert_element_type | solution.py:235
  21.9 0.9 fusion.9
  22.9 2.9 %bitcast_multiply_fusion = (f32[256,2560]{0,1:T(8,128)}, f32[256,2560]{0,1:T(8,128)S(1)}, f32[256,2560]{0,1:T(8,128)}) fusion(f32[256,40]{0,1:T(8,128)S(1)} %get-tuple-element.14, bf16[256,2816]{0,1:T(8,128)(2,1)S(1)} %multiply_convert_fusion, f32[256,40]{0,1:T(8,128)S(1)} %get-tuple-element.12, f32[256,40]{0,1:T(8,128)S(1)} %get-tuple-element.11), kind=kLoop, calls=%fused_computation.15 | loop fusion | flops 2621440 | bytes 9297920 | tf_op jit(solution)/shard_map/mul | solution.py:227
  25.7 2.1 %fusion.14.local_ref = f32[128,2560]{1,0:T(8,128)} fusion(f32[256,2560]{0,1:T(8,128)S(1)} %get-tuple-element.9, bf16[256,2816]{0,1:T(8,128)(2,1)S(1)} %multiply_convert_fusion), kind=kOutput, calls=%fused_computation.32 | convolution fusion | flops 503316480 | bytes 3997696 | tf_op jit(solution)/shard_map/dot_general | solution.py:225
  27.8 7.6 %shard_map.122 = f32[128,2560]{1,0:T(8,128)} custom-call(f32[128,2560]{1,0:T(8,128)} %fusion.14.local_ref, f32[1,2560]{1,0:T(1,128)} %broadcast_in_dim_reshape.4.decay_ref), custom_call_target="tpu_custom_call" | custom-call | tf_op jit(solution)/shard_map/pallas_call | solution.py:199
  35.4 3.9 %fusion.10 = f32[256,2560]{0,1:T(8,128)} fusion(f32[128,2560]{1,0:T(8,128)} %shard_map.122, bf16[256,2816]{0,1:T(8,128)(2,1)S(1)} %multiply_convert_fusion), kind=kOutput, calls=%fused_computation.28 | convolution fusion | flops 503316480 | bytes 3997696 | tf_op jit(solution)/shard_map/dot_general | solution.py:268
  39.3 2.1 %fusion = f32[2560,128]{0,1:T(8,128)} fusion(f32[256,2560]{0,1:T(8,128)S(1)} %copy-done.1, f32[128,2560]{1,0:T(8,128)S(1)} %copy-done, f32[2560]{0:T(1024)S(1)} %mul.226, bf16[256,2816]{0,1:T(8,128)(2,1)S(1)} %multiply_convert_fusion), kind=kOutput, calls=%fused_computation.1 | convolution fusion | flops 503971840 | bytes 5320704 | tf_op jit(solution)/shard_map/dot_general | solution.py:225
  41.4 1.7 %copy.51 = f32[2560,128]{1,0:T(8,128)S(1)} copy(f32[2560,128]{0,1:T(8,128)} %fusion) | data formatting | bytes 2621440 | tf_op jit(solution)/shard_map/transpose | solution.py:314
  43.3 1.6 %copy.52 = f32[2,2,2,2,2,2,2,2,10,128]{9,8,7,6,5,4,3,2,1,0:T(8,128)} copy(f32[2,2,2,2,2,2,2,2,10,128]{9,8,0,1,2,3,4,5,6,7:T(8,128)S(1)} %bitcast.112) | data formatting | bytes 2621440 | tf_op jit(solution)/shard_map/transpose | solution.py:138
  45.4 69.0 %shard_map.123 = f32[1,10,128]{2,1,0:T(8,128)} custom-call(f32[256,10,128]{2,1,0:T(8,128)} %bitcast.111, f32[1,128]{1,0:T(1,128)} %broadcast_in_dim.27.label_ref), custom_call_target="tpu_custom_call" | custom-call | tf_op jit(solution)/shard_map/pallas_call | solution.py:115
  114.5 7.5 %multiply_reduce_fusion = (f32[256]{0:T(256)S(1)}, f32[256,40,64]{0,2,1:T(8,128)}) fusion(f32[256,40,64]{0,2,1:T(8,128)} %bitcast.114, f32[256,40,64]{0,2,1:T(8,128)} %bitcast.115, f32[40]{0:T(128)S(1)} %copy-done.7, f32[256,40]{0,1:T(8,128)S(1)} %get-tuple-element.13, f32[256,40,64]{0,2,1:T(8,128)} %bitcast.116, f32[256,256,1]{1,0,2:T(8,128)S(1)} %copy-done.3, ...), kind=kOutput, calls=%fused_computation.20 | convolution fusion | flops 1013841664 | bytes 13411488 | tf_op jit(solution)/shard_map/dot_general | solution.py:247
  122.0 2.2 %copy.49 = f32[1,256,2560]{2,1,0:T(8,128)S(1)} copy(f32[1,256,2560]{1,2,0:T(8,128)} %bitcast.113) | data formatting | bytes 5242880 | tf_op jit(solution)/shard_map/reshape | solution.py:272
  124.2 3.4 %multiply_convert_fusion.1 = bf16[1,256,2560]{2,1,0:T(8,128)(2,1)} fusion(f32[1,256,2560]{2,1,0:T(8,128)S(1)} %copy.49, f32[2560]{0:T(1024)S(1)} %copy-done.5, f32[256]{0:T(256)S(1)} %add_rsqrt_fusion, bf16[1,256,2560]{2,1,0:T(8,128)(2,1)} %param.12), kind=kLoop, calls=%fused_computation.19 | loop fusion | flops 5898240 | bytes 5254144 | tf_op jit(solution)/shard_map/convert_element_type | solution.py:274
  (37 shorter events, 4.0 us)
Async XLA Ops:
  0.6 11.5 %copy-start.2 = (bf16[1,256,2560]{2,1,0:T(8,128)(2,1)S(1)}, bf16[1,256,2560]{2,1,0:T(8,128)(2,1)}, u32[]{:S(2)}) copy-start(bf16[1,256,2560]{2,1,0:T(8,128)(2,1)} %param.12) | copy-start | bytes 3932164
  1.6 12.5 %collective-permute-start = (bf16[1,3,2816]{2,1,0:T(4,128)(2,1)S(1)}, bf16[1,3,2816]{2,1,0:T(4,128)(2,1)S(1)}, u32[]{:S(2)}, u32[]{:S(2)}) collective-permute-start(bf16[1,3,2816]{2,1,0:T(4,128)(2,1)S(1)} %slice.60), channel_id=1, source_target_pairs={{0,1},{1,2},{2,3},{3,4},{4,5},{5,6},{6,7},{8,9},{9,10},{10,11},{11... | collective-permute-start | bytes 50696 | tf_op jit(solution)/shard_map/ppermute | solution.py:220
  14.4 0.9 copy-start.6
  35.3 3.9 %copy-start = (f32[128,2560]{1,0:T(8,128)S(1)}, f32[128,2560]{1,0:T(8,128)}, u32[]{:S(2)}) copy-start(f32[128,2560]{1,0:T(8,128)} %shard_map.122) | copy-start | bytes 3932164
  35.4 3.9 %copy-start.1 = (f32[256,2560]{0,1:T(8,128)S(1)}, f32[256,2560]{0,1:T(8,128)}, u32[]{:S(2)}) copy-start(f32[256,2560]{0,1:T(8,128)} %get-tuple-element.8) | copy-start | bytes 7864324
  43.3 71.2 %copy-start.3 = (f32[256,256,1]{1,0,2:T(8,128)S(1)}, f32[256,256,1]{1,0,2:T(8,128)}, u32[]{:S(2)}) copy-start(f32[256,256,1]{1,0,2:T(8,128)} %fusion.9) | copy-start | bytes 786436
  43.3 71.2 %copy-start.7 = (f32[40]{0:T(128)S(1)}, f32[40]{0:T(128)}, u32[]{:S(2)}) copy-start(f32[40]{0:T(128)} %param.18) | copy-start | bytes 484
  122.0 2.2 %copy-start.5 = (f32[2560]{0:T(1024)S(1)}, f32[2560]{0:T(1024)}, u32[]{:S(2)}) copy-start(f32[2560]{0:T(1024)} %param.19) | copy-start | bytes 30724
  124.2 3.4 %copy-start.4 = (f32[1,10,128]{2,1,0:T(8,128)S(1)}, f32[1,10,128]{2,1,0:T(8,128)}, u32[]{:S(2)}) copy-start(f32[1,10,128]{2,1,0:T(8,128)} %shard_map.123) | copy-start | bytes 15364

commit v14 on v13

--- a/solution.py
+++ b/solution.py
@@ -194,7 +194,7 @@
             link(send_buf, piece).wait_send()
 
 
-def carry_chain(local_state, decay, pieces=32):
+def carry_chain(local_state, decay, pieces=64):
     chunk = local_state.shape[0] // pieces
     return pl.pallas_call(
         functools.partial(_chain_kernel, chunk),

time: 129 us -> 129 us (level)
  no operation moved by 1% of the time
where the time goes in v14:
time: 129 us; the launch traced here: 128 us
  Pallas kernels  76.6 us (59%)
  other arithmetic  17.6 us (14%)
  matrix products  16.7 us (13%)
  local copies, waits for them, and re-layouts  13.9 us (11%)
  starting transfers between devices  1.74 us (1%)
  between operations  1.52 us (1%)
    pallas_call x1, Pallas kernels, reduce_scatter_blocks(): pl.pallas_call(functools.partial(_reduce_scatter_kernel, plan), out_shape...  68.5 us
    pallas_call x1, Pallas kernels, carry_chain(): pl.pallas_call(functools.partial(_chain_kernel, chunk), out_shape=jax.Sha...  8.13 us
    dot_general x1, matrix products, local_terms(): jnp.dot(masked_scores, scaled_x, precision=lax.Precision.HIGH)  7.51 us
    convert_element_type x1, other arithmetic, on_device(): activated = jax.nn.silu(conv_sum).astype(jnp.bfloat16)  4.8 us
    dot_general x2, matrix products, state_product(): lax.dot_general(b_wide, (weight[:, :, None] * x_wide).reshape(row_count,...  4.16 us
    dot_general x1, matrix products, finish_block(): jnp.dot(c_wide, h_in, precision=lax.Precision.HIGH)  3.92 us
    convert_element_type x1, other arithmetic, finish_block(): return (gated_out * inv_rms * norm_gain).astype(jnp.bfloat16)  3.38 us
    mul x1, other arithmetic, state_product(): weight[:, :, None] * x_wide  2.87 us
  transfers between devices with their start and end apart: 1, of which 0 were waited for; matrix products, arithmetic and copies ran while one was open for 8% of the time, Pallas kernels for 0%

profile of v14, /device:TPU:6, one launch (start us, length us, event | category | flops | bytes accessed | tf_op | source)
XLA Modules:
  0.0 128.2 jit_solution(6473490728411479166)
XLA Ops:
  0.6 0.9 slice.60
  1.6 1.7 %collective-permute-start = (bf16[1,3,2816]{2,1,0:T(4,128)(2,1)S(1)}, bf16[1,3,2816]{2,1,0:T(4,128)(2,1)S(1)}, u32[]{:S(2)}, u32[]{:S(2)}) collective-permute-start(bf16[1,3,2816]{2,1,0:T(4,128)(2,1)S(1)} %slice.60), channel_id=1, source_target_pairs={{0,1},{1,2},{2,3},{3,4},{4,5},{5,6},{6,7},{8,9},{9,10},{10,11},{11... | collective-permute-start | bytes 50696 | tf_op jit(solution)/shard_map/ppermute | solution.py:220
  4.0 0.8 copy_bitcast_fusion
  5.7 0.7 and_convert_fusion
  7.0 0.9 exponential_multiply_fusion.1
  7.8 1.1 slice_reduce_fusion.5
  8.9 1.7 %copy.45 = bf16[1,256,2816]{1,2,0:T(8,128)(2,1)S(1)} copy(bf16[1,256,2816]{2,1,0:T(8,128)(2,1)} %param.11) | data formatting | bytes 2883584 | tf_op args[0]
  10.7 0.7 broadcast_in_dim_reshape.4.decay_ref
  12.2 1.9 %copy.50 = f32[1,256,2560]{1,2,0:T(8,128)} copy(bf16[1,256,2560]{2,1,0:T(8,128)(2,1)S(1)} %copy-done.2) | data formatting | bytes 3932160 | tf_op jit(solution)/shard_map/convert_element_type | solution.py:272
  14.4 0.9 maximum_convert_fusion
  15.4 4.8 %multiply_convert_fusion = bf16[256,2816]{0,1:T(8,128)(2,1)S(1)} fusion(f32[1,259,2816]{1,2,0:T(8,128)S(1)} %maximum_convert_fusion, f32[2816]{0:T(1024)S(1)} %get-tuple-element.4, f32[2816]{0:T(1024)S(1)} %get-tuple-element.5, f32[2816]{0:T(1024)S(1)} %get-tuple-element.3, f32[2816]{0:T(1024)S(1)} %get-tuple-element.2, f32[2816]{0:T(1024)S(1)} %copy-done.6), kind=kLoop, calls=%fused_computation.14 | loop fusion | flops 9371648 | bytes 13032448 | tf_op jit(solution)/shard_map/convert_element_type | solution.py:298
  20.2 1.7 %slice_convert_fusion = f32[256,2560]{0,1:T(8,128)} fusion(bf16[256,2816]{0,1:T(8,128)(2,1)S(1)} %multiply_convert_fusion), kind=kLoop, calls=%fused_computation.24 | loop fusion | flops 655360 | bytes 3932160 | tf_op jit(solution)/shard_map/convert_element_type | solution.py:235
  21.9 0.9 fusion.9
  22.9 2.9 %bitcast_multiply_fusion = (f32[256,2560]{0,1:T(8,128)}, f32[256,2560]{0,1:T(8,128)S(1)}, f32[256,2560]{0,1:T(8,128)}) fusion(f32[256,40]{0,1:T(8,128)S(1)} %get-tuple-element.14, bf16[256,2816]{0,1:T(8,128)(2,1)S(1)} %multiply_convert_fusion, f32[256,40]{0,1:T(8,128)S(1)} %get-tuple-element.12, f32[256,40]{0,1:T(8,128)S(1)} %get-tuple-element.11), kind=kLoop, calls=%fused_computation.15 | loop fusion | flops 2621440 | bytes 9297920 | tf_op jit(solution)/shard_map/mul | solution.py:227
  25.7 2.1 %fusion.14.local_ref = f32[128,2560]{1,0:T(8,128)} fusion(f32[256,2560]{0,1:T(8,128)S(1)} %get-tuple-element.9, bf16[256,2816]{0,1:T(8,128)(2,1)S(1)} %multiply_convert_fusion), kind=kOutput, calls=%fused_computation.32 | convolution fusion | flops 503316480 | bytes 3997696 | tf_op jit(solution)/shard_map/dot_general | solution.py:225
  27.8 8.1 %shard_map.122 = f32[128,2560]{1,0:T(8,128)} custom-call(f32[128,2560]{1,0:T(8,128)} %fusion.14.local_ref, f32[1,2560]{1,0:T(1,128)} %broadcast_in_dim_reshape.4.decay_ref), custom_call_target="tpu_custom_call" | custom-call | tf_op jit(solution)/shard_map/pallas_call | solution.py:199
  35.9 3.9 %fusion.10 = f32[256,2560]{0,1:T(8,128)} fusion(f32[128,2560]{1,0:T(8,128)} %shard_map.122, bf16[256,2816]{0,1:T(8,128)(2,1)S(1)} %multiply_convert_fusion), kind=kOutput, calls=%fused_computation.28 | convolution fusion | flops 503316480 | bytes 3997696 | tf_op jit(solution)/shard_map/dot_general | solution.py:268
  39.9 2.1 %fusion = f32[2560,128]{0,1:T(8,128)} fusion(f32[256,2560]{0,1:T(8,128)S(1)} %copy-done.1, f32[128,2560]{1,0:T(8,128)S(1)} %copy-done, f32[2560]{0:T(1024)S(1)} %mul.226, bf16[256,2816]{0,1:T(8,128)(2,1)S(1)} %multiply_convert_fusion), kind=kOutput, calls=%fused_computation.1 | convolution fusion | flops 503971840 | bytes 5320704 | tf_op jit(solution)/shard_map/dot_general | solution.py:225
  42.0 1.7 %copy.51 = f32[2560,128]{1,0:T(8,128)S(1)} copy(f32[2560,128]{0,1:T(8,128)} %fusion) | data formatting | bytes 2621440 | tf_op jit(solution)/shard_map/transpose | solution.py:314
  43.9 1.6 %copy.52 = f32[2,2,2,2,2,2,2,2,10,128]{9,8,7,6,5,4,3,2,1,0:T(8,128)} copy(f32[2,2,2,2,2,2,2,2,10,128]{9,8,0,1,2,3,4,5,6,7:T(8,128)S(1)} %bitcast.112) | data formatting | bytes 2621440 | tf_op jit(solution)/shard_map/transpose | solution.py:138
  46.0 68.5 %shard_map.123 = f32[1,10,128]{2,1,0:T(8,128)} custom-call(f32[256,10,128]{2,1,0:T(8,128)} %bitcast.111, f32[1,128]{1,0:T(1,128)} %broadcast_in_dim.27.label_ref), custom_call_target="tpu_custom_call" | custom-call | tf_op jit(solution)/shard_map/pallas_call | solution.py:115
  114.5 7.5 %multiply_reduce_fusion = (f32[256]{0:T(256)S(1)}, f32[256,40,64]{0,2,1:T(8,128)}) fusion(f32[256,40,64]{0,2,1:T(8,128)} %bitcast.114, f32[256,40,64]{0,2,1:T(8,128)} %bitcast.115, f32[40]{0:T(128)S(1)} %copy-done.7, f32[256,40]{0,1:T(8,128)S(1)} %get-tuple-element.13, f32[256,40,64]{0,2,1:T(8,128)} %bitcast.116, f32[256,256,1]{1,0,2:T(8,128)S(1)} %copy-done.3, ...), kind=kOutput, calls=%fused_computation.20 | convolution fusion | flops 1013841664 | bytes 13411488 | tf_op jit(solution)/shard_map/dot_general | solution.py:247
  122.0 2.2 %copy.49 = f32[1,256,2560]{2,1,0:T(8,128)S(1)} copy(f32[1,256,2560]{1,2,0:T(8,128)} %bitcast.113) | data formatting | bytes 5242880 | tf_op jit(solution)/shard_map/reshape | solution.py:272
  124.2 3.4 %multiply_convert_fusion.1 = bf16[1,256,2560]{2,1,0:T(8,128)(2,1)} fusion(f32[1,256,2560]{2,1,0:T(8,128)S(1)} %copy.49, f32[2560]{0:T(1024)S(1)} %copy-done.5, f32[256]{0:T(256)S(1)} %add_rsqrt_fusion, bf16[1,256,2560]{2,1,0:T(8,128)(2,1)} %param.12), kind=kLoop, calls=%fused_computation.19 | loop fusion | flops 5898240 | bytes 5254144 | tf_op jit(solution)/shard_map/convert_element_type | solution.py:274
  (37 shorter events, 4.0 us)
Async XLA Ops:
  0.6 11.5 %copy-start.2 = (bf16[1,256,2560]{2,1,0:T(8,128)(2,1)S(1)}, bf16[1,256,2560]{2,1,0:T(8,128)(2,1)}, u32[]{:S(2)}) copy-start(bf16[1,256,2560]{2,1,0:T(8,128)(2,1)} %param.12) | copy-start | bytes 3932164
  1.6 12.5 %collective-permute-start = (bf16[1,3,2816]{2,1,0:T(4,128)(2,1)S(1)}, bf16[1,3,2816]{2,1,0:T(4,128)(2,1)S(1)}, u32[]{:S(2)}, u32[]{:S(2)}) collective-permute-start(bf16[1,3,2816]{2,1,0:T(4,128)(2,1)S(1)} %slice.60), channel_id=1, source_target_pairs={{0,1},{1,2},{2,3},{3,4},{4,5},{5,6},{6,7},{8,9},{9,10},{10,11},{11... | collective-permute-start | bytes 50696 | tf_op jit(solution)/shard_map/ppermute | solution.py:220
  14.4 0.9 copy-start.6
  35.9 3.9 %copy-start = (f32[128,2560]{1,0:T(8,128)S(1)}, f32[128,2560]{1,0:T(8,128)}, u32[]{:S(2)}) copy-start(f32[128,2560]{1,0:T(8,128)} %shard_map.122) | copy-start | bytes 3932164
  35.9 3.9 %copy-start.1 = (f32[256,2560]{0,1:T(8,128)S(1)}, f32[256,2560]{0,1:T(8,128)}, u32[]{:S(2)}) copy-start(f32[256,2560]{0,1:T(8,128)} %get-tuple-element.8) | copy-start | bytes 7864324
  43.8 70.7 %copy-start.3 = (f32[256,256,1]{1,0,2:T(8,128)S(1)}, f32[256,256,1]{1,0,2:T(8,128)}, u32[]{:S(2)}) copy-start(f32[256,256,1]{1,0,2:T(8,128)} %fusion.9) | copy-start | bytes 786436
  43.8 70.7 %copy-start.7 = (f32[40]{0:T(128)S(1)}, f32[40]{0:T(128)}, u32[]{:S(2)}) copy-start(f32[40]{0:T(128)} %param.18) | copy-start | bytes 484
  122.0 2.2 %copy-start.5 = (f32[2560]{0:T(1024)S(1)}, f32[2560]{0:T(1024)}, u32[]{:S(2)}) copy-start(f32[2560]{0:T(1024)} %param.19) | copy-start | bytes 30724
  124.2 3.4 %copy-start.4 = (f32[1,10,128]{2,1,0:T(8,128)S(1)}, f32[1,10,128]{2,1,0:T(8,128)}, u32[]{:S(2)}) copy-start(f32[1,10,128]{2,1,0:T(8,128)} %shard_map.123) | copy-start | bytes 15364
